TPU v7x, 128 devices: a whole 4x4x4 slice. The times are simulated.
128 devices in a mesh: blk: 16 (over x, z), beam: 8 (over y, core).
Axes of the slice: x: 4, y: 4, z: 4, core: 2. Of those that a mesh axis runs over, the one named last changes fastest.
Arguments:
- embeds: bfloat16 [4, 128, 2048], P(None, 'beam'), may hold values from -6 to 6
- attn_gain: float32 [2048], replicated, may hold values from 0.25 to 1.75
- w_query: bfloat16 [2048, 3072], P(None, 'blk'), may hold values from -0.125 to 0.125
- w_latent: bfloat16 [2048, 576], replicated, may hold values from -0.125 to 0.125
- latent_gain: float32 [512], replicated, may hold values from 0.3 to 3
- w_key_up: bfloat16 [16, 128, 512], P('blk'), may hold values from -0.5 to 0.5
- w_value_up: bfloat16 [16, 512, 128], P('blk'), may hold values from -0.25 to 0.25
- w_out: bfloat16 [2048, 2048], P('blk'), may hold values from -0.125 to 0.125
- ffn_gain: float32 [2048], replicated, may hold values from 0.25 to 1.75
- w_shared_gate: bfloat16 [2048, 2816], P(None, 'blk'), may hold values from -0.125 to 0.125
- w_shared_up: bfloat16 [2048, 2816], P(None, 'blk'), may hold values from -0.125 to 0.125
- w_shared_down: bfloat16 [2816, 2048], P('blk'), may hold values from -0.109375 to 0.109375
- w_expert_gate: bfloat16 [32, 2048, 2816], P('blk', None, 'beam'), may hold values from -0.125 to 0.125
- w_expert_up: bfloat16 [32, 2048, 2816], P('blk', None, 'beam'), may hold values from -0.125 to 0.125
- w_expert_down: bfloat16 [32, 2816, 2048], P('blk', 'beam'), may hold values from -0.15625 to 0.15625
- cache_pool: bfloat16 [16, 96, 128, 576], P('beam', 'blk'), may hold values from -1600 to 1600
- block_tables: int32 [16, 8, 64], P('beam'), may hold values from 0 to 95, as said below
- block_counts: int32 [16], P('beam'), may hold values from 4 to 64
- parents: int32 [4, 16, 8], P(None, 'beam'), may hold values from 0 to 7
- expert_ids: int32 [4, 128, 6], replicated, may hold values from 0 to 63, all different within a row; in each aligned block of 128 rows (0 to 127, 128 to 255, ..., all dimensions but the last counted through in order) at most 24 rows name the same one
- expert_weights: float32 [4, 128, 6], replicated, may hold values from 0.1 to 0.6
Outputs:
- layer_out: float32 [4, 128, 2048], P(None, ('blk', 'beam'))
Inputs may be any that keep to these rules, and one draw needn't show every extreme that they name: `block_tables`: for each group g, entries j below block_counts[g] of one beam name different physical blocks; entries at or beyond block_counts[g] are never read. `expert_ids`: the experts of one row differ; within one step all rows together name one expert at most 24 times.
All inputs are finite; a program needn't handle non-finite values.
Results may differ from a plain program's by a relative error of at most 0.034.
Values may be sent and summed in bfloat16 or wider, within the bound.
No kernel may reach another device: no remote copies, remote signals or barrier semaphores. Data moves between devices by JAX's collectives and lax.ppermute only.
A program may use at most 128 MiB of HBM per device.

v0:
```python
import jax
import jax.numpy as jnp
from jax import lax
from jax.sharding import PartitionSpec as P

EXPERTS = 64
FFE = 1408


THETA = 50000.0
EPS = 1e-06
NEG = -1e30


def combined_all(shard, axis, combine):
    everything = jax.tree.map(lambda part: lax.all_gather(part, axis), shard)
    initial = jax.tree.map(lambda part: part[0], everything)

    def step(k, so_far):
        return combine(so_far, jax.tree.map(lambda part: part[k], everything))

    return lax.fori_loop(1, lax.axis_size(axis), step, initial)


def rms_scale(values, gain):
    mean_sq = jnp.mean(values * values, axis=-1, keepdims=True)
    return values * lax.rsqrt(mean_sq + EPS) * gain


def rotate(values, position):
    half_dim = values.shape[-1] // 2
    frequency = THETA ** (-jnp.arange(half_dim, dtype=jnp.float32) * 2.0 / values.shape[-1])
    angles = position[..., None] * frequency
    cosine = jnp.cos(angles)
    sine_part = jnp.sin(angles)
    lower_half = values[..., :half_dim]
    upper_half = values[..., half_dim:]
    return jnp.concatenate(
        [
            lower_half * cosine - upper_half * sine_part,
            lower_half * sine_part + upper_half * cosine,
        ],
        axis=-1,
    )


def combine(earlier, later):
    top_first, sum_first, lat_first = earlier
    top_second, sum_second, lat_second = later
    top_score = jnp.maximum(top_first, top_second)
    scale_first = jnp.exp(top_first - top_score)
    scale_second = jnp.exp(top_second - top_score)
    return (
        top_score,
        sum_first * scale_first + sum_second * scale_second,
        lat_first * scale_first[..., None] + lat_second * scale_second[..., None],
    )


def partial_attend(scores, key_mask, values, form):
    masked = jnp.where(key_mask, scores, NEG)
    top_score = jnp.max(masked, axis=-1)
    weights = jnp.where(key_mask, jnp.exp(masked - top_score[..., None]), 0.0)
    weight_sum = jnp.sum(weights, axis=-1)
    latent_sum = jnp.einsum(
        form, weights.astype(jnp.bfloat16), values, preferred_element_type=jnp.float32
    )
    return (top_score, weight_sum, latent_sum)


def per_device(
    embeds,
    attn_gain,
    w_query,
    w_latent,
    latent_gain,
    w_key_up,
    w_value_up,
    w_out,
    ffn_gain,
    w_shared_gate,
    w_shared_up,
    w_shared_down,
    w_expert_gate,
    w_expert_up,
    w_expert_down,
    cache_pool,
    block_tables,
    block_counts,
    parents,
    expert_ids,
    expert_weights,
):
    step_count, row_dev, model_width = embeds.shape
    group_count, beam_count, max_blocks = block_tables.shape
    heads_dev, head_in, latent = w_key_up.shape
    entry_width = cache_pool.shape[3]
    pool_dev = cache_pool.shape[1]
    block_len = cache_pool.shape[2]
    value_dim = w_value_up.shape[2]
    pair_dev = w_expert_gate.shape[0]
    unit_dev = w_expert_gate.shape[2]
    topk_count = expert_ids.shape[2]
    blk_index = lax.axis_index("blk")
    beam_index = lax.axis_index("beam")
    total_rows = row_dev * lax.axis_size("beam")
    capacity = 2 * total_rows * topk_count // EXPERTS
    score_scale = (entry_width - latent + head_in) ** (-0.5)
    phys_ids = blk_index * pool_dev + jnp.arange(pool_dev, dtype=jnp.int32)
    cache_keys = cache_pool.reshape(group_count, pool_dev * block_len, entry_width)
    cache_values = cache_keys[:, :, :latent]
    recent = jnp.zeros((group_count, beam_count, step_count, entry_width), jnp.bfloat16)
    tables = block_tables
    base_pos = (block_counts * block_len).astype(jnp.float32)
    valid = jnp.arange(max_blocks, dtype=jnp.int32)[None, None, :] < block_counts[:, None, None]
    pair_half = beam_index * unit_dev // FFE
    local_experts = (blk_index * pair_dev + jnp.arange(pair_dev, dtype=jnp.int32)) * 2 + pair_half
    results = []
    for decode_step in range(step_count):
        parent = parents[decode_step]
        recent = jnp.take_along_axis(recent, parent[:, :, None, None], axis=1)
        tables = jnp.take_along_axis(tables, parent[:, :, None], axis=1)
        tokens = embeds[decode_step]
        normed = rms_scale(tokens.astype(jnp.float32), attn_gain).astype(jnp.bfloat16)
        queries = jnp.dot(normed, w_query, preferred_element_type=jnp.float32).astype(jnp.bfloat16)
        queries = queries.reshape(row_dev, heads_dev, w_query.shape[1] // heads_dev)
        position = jnp.repeat(base_pos + decode_step, beam_count)
        query_latent = jnp.einsum(
            "rhn,hnc->rhc", queries[:, :, :head_in], w_key_up, preferred_element_type=jnp.float32
        )
        query_rope = rotate(queries[:, :, head_in:].astype(jnp.float32), position[:, None])
        query_full = jnp.concatenate([query_latent, query_rope], axis=-1).astype(jnp.bfloat16)
        projected = jnp.dot(normed, w_latent, preferred_element_type=jnp.float32)
        new_entry = jnp.concatenate(
            [
                rms_scale(projected[:, :latent], latent_gain),
                rotate(projected[:, latent:], position),
            ],
            axis=-1,
        ).astype(jnp.bfloat16)
        recent = recent.at[:, :, decode_step].set(
            new_entry.reshape(group_count, beam_count, entry_width)
        )
        all_queries = lax.all_gather(query_full, "blk", axis=1, tiled=True)
        head_count = all_queries.shape[1]
        grouped = all_queries.reshape(group_count, beam_count * head_count, entry_width)
        scores = (
            jnp.einsum("gqe,gke->gqk", grouped, cache_keys, preferred_element_type=jnp.float32)
            * score_scale
        )
        block_used = (
            jnp.sum(
                ((tables[:, :, :, None] == phys_ids) & valid[..., None]).astype(jnp.int32), axis=2
            )
            > 0
        )
        key_mask = jnp.repeat(jnp.repeat(block_used, block_len, axis=2), head_count, axis=1)
        top_score, weight_sum, latent_sum = partial_attend(
            scores, key_mask, cache_values, "gqk,gkc->gqc"
        )
        top_score = top_score.reshape(row_dev, head_count)
        weight_sum = weight_sum.reshape(row_dev, head_count)
        latent_sum = latent_sum.reshape(row_dev, head_count, latent)
        merged = combined_all((top_score, weight_sum, latent_sum), "blk", combine)
        head_start = blk_index * heads_dev
        pooled = tuple(
            (lax.dynamic_slice_in_dim(member, head_start, heads_dev, 1) for member in merged)
        )
        recent_rows = recent.reshape(row_dev, step_count, entry_width)[:, : decode_step + 1]
        recent_scores = (
            jnp.einsum("rhe,rse->rhs", query_full, recent_rows, preferred_element_type=jnp.float32)
            * score_scale
        )
        recent_part = partial_attend(
            recent_scores,
            jnp.ones(recent_scores.shape, bool),
            recent_rows[:, :, :latent],
            "rhs,rsc->rhc",
        )
        top_score, weight_sum, latent_sum = combine(pooled, recent_part)
        attended = (latent_sum / weight_sum[..., None]).astype(jnp.bfloat16)
        head_out = jnp.einsum(
            "rhc,hcv->rhv", attended, w_value_up, preferred_element_type=jnp.float32
        ).astype(jnp.bfloat16)
        attn_part = jnp.dot(
            head_out.reshape(row_dev, heads_dev * value_dim),
            w_out,
            preferred_element_type=jnp.float32,
        )
        attn_total = lax.psum(attn_part, "blk")
        resid = tokens.astype(jnp.float32) + attn_total
        ffn_in = rms_scale(resid, ffn_gain).astype(jnp.bfloat16)
        all_rows = lax.all_gather(ffn_in, "beam", axis=0, tiled=True)
        matches = expert_ids[decode_step][:, :, None] == local_experts
        routed = jnp.any(matches, axis=1)
        row_weight = jnp.sum(
            jnp.where(matches, expert_weights[decode_step][:, :, None], 0.0), axis=1
        )
        slot_index = jnp.cumsum(routed.astype(jnp.int32), axis=0) - 1
        slot_index = jnp.where(routed, slot_index, capacity)
        expert_cols = jnp.broadcast_to(
            jnp.arange(pair_dev, dtype=jnp.int32)[None, :], (total_rows, pair_dev)
        )
        row_numbers = jnp.broadcast_to(
            jnp.arange(total_rows, dtype=jnp.int32)[:, None], (total_rows, pair_dev)
        )
        slot_rows = (
            jnp.full((pair_dev, capacity), total_rows, jnp.int32)
            .at[expert_cols, slot_index]
            .set(row_numbers, mode="drop")
        )
        weight_pad = jnp.concatenate([row_weight.T, jnp.zeros((pair_dev, 1), jnp.float32)], axis=1)
        slot_weight = jnp.take_along_axis(weight_pad, slot_rows, axis=1)
        picked = jnp.take(all_rows, slot_rows, axis=0, mode="fill", fill_value=0)
        gate_val = jnp.einsum(
            "ecd,edf->ecf", picked, w_expert_gate, preferred_element_type=jnp.float32
        )
        up_val = jnp.einsum("ecd,edf->ecf", picked, w_expert_up, preferred_element_type=jnp.float32)
        activation = (jax.nn.silu(gate_val) * up_val).astype(jnp.bfloat16)
        down_out = (
            jnp.einsum(
                "ecf,efd->ecd", activation, w_expert_down, preferred_element_type=jnp.float32
            )
            * slot_weight[..., None]
        )
        partial_term = (
            jnp.zeros((total_rows, model_width), jnp.float32)
            .at[slot_rows.reshape(-1)]
            .add(down_out.reshape(-1, model_width), mode="drop")
        )
        shared_act = (
            jax.nn.silu(jnp.dot(ffn_in, w_shared_gate, preferred_element_type=jnp.float32))
            * jnp.dot(ffn_in, w_shared_up, preferred_element_type=jnp.float32)
        ).astype(jnp.bfloat16)
        own_rows = jnp.dot(
            shared_act, w_shared_down, preferred_element_type=jnp.float32
        ) + jnp.where(blk_index == 0, resid, 0.0)
        row_start = beam_index * row_dev
        partial_term = lax.dynamic_update_slice_in_dim(
            partial_term,
            lax.dynamic_slice_in_dim(partial_term, row_start, row_dev, 0) + own_rows,
            row_start,
            0,
        )
        summed = lax.psum_scatter(partial_term, ("blk", "beam"), scatter_dimension=0, tiled=True)
        results.append(summed)
    return jnp.stack(results)


def solution(mesh):
    placed = (
        P(None, "beam", None),
        P(),
        P(None, "blk"),
        P(),
        P(),
        P("blk", None, None),
        P("blk", None, None),
        P("blk", None),
        P(),
        P(None, "blk"),
        P(None, "blk"),
        P("blk", None),
        P("blk", None, "beam"),
        P("blk", None, "beam"),
        P("blk", "beam", None),
        P("beam", "blk", None, None),
        P("beam", None, None),
        P("beam"),
        P(None, "beam", None),
        P(),
        P(),
    )
    return jax.shard_map(
        per_device,
        mesh=mesh,
        in_specs=placed,
        out_specs=P(None, ("blk", "beam"), None),
        check_vma=False,
    )
```

profile of v0, /device:TPU:0, one launch (start us, length us, event | category | flops | bytes accessed | tf_op | source)
XLA Modules:
  0.0 968.9 jit_solution(11336190134766764950)
XLA Ops:
  19.6 25.3 %all_gather.60 = bf16[16,16,576]{2,0,1:T(8,128)(2,1)S(1)} all-gather(bf16[16,1,576]{2,0,1:T(8,128)(2,1)S(1)} %pad_maximum_fusion.4), channel_id=1, replica_groups=mesh['blk'=16,'beam'=8] {'blk'}, dimensions={1}, use_global_device_ids=true | all-gather | bytes 313344 | tf_op jit(solution)/shard_map/all_gather | solution.py:144
  44.9 3.9 copy.230
  48.9 2.5 fusion.389
  59.6 23.7 %all_gather.65 = bf16[16,16,576]{2,0,1:T(8,128)(2,1)S(1)} all-gather(bf16[16,1,576]{2,0,1:T(8,128)(2,1)S(1)} %pad_maximum_fusion.5), channel_id=1, replica_groups=mesh['blk'=16,'beam'=8] {'blk'}, dimensions={1}, use_global_device_ids=true | all-gather | bytes 313344 | tf_op jit(solution)/shard_map/all_gather | solution.py:144
  87.3 22.2 %all_gather.70 = bf16[16,16,576]{2,0,1:T(8,128)(2,1)S(1)} all-gather(bf16[16,1,576]{2,0,1:T(8,128)(2,1)S(1)} %pad_maximum_fusion.6), channel_id=1, replica_groups=mesh['blk'=16,'beam'=8] {'blk'}, dimensions={1}, use_global_device_ids=true | all-gather | bytes 313344 | tf_op jit(solution)/shard_map/all_gather | solution.py:144
  109.8 2.5 fusion.391
  115.2 23.7 %all_gather.75 = bf16[16,16,576]{2,0,1:T(8,128)(2,1)S(1)} all-gather(bf16[16,1,576]{2,0,1:T(8,128)(2,1)S(1)} %pad_maximum_fusion.7), channel_id=1, replica_groups=mesh['blk'=16,'beam'=8] {'blk'}, dimensions={1}, use_global_device_ids=true | all-gather | bytes 313344 | tf_op jit(solution)/shard_map/all_gather | solution.py:144
  139.1 2.6 fusion.392
  148.2 11.5 %scatter_fusion.3 = s32[2,24]{1,0:T(2,128)S(1)} fusion(s32[2,24]{1,0:T(2,128)S(1)} %broadcast.828.clone, s32[256]{0:T(256)S(1)} %reshape.1849, s32[256]{0:T(256)S(1)} %reshape.1809), kind=kCustom, calls=%fused_computation.22 | custom fusion | bytes 5120 | tf_op jit(solution)/shard_map/scatter | solution.py:210
  161.5 3.2 fusion.298
  164.8 2.4 fusion.289
  177.1 11.5 %scatter_fusion.2 = s32[2,24]{1,0:T(2,128)S(1)} fusion(s32[2,24]{1,0:T(2,128)S(1)} %broadcast.828.clone.1, s32[256]{0:T(256)S(1)} %reshape.1835, s32[256]{0:T(256)S(1)} %reshape.1809), kind=kCustom, calls=%fused_computation.20 | custom fusion | bytes 5120 | tf_op jit(solution)/shard_map/scatter | solution.py:210
  193.8 11.5 %scatter_fusion.1 = s32[2,24]{1,0:T(2,128)S(1)} fusion(s32[2,24]{1,0:T(2,128)S(1)} %broadcast.828.clone.2, s32[256]{0:T(256)S(1)} %reshape.1821, s32[256]{0:T(256)S(1)} %reshape.1809), kind=kCustom, calls=%fused_computation.18 | custom fusion | bytes 5120 | tf_op jit(solution)/shard_map/scatter | solution.py:210
  210.6 11.5 %scatter_fusion = s32[2,24]{1,0:T(2,128)S(1)} fusion(s32[2,24]{1,0:T(2,128)S(1)} %broadcast.828.clone.3, s32[256]{0:T(256)S(1)} %reshape.1807, s32[256]{0:T(256)S(1)} %reshape.1809), kind=kCustom, calls=%fused_computation.16 | custom fusion | bytes 5120 | tf_op jit(solution)/shard_map/scatter | solution.py:210
  227.5 21.2 %all_gather.61 = f32[16,16,16]{2,1,0:T(8,128)S(1)} all-gather(f32[1,16,16]{2,1,0:T(8,128)S(1)} %all_gather_reshape.36), channel_id=1, replica_groups=mesh['blk'=16,'beam'=8] {'blk'}, dimensions={0}, use_global_device_ids=true | all-gather | bytes 17408 | tf_op jit(solution)/shard_map/all_gather | solution.py:16
  248.8 23.8 %all_gather.62 = f32[16,16,16]{2,1,0:T(8,128)S(1)} all-gather(f32[1,16,16]{2,1,0:T(8,128)S(1)} %all_gather_reshape.37), channel_id=1, replica_groups=mesh['blk'=16,'beam'=8] {'blk'}, dimensions={0}, use_global_device_ids=true | all-gather | bytes 17408 | tf_op jit(solution)/shard_map/all_gather | solution.py:16
  279.1 21.0 %all_gather.66 = f32[16,16,16]{2,1,0:T(8,128)S(1)} all-gather(f32[1,16,16]{2,1,0:T(8,128)S(1)} %all_gather_reshape.39), channel_id=1, replica_groups=mesh['blk'=16,'beam'=8] {'blk'}, dimensions={0}, use_global_device_ids=true | all-gather | bytes 17408 | tf_op jit(solution)/shard_map/all_gather | solution.py:16
  300.9 23.7 %all_gather.67 = f32[16,16,16]{2,1,0:T(8,128)S(1)} all-gather(f32[1,16,16]{2,1,0:T(8,128)S(1)} %all_gather_reshape.40), channel_id=1, replica_groups=mesh['blk'=16,'beam'=8] {'blk'}, dimensions={0}, use_global_device_ids=true | all-gather | bytes 17408 | tf_op jit(solution)/shard_map/all_gather | solution.py:16
  331.0 21.1 %all_gather.71 = f32[16,16,16]{2,1,0:T(8,128)S(1)} all-gather(f32[1,16,16]{2,1,0:T(8,128)S(1)} %all_gather_reshape.42), channel_id=1, replica_groups=mesh['blk'=16,'beam'=8] {'blk'}, dimensions={0}, use_global_device_ids=true | all-gather | bytes 17408 | tf_op jit(solution)/shard_map/all_gather | solution.py:16
  352.9 23.4 %all_gather.72 = f32[16,16,16]{2,1,0:T(8,128)S(1)} all-gather(f32[1,16,16]{2,1,0:T(8,128)S(1)} %all_gather_reshape.43), channel_id=1, replica_groups=mesh['blk'=16,'beam'=8] {'blk'}, dimensions={0}, use_global_device_ids=true | all-gather | bytes 17408 | tf_op jit(solution)/shard_map/all_gather | solution.py:16
  381.2 21.3 %all_gather.76 = f32[16,16,16]{2,1,0:T(8,128)S(1)} all-gather(f32[1,16,16]{2,1,0:T(8,128)} %all_gather_reshape.45), channel_id=1, replica_groups=mesh['blk'=16,'beam'=8] {'blk'}, dimensions={0}, use_global_device_ids=true | all-gather | bytes 17408 | tf_op jit(solution)/shard_map/all_gather | solution.py:16
  403.3 23.1 %all_gather.77 = f32[16,16,16]{2,1,0:T(8,128)S(1)} all-gather(f32[1,16,16]{2,1,0:T(8,128)S(1)} %all_gather_reshape.46), channel_id=1, replica_groups=mesh['blk'=16,'beam'=8] {'blk'}, dimensions={0}, use_global_device_ids=true | all-gather | bytes 17408 | tf_op jit(solution)/shard_map/all_gather | solution.py:16
  444.1 29.7 %while.80 = (s32[]{:T(128)}, f32[16,16]{1,0:T(8,128)S(1)}, f32[16,16]{1,0:T(8,128)S(1)}, f32[16,16,512]{2,1,0:T(8,128)S(1)}, f32[16,16,16]{2,1,0:T(8,128)}, /*in...) while((s32[]{:T(128)}, f32[16,16]{1,0:T(8,128)S(1)}, ...), condition=%wide.region_8.10_spmd, body=%wide.region_7.9_spmd.sunk | while | flops 394757 | bytes 1583255 | solution.py:22
  477.3 29.6 %while.81 = (s32[]{:T(128)}, f32[16,16]{1,0:T(8,128)S(1)}, f32[16,16]{1,0:T(8,128)S(1)}, f32[16,16,512]{2,1,0:T(8,128)S(1)}, f32[16,16,16]{2,1,0:T(8,128)}, /*in...) while((s32[]{:T(128)}, f32[16,16]{1,0:T(8,128)S(1)}, ...), condition=%wide.region_23.28_spmd, body=%wide.region_22.27_spmd.sunk | while | flops 394757 | bytes 1583255 | solution.py:22
  510.6 29.6 %while.82 = (s32[]{:T(128)}, f32[16,16]{1,0:T(8,128)S(1)}, f32[16,16]{1,0:T(8,128)S(1)}, f32[16,16,512]{2,1,0:T(8,128)S(1)}, f32[16,16,16]{2,1,0:T(8,128)}, /*in...) while((s32[]{:T(128)}, f32[16,16]{1,0:T(8,128)S(1)}, ...), condition=%wide.region_40.45_spmd, body=%wide.region_39.44_spmd.sunk | while | flops 394757 | bytes 1583255 | solution.py:22
  543.8 38.8 %while.83 = (s32[]{:T(128)}, f32[16,16]{1,0:T(8,128)S(1)}, f32[16,16]{1,0:T(8,128)}, f32[16,16,512]{2,1,0:T(8,128)S(1)}, f32[16,16,16]{2,1,0:T(8,128)}, /*index=...) while((s32[]{:T(128)}, f32[16,16]{1,0:T(8,128)S(1)}, ...), condition=%wide.region_57.62_spmd, body=%wide.region_56.61_spmd.sunk | while | flops 394757 | bytes 1583255 | solution.py:22
  598.0 82.2 %all-reduce.15.cloned.1.call-done = (f32[16,2048]{1,0:T(8,128)}, f32[16,2048]{1,0:T(8,128)}, f32[16,2048]{1,0:T(8,128)}, f32[16,2048]{1,0:T(8,128)}) async-done(((f32[16,2048]{1,0:T(8,128)}, f32[16,2048]{1,0:T(8,128)}, f32[16,2048]{1,0:T(8,128)}, f32[16,2048]{1,0:T(8,128)}), (f32[16,2048]{1,0:T(8,128)}, f32[16,2048]{1,0:T(8,128)}, f32[16,2048]{1,0:T(8,128)}, ...) | async-done | bytes 524304 | tf_op jit(solution)/shard_map/psum | solution.py:190
  682.9 14.5 %all_gather.79 = bf16[128,2048]{1,0:T(8,128)(2,1)} all-gather(bf16[16,2048]{1,0:T(8,128)(2,1)S(1)} %get-tuple-element.895), channel_id=1, replica_groups=mesh['blk'=16,'beam'=8] {'beam'}, dimensions={0}, use_global_device_ids=true | all-gather | bytes 589824 | tf_op jit(solution)/shard_map/all_gather | solution.py:193
  699.5 14.3 %all_gather.74 = bf16[128,2048]{1,0:T(8,128)(2,1)} all-gather(bf16[16,2048]{1,0:T(8,128)(2,1)S(1)} %get-tuple-element.894), channel_id=1, replica_groups=mesh['blk'=16,'beam'=8] {'beam'}, dimensions={0}, use_global_device_ids=true | all-gather | bytes 589824 | tf_op jit(solution)/shard_map/all_gather | solution.py:193
  714.7 14.6 %all_gather.69 = bf16[128,2048]{1,0:T(8,128)(2,1)} all-gather(bf16[16,2048]{1,0:T(8,128)(2,1)S(1)} %get-tuple-element.893), channel_id=1, replica_groups=mesh['blk'=16,'beam'=8] {'beam'}, dimensions={0}, use_global_device_ids=true | all-gather | bytes 589824 | tf_op jit(solution)/shard_map/all_gather | solution.py:193
  730.2 14.2 %all_gather.64 = bf16[128,2048]{1,0:T(8,128)(2,1)} all-gather(bf16[16,2048]{1,0:T(8,128)(2,1)S(1)} %get-tuple-element.892), channel_id=1, replica_groups=mesh['blk'=16,'beam'=8] {'beam'}, dimensions={0}, use_global_device_ids=true | all-gather | bytes 589824 | tf_op jit(solution)/shard_map/all_gather | solution.py:193
  747.4 2.7 fusion.67
  750.2 3.9 convolution_multiply_fusion
  754.0 2.6 scatter_custom_fusion.7
  758.8 3.4 fusion.66
  762.2 3.9 convolution_multiply_fusion.1
  766.1 2.7 scatter_custom_fusion.5
  768.8 2.7 fusion.13
  771.5 2.7 fusion.15
  776.4 3.4 fusion.65
  779.7 3.9 convolution_multiply_fusion.2
  783.7 2.8 scatter_custom_fusion.3
  786.5 2.7 fusion.17
  791.2 3.4 fusion.64
  794.5 3.9 convolution_multiply_fusion.3
  798.5 2.6 scatter_custom_fusion.1
  801.1 2.7 fusion.19
  803.8 154.0 %all-reduce.13.cloned.1.call-done = (f32[128,2048]{1,0:T(8,128)}, f32[128,2048]{1,0:T(8,128)}, f32[128,2048]{1,0:T(8,128)}, f32[128,2048]{1,0:T(8,128)}) async-done(((f32[128,2048]{1,0:T(8,128)}, f32[128,2048]{1,0:T(8,128)}, f32[128,2048]{1,0:T(8,128)}, f32[128,2048]{1,0:T(8,128)}), (f32[128,2048]{1,0:T(8,128)}, f32[128,2048]{1,0:T(8,128)}, f32[128,2048]{1,0:T(8,128)}, ...) | async-done | bytes 4194320
  (600 shorter events, 271.6 us)
Async XLA Ops:
  6.5 743.6 %copy-start = (bf16[2,352,2048]{2,1,0:T(8,128)(2,1)S(1)}, bf16[2,352,2048]{2,1,0:T(8,128)(2,1)}, u32[]{:S(2)}) copy-start(bf16[2,352,2048]{2,1,0:T(8,128)(2,1)} %param.59) | copy-start | bytes 8650756
  6.5 436.5 %all-gather.5.cloned.1.call-start = ((), (), s32[]{:S(2)}) async-start(), calls=%async_computation | async-start | bytes 8912896 | tf_op jit(solution)/shard_map/all_gather | solution.py:16
  53.5 422.8 %all-gather.7.cloned.1.call-start = ((), (), s32[]{:S(2)}) async-start(), calls=%async_computation.1 | async-start | bytes 8912896 | tf_op jit(solution)/shard_map/all_gather | solution.py:16
  54.0 29.5 %copy-start.2 = (bf16[2,6,128,576]{3,2,1,0:T(8,128)(2,1)S(1)}, bf16[2,6,128,576]{3,2,1,0:T(8,128)(2,1)}, u32[]{:S(2)}) copy-start(bf16[2,6,128,576]{3,2,1,0:T(8,128)(2,1)} %copy.230) | copy-start | bytes 5308420
  58.9 27.9 %copy-start.53 = (bf16[16,1,32]{2,0,1:T(8,128)(2,1)}, bf16[16,1,32]{2,0,1:T(8,128)(2,1)S(1)}, u32[]{:S(2)}) copy-start(bf16[16,1,32]{2,0,1:T(8,128)(2,1)S(1)} %get-tuple-element.955) | copy-start | bytes 3076
  58.9 27.9 %copy-start.55 = (bf16[16,1,32]{2,0,1:T(8,128)(2,1)}, bf16[16,1,32]{2,0,1:T(8,128)(2,1)S(1)}, u32[]{:S(2)}) copy-start(bf16[16,1,32]{2,0,1:T(8,128)(2,1)S(1)} %get-tuple-element.956) | copy-start | bytes 3076
  58.9 55.7 %copy-start.49 = (bf16[16,1,32]{2,0,1:T(8,128)(2,1)}, bf16[16,1,32]{2,0,1:T(8,128)(2,1)S(1)}, u32[]{:S(2)}) copy-start(bf16[16,1,32]{2,0,1:T(8,128)(2,1)S(1)} %get-tuple-element.912) | copy-start | bytes 3076
  58.9 55.7 %copy-start.51 = (bf16[16,1,32]{2,0,1:T(8,128)(2,1)}, bf16[16,1,32]{2,0,1:T(8,128)(2,1)S(1)}, u32[]{:S(2)}) copy-start(bf16[16,1,32]{2,0,1:T(8,128)(2,1)S(1)} %get-tuple-element.913) | copy-start | bytes 3076
  86.5 423.0 %all-gather.9.cloned.1.call-start = ((), (), s32[]{:S(2)}) async-start(), calls=%async_computation.2 | async-start | bytes 8912896 | tf_op jit(solution)/shard_map/all_gather | solution.py:16
  86.7 26.5 %copy-start.3 = (bf16[2,6,128,576]{3,2,1,0:T(8,128)(2,1)S(1)}, bf16[2,6,128,576]{3,2,1,0:T(8,128)(2,1)}, u32[]{:S(2)}) copy-start(bf16[2,6,128,576]{3,2,1,0:T(8,128)(2,1)} %copy.230) | copy-start | bytes 5308420
  114.4 428.2 %all-gather.11.cloned.1.call-start = ((), (), s32[]{:S(2)}) async-start(), calls=%async_computation.3 | async-start | bytes 8912896 | tf_op jit(solution)/shard_map/all_gather | solution.py:16
  114.6 28.0 %copy-start.4 = (bf16[2,6,128,576]{3,2,1,0:T(8,128)(2,1)S(1)}, bf16[2,6,128,576]{3,2,1,0:T(8,128)(2,1)}, u32[]{:S(2)}) copy-start(bf16[2,6,128,576]{3,2,1,0:T(8,128)(2,1)} %copy.230) | copy-start | bytes 5308420
  143.8 536.4 %all-reduce.15.cloned.1.call-start = ((), (), s32[]{:S(2)}) async-start(), calls=%async_computation.5 | async-start | bytes 1048576 | tf_op jit(solution)/shard_map/psum | solution.py:190
  144.5 15.2 %copy-start.73 = (s32[2]{0:T(128)}, s32[2]{0:T(128)S(1)}, u32[]{:S(2)}) copy-start(s32[2]{0:T(128)S(1)} %multiply_add_fusion) | copy-start | bytes 28
  210.5 14.5 %copy-start.37 = (s32[128,6]{0,1:T(8,128)S(1)}, s32[128,6]{0,1:T(8,128)}, u32[]{:S(2)}) copy-start(s32[128,6]{0,1:T(8,128)} %copy-done.36) | copy-start | bytes 9220
  210.5 14.5 %copy-start.39 = (s32[128,6]{0,1:T(8,128)S(1)}, s32[128,6]{0,1:T(8,128)}, u32[]{:S(2)}) copy-start(s32[128,6]{0,1:T(8,128)} %copy-done.38) | copy-start | bytes 9220
  210.6 15.3 %copy-start.83 = (s32[2,24,1]{1,0,2:T(2,128)S(1)}, s32[2,24,1]{1,0,2:T(2,128)}, u32[]{:S(2)}) copy-start(s32[2,24,1]{1,0,2:T(2,128)} %bitcast_or_fusion) | copy-start | bytes 580
  210.6 38.1 %copy-start.66 = (f32[2,128]{1,0:T(2,128)S(1)}, f32[2,128]{1,0:T(2,128)}, u32[]{:S(2)}) copy-start(f32[2,128]{1,0:T(2,128)} %get-tuple-element.891) | copy-start | bytes 3076
  210.6 62.0 %copy-start.29 = (bf16[16,512]{1,0:T(8,128)(2,1)S(1)}, bf16[16,512]{1,0:T(8,128)(2,1)}, u32[]{:S(2)}) copy-start(bf16[16,512]{1,0:T(8,128)(2,1)} %copy-done.28) | copy-start | bytes 49156
  210.6 62.0 %copy-start.46 = (bf16[16,1,32]{2,0,1:T(8,128)(2,1)S(1)}, bf16[16,1,32]{2,0,1:T(8,128)(2,1)}, u32[]{:S(2)}) copy-start(bf16[16,1,32]{2,0,1:T(8,128)(2,1)} %copy-done.45) | copy-start | bytes 3076
  210.6 62.0 %copy-start.48 = (bf16[16,1,32]{2,0,1:T(8,128)(2,1)S(1)}, bf16[16,1,32]{2,0,1:T(8,128)(2,1)}, u32[]{:S(2)}) copy-start(bf16[16,1,32]{2,0,1:T(8,128)(2,1)} %copy-done.47) | copy-start | bytes 3076
  210.6 66.6 %copy-start.35 = (bf16[16,512]{1,0:T(8,128)(2,1)S(1)}, bf16[16,512]{1,0:T(8,128)(2,1)}, u32[]{:S(2)}) copy-start(bf16[16,512]{1,0:T(8,128)(2,1)} %copy-done.34) | copy-start | bytes 49156
  210.6 66.6 %copy-start.58 = (bf16[16,1,32]{2,0,1:T(8,128)(2,1)S(1)}, bf16[16,1,32]{2,0,1:T(8,128)(2,1)}, u32[]{:S(2)}) copy-start(bf16[16,1,32]{2,0,1:T(8,128)(2,1)} %copy-done.57) | copy-start | bytes 3076
  210.6 66.6 %copy-start.60 = (bf16[16,1,32]{2,0,1:T(8,128)(2,1)S(1)}, bf16[16,1,32]{2,0,1:T(8,128)(2,1)}, u32[]{:S(2)}) copy-start(bf16[16,1,32]{2,0,1:T(8,128)(2,1)} %copy-done.59) | copy-start | bytes 3076
  222.1 107.0 %copy-start.33 = (bf16[16,512]{1,0:T(8,128)(2,1)S(1)}, bf16[16,512]{1,0:T(8,128)(2,1)}, u32[]{:S(2)}) copy-start(bf16[16,512]{1,0:T(8,128)(2,1)} %copy-done.32) | copy-start | bytes 49156
  222.1 107.0 %copy-start.54 = (bf16[16,1,32]{2,0,1:T(8,128)(2,1)S(1)}, bf16[16,1,32]{2,0,1:T(8,128)(2,1)}, u32[]{:S(2)}) copy-start(bf16[16,1,32]{2,0,1:T(8,128)(2,1)} %copy-done.53) | copy-start | bytes 3076
  222.1 107.0 %copy-start.56 = (bf16[16,1,32]{2,0,1:T(8,128)(2,1)S(1)}, bf16[16,1,32]{2,0,1:T(8,128)(2,1)}, u32[]{:S(2)}) copy-start(bf16[16,1,32]{2,0,1:T(8,128)(2,1)} %copy-done.55) | copy-start | bytes 3076
  222.1 157.1 %copy-start.31 = (bf16[16,512]{1,0:T(8,128)(2,1)S(1)}, bf16[16,512]{1,0:T(8,128)(2,1)}, u32[]{:S(2)}) copy-start(bf16[16,512]{1,0:T(8,128)(2,1)} %copy-done.30) | copy-start | bytes 49156
  222.2 157.1 %copy-start.50 = (bf16[16,1,32]{2,0,1:T(8,128)(2,1)S(1)}, bf16[16,1,32]{2,0,1:T(8,128)(2,1)}, u32[]{:S(2)}) copy-start(bf16[16,1,32]{2,0,1:T(8,128)(2,1)} %copy-done.49) | copy-start | bytes 3076
  222.2 157.1 %copy-start.52 = (bf16[16,1,32]{2,0,1:T(8,128)(2,1)S(1)}, bf16[16,1,32]{2,0,1:T(8,128)(2,1)}, u32[]{:S(2)}) copy-start(bf16[16,1,32]{2,0,1:T(8,128)(2,1)} %copy-done.51) | copy-start | bytes 3076
  248.7 24.7 %copy-start.26 = (f32[16,16,16]{2,1,0:T(8,128)}, f32[16,16,16]{2,1,0:T(8,128)S(1)}, u32[]{:S(2)}) copy-start(f32[16,16,16]{2,1,0:T(8,128)S(1)} %all_gather.61) | copy-start | bytes 49156
  300.2 51.9 %copy-start.24 = (f32[16,16,16]{2,1,0:T(8,128)}, f32[16,16,16]{2,1,0:T(8,128)S(1)}, u32[]{:S(2)}) copy-start(f32[16,16,16]{2,1,0:T(8,128)S(1)} %all_gather.66) | copy-start | bytes 49156
  300.9 137.3 %copy-start.81 = (s32[2,24]{1,0:T(2,128)S(1)}, s32[2,24]{1,0:T(2,128)}, u32[]{:S(2)}) copy-start(s32[2,24]{1,0:T(2,128)} %compare_select_fusion.13) | copy-start | bytes 580
  300.9 139.1 %copy-start.67 = (f32[128,2]{0,1:T(2,128)S(1)}, f32[128,2]{0,1:T(2,128)}, u32[]{:S(2)}) copy-start(f32[128,2]{0,1:T(2,128)} %get-tuple-element.793) | copy-start | bytes 3076
  330.2 112.2 %copy-start.82 = (s32[2,24]{1,0:T(2,128)S(1)}, s32[2,24]{1,0:T(2,128)}, u32[]{:S(2)}) copy-start(s32[2,24]{1,0:T(2,128)} %compare_select_fusion.15) | copy-start | bytes 580
  352.1 50.4 %copy-start.22 = (f32[16,16,16]{2,1,0:T(8,128)}, f32[16,16,16]{2,1,0:T(8,128)S(1)}, u32[]{:S(2)}) copy-start(f32[16,16,16]{2,1,0:T(8,128)S(1)} %all_gather.71) | copy-start | bytes 49156
  376.3 66.7 %copy-start.23 = (f32[16,16,16]{2,1,0:T(8,128)}, f32[16,16,16]{2,1,0:T(8,128)S(1)}, u32[]{:S(2)}) copy-start(f32[16,16,16]{2,1,0:T(8,128)S(1)} %all_gather.72) | copy-start | bytes 49156
  402.5 27.8 %copy-start.20 = (f32[16,16,16]{2,1,0:T(8,128)}, f32[16,16,16]{2,1,0:T(8,128)S(1)}, u32[]{:S(2)}) copy-start(f32[16,16,16]{2,1,0:T(8,128)S(1)} %all_gather.76) | copy-start | bytes 49156
  426.4 16.6 %copy-start.21 = (f32[16,16,16]{2,1,0:T(8,128)}, f32[16,16,16]{2,1,0:T(8,128)S(1)}, u32[]{:S(2)}) copy-start(f32[16,16,16]{2,1,0:T(8,128)S(1)} %all_gather.77) | copy-start | bytes 49156
  543.7 43.5 %copy-start.10 = (bf16[1,512,128]{2,1,0:T(8,128)(2,1)S(1)}, bf16[1,512,128]{2,1,0:T(8,128)(2,1)}, u32[]{:S(2)}) copy-start(bf16[1,512,128]{2,1,0:T(8,128)(2,1)} %param.51) | copy-start | bytes 393220
  583.6 96.6 %copy-start.8 = (bf16[4,16,2048]{2,1,0:T(8,128)(2,1)S(1)}, bf16[4,16,2048]{2,1,0:T(8,128)(2,1)}, u32[]{:S(2)}) copy-start(bf16[4,16,2048]{2,1,0:T(8,128)(2,1)} %param.45) | copy-start | bytes 786436
  583.6 98.1 %copy-start.63 = (f32[2048]{0:T(1024)S(1)}, f32[2048]{0:T(1024)}, u32[]{:S(2)}) copy-start(f32[2048]{0:T(1024)} %param.53) | copy-start | bytes 24580
  595.6 362.2 %all-reduce.13.cloned.1.call-start = ((), (), s32[]{:S(2)}) async-start(), calls=%async_computation.4 | async-start | bytes 8388608
  680.2 33.6 %copy-start.6 = (bf16[2048,176]{0,1:T(8,128)(2,1)S(1)}, bf16[2048,176]{0,1:T(8,128)(2,1)}, u32[]{:S(2)}) copy-start(bf16[2048,176]{0,1:T(8,128)(2,1)} %param.54) | copy-start | bytes 2162692
  682.9 61.5 %copy-start.15 = (bf16[16,2048]{1,0:T(8,128)(2,1)}, bf16[16,2048]{1,0:T(8,128)(2,1)S(1)}, u32[]{:S(2)}) copy-start(bf16[16,2048]{1,0:T(8,128)(2,1)S(1)} %get-tuple-element.893) | copy-start | bytes 196612
  682.9 61.4 %copy-start.16 = (bf16[16,2048]{1,0:T(8,128)(2,1)}, bf16[16,2048]{1,0:T(8,128)(2,1)S(1)}, u32[]{:S(2)}) copy-start(bf16[16,2048]{1,0:T(8,128)(2,1)S(1)} %get-tuple-element.894) | copy-start | bytes 196612
  682.9 61.4 %copy-start.18 = (bf16[16,2048]{1,0:T(8,128)(2,1)}, bf16[16,2048]{1,0:T(8,128)(2,1)S(1)}, u32[]{:S(2)}) copy-start(bf16[16,2048]{1,0:T(8,128)(2,1)S(1)} %get-tuple-element.895) | copy-start | bytes 196612
  699.5 47.9 %copy-start.76 = (pred[2,24]{1,0:T(4,128)(4,1)S(1)}, pred[2,24]{1,0:T(4,128)(4,1)}, u32[]{:S(2)}) copy-start(pred[2,24]{1,0:T(4,128)(4,1)} %compare_and_fusion) | copy-start | bytes 148
  (44 other events, 215.4 us)
Sparse Core Ops, SparseCore 0:
  53.6 73.2 all-gather.4
  129.1 70.4 all-gather.6
  201.7 71.7 all-gather.8
  275.6 71.3 all-gather.10
  595.8 84.4 all-reduce.14
  803.9 153.8 all-reduce.12
where the time goes:
time: 984 us; the launch traced here: 969 us
  blocking collectives  331 us (34%)
  waiting for transfers between devices  236 us (24%)
  other arithmetic  187 us (19%)
  local copies, waits for them, and re-layouts  113 us (11%)
  matrix products  83.1 us (8%)
  between operations  15.3 us (2%)
    all_gather x8, blocking collectives, combined_all(): everything = jax.tree.map(lambda part: lax.all_gather(part, axis), shard)  179 us
    unnamed x7, waiting for transfers between devices  154 us
    all_gather x4, blocking collectives, per_device(): all_queries = lax.all_gather(query_full, 'blk', axis=1, tiled=True)  94.8 us
    psum x1, waiting for transfers between devices, per_device(): attn_total = lax.psum(attn_part, 'blk')  82.2 us
    add x60, other arithmetic, combine(): lat_first * scale_first[..., None] + lat_second * scale_second[..., None]  72.7 us
    all_gather x4, blocking collectives, per_device(): all_rows = lax.all_gather(ffn_in, 'beam', axis=0, tiled=True)  57.6 us
    add x60, other arithmetic, combine(): sum_first * scale_first + sum_second * scale_second  53.2 us
    scatter x4, local copies, waits for them, and re-layouts, per_device(): slot_rows = jnp.full((pair_dev, capacity), total_rows, jnp.int32).at[expe...  45.9 us
  transfers between devices with their start and end apart: 6, of which 2 were waited for; matrix products, arithmetic and copies ran while one was open for 24% of the time, Pallas kernels for 0%

commit v1 on v0

v1 whole, which is shorter than its diff:
```python
import jax
import jax.numpy as jnp
from jax import lax
from jax.experimental import pallas as pl
from jax.experimental.pallas import tpu as pltpu
from jax.sharding import Mesh, PartitionSpec as P

FFE = 1408
THETA = 50000.0
EPS = 1e-06
NEG = -1e30

BLK = ("x", "z")
BEAM = ("y", "core")
ROWS_ORDER = BEAM + BLK
OUT_ORDER = BLK + BEAM


def rms_scale(values, gain):
    mean_sq = jnp.mean(values * values, axis=-1, keepdims=True)
    return values * lax.rsqrt(mean_sq + EPS) * gain


def rotate(values, cosine, sine):
    half = values.shape[-1] // 2
    lower, upper = values[..., :half], values[..., half:]
    return jnp.concatenate(
        [lower * cosine - upper * sine, lower * sine + upper * cosine], axis=-1
    )


def shifted(value, axis, size, by):
    return lax.ppermute(value, axis, [(i, (i + by) % size) for i in range(size)])


def gather_blk(value):
    nx, nz = lax.axis_size("x"), lax.axis_size("z")
    along_x = jnp.stack([value] + [shifted(value, "x", nx, s) for s in range(1, nx)])
    both = [along_x] + [shifted(along_x, "z", nz, s) for s in range(1, nz)]
    return jnp.concatenate(both, axis=0)


def attend_kernel(
    info_ref, q_ref, cache_ref, entry_ref, parent_ref, table_ref, wv_ref, out_ref, lat_ref, lse_ref
):
    heads, groups, rows, width = q_ref.shape
    beams, max_blocks = table_ref.shape[1:]
    steps = rows // beams
    pool, block_len = cache_ref.shape[1:3]
    latent = wv_ref.shape[1]
    scale = (width - latent + 128) ** (-0.5)
    blk = info_ref[heads]
    lane = lambda shape: lax.broadcasted_iota(jnp.int32, shape, len(shape) - 1)
    sub = lambda shape: lax.broadcasted_iota(jnp.int32, shape, len(shape) - 2)
    f32 = jnp.float32
    for g in range(groups):
        shape = (beams, 128)
        origin = (lane(shape) == sub(shape)).astype(f32)
        kept = []
        for t in range(steps):
            choose = (lane((beams, beams)) == parent_ref[g, :, t : t + 1]).astype(f32)
            origin = jnp.dot(choose, origin, preferred_element_type=f32)
            origin = origin + (lane(shape) == sub(shape) + beams * (1 + t)).astype(f32)
            kept.append(origin)
        origin = jnp.concatenate(kept, axis=0)
        table = table_ref[g]
        live = lane(table.shape) < info_ref[heads + 1 + g]
        used = jnp.zeros((beams, 128), f32)
        for p in range(pool):
            hit = jnp.where((table == blk * pool + p) & live, 1.0, 0.0)
            hit = jnp.max(hit, axis=1, keepdims=True)
            used = used + jnp.where(lane(used.shape) == p, hit, 0.0)
        used = jnp.dot(origin[:, :beams], used, preferred_element_type=f32)
        bias = jnp.concatenate(
            [jnp.broadcast_to(used[:, p : p + 1], (rows, block_len)) for p in range(pool)], axis=1
        )
        bias = jnp.where(bias > 0.5, 0.0, NEG)
        seen = origin[:, beams : beams + rows]
        recent_bias = jnp.where((seen > 0.5) & (blk == 0), 0.0, NEG)

        q = q_ref[:, g].reshape(heads * rows, width)
        keys = cache_ref[g].reshape(pool * block_len, width)
        entry = entry_ref[g]
        over_width = (((1,), (1,)), ((), ()))
        scores = lax.dot_general(q, keys, over_width, preferred_element_type=f32)
        scores = scores.reshape(heads, rows, pool * block_len) * scale + bias[None]
        recent = lax.dot_general(q, entry, over_width, preferred_element_type=f32)
        recent = recent.reshape(heads, rows, rows) * scale + recent_bias[None]
        top = jnp.maximum(
            jnp.max(scores, axis=-1, keepdims=True), jnp.max(recent, axis=-1, keepdims=True)
        )
        weights = jnp.exp(scores - top)
        recent = jnp.exp(recent - top)
        total = jnp.sum(weights, axis=-1, keepdims=True) + jnp.sum(recent, axis=-1, keepdims=True)
        weights = weights.astype(jnp.bfloat16).reshape(heads * rows, pool * block_len)
        recent = recent.astype(jnp.bfloat16).reshape(heads * rows, rows)
        lat = jnp.dot(weights, keys[:, :latent], preferred_element_type=f32)
        lat = lat + jnp.dot(recent, entry[:, :latent], preferred_element_type=f32)
        lat = lat.reshape(heads, rows, latent) / total
        lat_ref[:, g * rows : (g + 1) * rows, :] = lat.astype(jnp.bfloat16)
        lse = jnp.where(top > 0.1 * NEG, top + jnp.log(total), NEG)
        lse_ref[:, g * rows : (g + 1) * rows, :] = jnp.broadcast_to(lse, (heads, rows, 128))

    rows_all = groups * rows
    diagonal = lane((rows_all, 128)) == sub((rows_all, 128))
    for h in range(heads):
        home = info_ref[h]
        value = jnp.dot(lat_ref[h], wv_ref[home], preferred_element_type=f32)
        out_ref[home, :rows_all, :] = value.astype(jnp.bfloat16)
        line = jnp.sum(jnp.where(diagonal, lse_ref[h], 0.0), axis=0, keepdims=True)
        first = line.astype(jnp.bfloat16).astype(f32)
        second = (line - first).astype(jnp.bfloat16).astype(f32)
        third = line - first - second
        place = sub((16, 128))
        tail = jnp.where(place == 0, first, 0.0)
        tail = jnp.where(place == 1, second, tail)
        tail = jnp.where(place == 2, third, tail)
        out_ref[home, rows_all:, :] = tail.astype(jnp.bfloat16)


def attend(info, queries, cache, entries, parents, tables, w_value):
    heads, groups, rows, _ = queries.shape
    value = w_value.shape[2]
    rows_all = groups * rows
    vmem = pl.BlockSpec(memory_space=pltpu.VMEM)
    return pl.pallas_call(
        attend_kernel,
        out_shape=jax.ShapeDtypeStruct((heads, rows_all + 16, value), jnp.bfloat16),
        in_specs=[pl.BlockSpec(memory_space=pltpu.SMEM)] + [vmem] * 6,
        out_specs=vmem,
        scratch_shapes=[
            pltpu.VMEM((heads, rows_all, w_value.shape[1]), jnp.bfloat16),
            pltpu.VMEM((heads, rows_all, 128), jnp.float32),
        ],
        compiler_params=pltpu.CompilerParams(vmem_limit_bytes=48 << 20),
        name="attend",
    )(info, queries, cache, entries, parents, tables, w_value)


def per_device(
    embeds,
    attn_gain,
    w_query,
    w_latent,
    latent_gain,
    w_key_up,
    w_value_up,
    w_out,
    ffn_gain,
    w_shared_gate,
    w_shared_up,
    w_shared_down,
    w_expert_gate,
    w_expert_up,
    w_expert_down,
    cache_pool,
    block_tables,
    block_counts,
    parents,
    expert_ids,
    expert_weights,
):
    f32, bf16 = jnp.float32, jnp.bfloat16
    steps, row_dev, width = embeds.shape
    groups, beams, _ = block_tables.shape
    head_in, latent = w_key_up.shape[1:]
    entry_width = cache_pool.shape[3]
    block_len = cache_pool.shape[2]
    rope = entry_width - latent
    pair_dev, _, unit_dev = w_expert_gate.shape
    total_rows = expert_ids.shape[1]
    nx, nz = lax.axis_size("x"), lax.axis_size("z")
    blk_size = nx * nz
    x, z = lax.axis_index("x"), lax.axis_index("z")
    blk = lax.axis_index(BLK)
    beam = lax.axis_index(BEAM)

    w_value = lax.all_gather(w_value_up, BLK, axis=0, tiled=True)

    tokens = embeds.reshape(steps, groups, beams, width).transpose(1, 0, 2, 3)
    tokens = tokens.reshape(steps * row_dev, width)
    normed = rms_scale(tokens.astype(f32), attn_gain).astype(bf16)
    queries = jnp.dot(normed, w_query, preferred_element_type=f32).astype(bf16)
    position = (block_counts * block_len).astype(f32)[:, None] + jnp.arange(steps, dtype=f32)
    position = jnp.repeat(position.reshape(-1), beams)
    frequency = THETA ** (-jnp.arange(rope // 2, dtype=f32) * 2.0 / rope)
    angles = position[:, None] * frequency
    cosine, sine = jnp.cos(angles), jnp.sin(angles)
    query_latent = jnp.dot(queries[:, :head_in], w_key_up[0], preferred_element_type=f32)
    query_rope = rotate(queries[:, head_in:].astype(f32), cosine, sine)
    query_full = jnp.concatenate([query_latent, query_rope], axis=-1).astype(bf16)
    all_queries = gather_blk(query_full)

    projected = jnp.dot(normed, w_latent, preferred_element_type=f32)
    entries = jnp.concatenate(
        [rms_scale(projected[:, :latent], latent_gain), rotate(projected[:, latent:], cosine, sine)],
        axis=-1,
    ).astype(bf16)

    near = jnp.arange(blk_size, dtype=jnp.int32)
    homes = (x - near % nx) % nx * nz + (z - near // nx) % nz
    info = jnp.concatenate([homes, blk[None], block_counts]).astype(jnp.int32)
    partial_heads = attend(
        info,
        all_queries.reshape(blk_size, groups, steps * beams, entry_width),
        cache_pool,
        entries.reshape(groups, steps * beams, entry_width),
        parents.transpose(1, 2, 0),
        block_tables,
        w_value,
    )
    rows_all = steps * row_dev
    parts = lax.all_to_all(partial_heads, BLK, 0, 0)
    lse = jnp.sum(parts[:, rows_all : rows_all + 3, :rows_all].astype(f32), axis=1)
    share = jnp.exp(lse - jnp.max(lse, axis=0))
    share = share / jnp.sum(share, axis=0)
    head_out = jnp.sum(parts[:, :rows_all].astype(f32) * share[:, :, None], axis=0).astype(bf16)
    head_out = head_out.reshape(groups, steps, beams, -1).transpose(0, 2, 1, 3)
    attn_part = jnp.dot(head_out.reshape(rows_all, -1), w_out, preferred_element_type=f32)
    attn_part = attn_part.astype(bf16).reshape(row_dev, steps, width)
    attn_total = jnp.sum(lax.all_to_all(attn_part, BLK, 0, 0).astype(f32), axis=0)
    own_tokens = lax.dynamic_slice_in_dim(embeds, blk, 1, 1)[:, 0].astype(f32)
    resid = own_tokens + attn_total
    ffn_in = rms_scale(resid, ffn_gain).astype(bf16)

    spread = jnp.broadcast_to(ffn_in, (total_rows, steps, width))
    all_rows = lax.all_to_all(spread, ROWS_ORDER, 0, 0).reshape(total_rows * steps, width)

    pair_half = beam * unit_dev // FFE
    local_experts = (blk * pair_dev + jnp.arange(pair_dev, dtype=jnp.int32)) * 2 + pair_half
    matches = expert_ids[:, :, :, None] == local_experts
    row_weight = jnp.sum(jnp.where(matches, expert_weights[:, :, :, None], 0.0), axis=2)
    row_weight = row_weight.transpose(1, 0, 2).reshape(total_rows * steps, pair_dev)
    total = None
    for e in range(pair_dev):
        gate_val = jnp.dot(all_rows, w_expert_gate[e], preferred_element_type=f32)
        up_val = jnp.dot(all_rows, w_expert_up[e], preferred_element_type=f32)
        activation = (jax.nn.silu(gate_val) * up_val * row_weight[:, e : e + 1]).astype(bf16)
        down = jnp.dot(activation, w_expert_down[e], preferred_element_type=f32)
        total = down if total is None else total + down

    beam_rows = lax.dynamic_slice_in_dim(all_rows, beam * rows_all, rows_all, 0)
    shared_act = (
        jax.nn.silu(jnp.dot(beam_rows, w_shared_gate, preferred_element_type=f32))
        * jnp.dot(beam_rows, w_shared_up, preferred_element_type=f32)
    ).astype(bf16)
    own = jnp.dot(shared_act, w_shared_down, preferred_element_type=f32)
    own_resid = lax.dynamic_update_slice_in_dim(jnp.zeros_like(own), resid, blk * steps, 0)
    own = own + own_resid
    held = lax.dynamic_slice_in_dim(total, beam * rows_all, rows_all, 0)
    total = lax.dynamic_update_slice_in_dim(total, held + own, beam * rows_all, 0)
    total = total.astype(bf16).reshape(total_rows, steps, width)
    result = jnp.sum(lax.all_to_all(total, OUT_ORDER, 0, 0).astype(f32), axis=0)
    return result[:, None]


def solution(mesh):
    devices = mesh.devices.reshape(4, 4, 4, 2)
    split = Mesh(devices, ("x", "z", "y", "core"))
    placed = (
        P(None, BEAM, None),
        P(),
        P(None, BLK),
        P(),
        P(),
        P(BLK, None, None),
        P(BLK, None, None),
        P(BLK, None),
        P(),
        P(None, BLK),
        P(None, BLK),
        P(BLK, None),
        P(BLK, None, BEAM),
        P(BLK, None, BEAM),
        P(BLK, BEAM, None),
        P(BEAM, BLK, None, None),
        P(BEAM, None, None),
        P(BEAM),
        P(None, BEAM, None),
        P(),
        P(),
    )
    return jax.shard_map(
        per_device,
        mesh=split,
        in_specs=placed,
        out_specs=P(None, OUT_ORDER, None),
        check_vma=False,
    )
```

time: 984 us -> 223 us (0.23); the launches traced: 969 us -> 221 us
  blocking collectives: 331 us -> 48.9 us
  other arithmetic: 187 us -> 10.5 us
  waiting for transfers between devices: 236 us -> 70.6 us
  local copies, waits for them, and re-layouts: 113 us -> 23.2 us
  matrix products: 83.1 us -> 25.9 us
  starting transfers between devices: 0.74 us -> 23.3 us
    all_gather x16 -> x0, blocking collectives: 331 us -> none  [the longest x8 179 us: combined_all(): everything = jax.tree.map(lambda part: lax.all_gather(part, axis), shard)]
    unnamed x7 -> x1, waiting for transfers between devices: 154 us -> 0.71 us
    add x123 -> x4, other arithmetic: 126 us -> 0.13 us  [the longest x1 0.07 us: per_device(): (block_counts * block_len).astype(f32)[:, None]]
    psum x1 -> x0, waiting for transfers between devices: 82.2 us -> none  [per_device(): attn_total = lax.psum(attn_part, 'blk')]
    dot_general x46 -> x10, matrix products: 83.1 us -> 25.9 us  [the longest x2 14.9 us: per_device(): down = jnp.dot(activation, w_expert_down[e], preferred_element_type=f32)]
    all_to_all x0 -> x2, blocking collectives: none -> 48.9 us  [the longest x1 35.3 us: per_device(): result = jnp.sum(lax.all_to_all(total, OUT_ORDER, 0, 0).astype(f32), axis=0)]
    scatter x8 -> x0, local copies, waits for them, and re-layouts: 46.8 us -> none  [the longest x4 45.9 us: per_device(): slot_rows = jnp.full((pair_dev, capacity), total_rows, jnp.int32).at[expe...]
    all_to_all x0 -> x2, waiting for transfers between devices: none -> 36.2 us  [the longest x1 28.7 us: per_device(): lax.all_to_all(spread, ROWS_ORDER, 0, 0).reshape(total_rows * steps, width)]
  transfers between devices with their start and end apart: 6 -> 9, of which waited for: 2 -> 5; matrix products, arithmetic and copies ran while one was open for 24% -> 5% of each run, Pallas kernels for 0% -> 0%
where the time goes in v1:
time: 223 us; the launch traced here: 221 us
  waiting for transfers between devices  70.6 us (32%)
  blocking collectives  48.9 us (22%)
  matrix products  25.9 us (12%)
  starting transfers between devices  23.3 us (10%)
  local copies, waits for them, and re-layouts  23.2 us (10%)
  between operations  13.7 us (6%)
  other arithmetic  10.5 us (5%)
  Pallas kernels  5.14 us (2%)
    all_to_all x1, blocking collectives, per_device(): result = jnp.sum(lax.all_to_all(total, OUT_ORDER, 0, 0).astype(f32), axis=0)  35.3 us
    all_to_all x1, waiting for transfers between devices, per_device(): lax.all_to_all(spread, ROWS_ORDER, 0, 0).reshape(total_rows * steps, width)  28.7 us
    all_gather x1, waiting for transfers between devices, per_device(): w_value = lax.all_gather(w_value_up, BLK, axis=0, tiled=True)  19.7 us
    dot_general x2, matrix products, per_device(): down = jnp.dot(activation, w_expert_down[e], preferred_element_type=f32)  14.9 us
    ppermute x6, waiting for transfers between devices, shifted(): lax.ppermute(value, axis, [(i, (i + by) % size) for i in range(size)])  14 us
    all_to_all x1, blocking collectives, per_device(): parts = lax.all_to_all(partial_heads, BLK, 0, 0)  13.6 us
    ppermute x6, starting transfers between devices, shifted(): lax.ppermute(value, axis, [(i, (i + by) % size) for i in range(size)])  12.3 us
    unnamed x43, local copies, waits for them, and re-layouts  9.66 us
  transfers between devices with their start and end apart: 9, of which 5 were waited for; matrix products, arithmetic and copies ran while one was open for 5% of the time, Pallas kernels for 0%

profile of v1, /device:TPU:0, one launch (start us, length us, event | category | flops | bytes accessed | tf_op | source)
XLA Modules:
  0.0 221.3 jit_solution(7890886451199980690)
XLA Ops:
  6.5 0.7 all-gather.2.cloned.1.call-update
  7.3 1.0 convert_bitcast_fusion
  8.3 1.1 fusion.51
  10.1 1.5 convolution_convert_fusion.2
  11.6 0.8 fusion.101
  12.4 0.2 fusion.81
  12.7 0.1 convolution_convert_fusion.1
  12.9 1.6 collective-permute-start
  14.5 2.7 %collective-permute-start.1 = (bf16[64,576]{1,0:T(8,128)(2,1)S(1)}, bf16[64,576]{1,0:T(8,128)(2,1)S(1)}, u32[]{:S(2)}, u32[]{:S(2)}) collective-permute-start(bf16[64,576]{1,0:T(8,128)(2,1)S(1)} %pad_maximum_fusion.1), channel_id=1, source_target_pairs={{0,64},{32,96},{64,0},{96,32},{1,65},{33,97},{65,1},{97,33},{2,66}... | collective-permute-start | bytes 221192 | tf_op jit(solution)/shard_map/ppermute | solution.py:33
  17.2 1.4 collective-permute-start.2
  18.7 3.9 %copy.54.cache_ref = bf16[2,6,128,576]{3,2,1,0:T(8,128)(2,1)} copy(bf16[2,6,128,576]{2,3,1,0:T(8,128)(2,1)} %param.36) | data formatting | bytes 3538944 | tf_op args[15]
  23.2 2.0 collective-permute-start.3
  25.2 3.6 %collective-permute-start.4 = (bf16[4,64,576]{2,1,0:T(8,128)(2,1)S(1)}, bf16[4,64,576]{2,1,0:T(8,128)(2,1)S(1)}, u32[]{:S(2)}, u32[]{:S(2)}) collective-permute-start(bf16[4,64,576]{2,1,0:T(8,128)(2,1)S(1)} %pad_maximum_fusion), channel_id=1, source_target_pairs={{0,16},{8,24},{16,0},{24,8},{1,17},{9,25},{17,1},{25,9},{2,18},{10... | collective-permute-start | bytes 884744 | tf_op jit(solution)/shard_map/ppermute | solution.py:33
  28.8 1.0 collective-permute-start.5
  29.8 6.1 %collective-permute-done.3 = bf16[4,64,576]{2,1,0:T(8,128)(2,1)S(1)} collective-permute-done((bf16[4,64,576]{2,1,0:T(8,128)(2,1)S(1)}, bf16[4,64,576]{2,1,0:T(8,128)(2,1)S(1)}, u32[]{:S(2)}, u32[]{:S(2)}) %collective-permute-start.3) | collective-permute-done | bytes 294944 | tf_op jit(solution)/shard_map/ppermute | solution.py:33
  36.0 7.9 %collective-permute-done.4 = bf16[4,64,576]{2,1,0:T(8,128)(2,1)S(1)} collective-permute-done((bf16[4,64,576]{2,1,0:T(8,128)(2,1)S(1)}, bf16[4,64,576]{2,1,0:T(8,128)(2,1)S(1)}, u32[]{:S(2)}, u32[]{:S(2)}) %collective-permute-start.4) | collective-permute-done | bytes 294944 | tf_op jit(solution)/shard_map/ppermute | solution.py:33
  44.0 1.0 copy-done.3
  45.0 19.7 %all-gather.2.cloned.1.call-done.wv_ref = bf16[16,512,128]{2,1,0:T(8,128)(2,1)} async-done(((bf16[1,512,128]{2,1,0:T(8,128)(2,1)}), bf16[16,512,128]{2,1,0:T(8,128)(2,1)}) %all-gather.2.cloned.1.call-update) | async-done | bytes 2097168 | tf_op jit(solution)/shard_map/all_gather | solution.py:178
  64.7 1.5 copy-done.1
  66.2 1.6 copy-done.2
  67.8 1.3 copy-done.4
  69.2 5.1 %attend.1 = bf16[16,80,128]{2,1,0:T(8,128)(2,1)S(1)} custom-call(s32[19]{0:T(128)S(1)} %pad_add_fusion.info_ref, bf16[16,2,32,576]{3,2,1,0:T(8,128)(2,1)S(1)} %copy-done.4, bf16[2,6,128,576]{3,2,1,0:T(8,128)(2,1)S(1)} %copy-done.1, bf16[2,32,576]{2,1,0:T(8,128)(2,1)S(1)} %pad_maximum_fusion.2.entry_ref, s32[2,8,4]{2,1,0:T(8,128)S(1)} %bitcast.101, ...), custom_call_target="tpu_custom_call" | custom-call | tf_op jit(solution)/shard_map/attend/pallas_call | solution.py:126
  74.3 13.6 %all_to_all.20 = bf16[16,80,128]{2,1,0:T(8,128)(2,1)S(1)} all-to-all(bf16[16,80,128]{2,1,0:T(8,128)(2,1)S(1)} %attend.1), channel_id=1, replica_groups=mesh['x'=4,'z'=4,'y'=4,'core'=2] {'x','z'}, dimensions={0} | all-to-all | bytes 655360 | tf_op jit(solution)/shard_map/all_to_all | solution.py:213
  88.0 0.2 multiply_reduce_fusion
  88.2 0.2 convolution_convert_fusion
  88.4 0.8 reshape.224
  89.2 3.7 %all-to-all-start.1 = ((bf16[16,4,2048]{2,1,0:T(4,128)(2,1)}), bf16[16,4,2048]{2,1,0:T(4,128)(2,1)S(1)}, u32[]{:S(2)}, u32[]{:S(2)}) async-start(bf16[16,4,2048]{2,1,0:T(4,128)(2,1)} %reshape.224), calls=%async_computation.1 | async-start | bytes 524288 | tf_op jit(solution)/shard_map/all_to_all | solution.py:221
  92.9 0.9 constant_dynamic-slice_fusion
  93.9 7.5 %all-to-all-done.1 = bf16[16,4,2048]{2,1,0:T(4,128)(2,1)S(1)} async-done(((bf16[16,4,2048]{2,1,0:T(4,128)(2,1)}), bf16[16,4,2048]{2,1,0:T(4,128)(2,1)S(1)}, u32[]{:S(2)}, u32[]{:S(2)}) %all-to-all-start.1) | async-done | bytes 262176 | tf_op jit(solution)/shard_map/all_to_all | solution.py:221
  101.5 0.1 multiply_reduce_fusion.2
  101.7 2.4 %broadcast_in_dim.18 = bf16[128,4,2048]{2,1,0:T(4,128)(2,1)} broadcast(bf16[4,2048]{1,0:T(4,128)(2,1)S(1)} %multiply_convert_fusion.1), dimensions={1,2} | broadcast | bytes 2113536 | tf_op jit(solution)/shard_map/broadcast_in_dim | solution.py:226
  104.1 7.4 %all-to-all-start.2 = ((bf16[128,4,2048]{2,1,0:T(4,128)(2,1)}), bf16[128,4,2048]{2,1,0:T(4,128)(2,1)}, u32[]{:S(2)}, u32[]{:S(2)}) async-start(bf16[128,4,2048]{2,1,0:T(4,128)(2,1)} %broadcast_in_dim.18), calls=%async_computation.2 | async-start | bytes 4194304 | tf_op jit(solution)/shard_map/all_to_all | solution.py:227
  111.6 0.1 copy.56
  111.8 0.1 reshape.226
  111.9 28.7 %all-to-all-done.2 = bf16[128,4,2048]{2,1,0:T(4,128)(2,1)} async-done(((bf16[128,4,2048]{2,1,0:T(4,128)(2,1)}), bf16[128,4,2048]{2,1,0:T(4,128)(2,1)}, u32[]{:S(2)}, u32[]{:S(2)}) %all-to-all-start.2) | async-done | bytes 2097184 | tf_op jit(solution)/shard_map/all_to_all | solution.py:227
  140.6 4.0 %reshape.225 = bf16[512,2048]{1,0:T(8,128)(2,1)} reshape(bf16[128,4,2048]{2,1,0:T(4,128)(2,1)} %all-to-all-done.2) | data formatting | bytes 4194304 | tf_op jit(solution)/shard_map/reshape | solution.py:227
  144.5 3.9 %fusion.9 = f32[512,352]{0,1:T(8,128)} fusion(bf16[512,2048]{1,0:T(8,128)(2,1)} %reshape.225, bf16[2,2048,352]{1,2,0:T(8,128)(2,1)} %param.33), kind=kOutput, calls=%fused_computation.12 | convolution fusion | flops 738197504 | bytes 4259840 | tf_op jit(solution)/shard_map/dot_general | solution.py:236
  148.5 1.8 fusion.3
  150.3 0.4 fusion.60
  150.7 2.1 fusion.38
  152.8 6.8 %fusion.5 = f32[512,2048]{1,0:T(8,128)} fusion(bf16[2,352,2048]{2,1,0:T(8,128)(2,1)} %param.35, bf16[512,2048]{1,0:T(8,128)(2,1)} %reshape.225, bf16[2,2048,352]{1,2,0:T(8,128)(2,1)} %param.34, f32[512,352]{0,1:T(8,128)} %fusion.9, f32[512]{0:T(512)S(1)} %bitcast.125), kind=kOutput, calls=%fused_computation.8 | convolution fusion | flops 1477656576 | bytes 9897984 | tf_op jit(solution)/shard_map/dot_general | solution.py:239
  159.7 8.1 %convolution_add_fusion = f32[512,2048]{1,0:T(8,128)} fusion(f32[512,2048]{1,0:T(8,128)} %fusion.5, bf16[2,352,2048]{2,1,0:T(8,128)(2,1)} %param.35, bf16[512,2048]{1,0:T(8,128)(2,1)} %reshape.225, bf16[2,2048,352]{1,2,0:T(8,128)(2,1)} %param.34, f32[512,352]{0,1:T(8,128)} %fusion.3, f32[512]{0:T(512)S(1)} %bitcast.124), kind=kOutput, calls=%fused_computation.1 | convolution fusion | flops 1478705152 | bytes 14092288 | tf_op jit(solution)/shard_map/dot_general | solution.py:239
  167.7 1.9 add_dynamic-update-slice_fusion
  169.6 3.8 %convert_element_type.110 = bf16[512,2048]{1,0:T(8,128)(2,1)} convert(f32[512,2048]{1,0:T(8,128)} %add_dynamic-update-slice_fusion) | non-fusion elementwise | flops 1048576 | bytes 6291456 | tf_op jit(solution)/shard_map/convert_element_type | solution.py:252
  173.5 4.1 %reshape.227 = bf16[128,4,2048]{2,1,0:T(4,128)(2,1)} reshape(bf16[512,2048]{1,0:T(8,128)(2,1)} %convert_element_type.110) | data formatting | bytes 4194304 | tf_op jit(solution)/shard_map/reshape | solution.py:252
  177.6 35.3 %all_to_all.21 = bf16[128,4,2048]{2,1,0:T(4,128)(2,1)S(1)} all-to-all(bf16[128,4,2048]{2,1,0:T(4,128)(2,1)} %reshape.227), channel_id=1, replica_groups=mesh['x'=4,'z'=4,'y'=4,'core'=2] {'x','z','y','core'}, dimensions={0} | all-to-all | bytes 4194304 | tf_op jit(solution)/shard_map/all_to_all | solution.py:253
  212.9 0.9 convert_reduce_fusion
  213.8 0.6 broadcast_in_dim.21
  (78 shorter events, 2.1 us)
Async XLA Ops:
  6.5 5.1 %copy-start = (bf16[2048,576]{0,1:T(8,128)(2,1)S(1)}, bf16[2048,576]{0,1:T(8,128)(2,1)}, u32[]{:S(2)}) copy-start(bf16[2048,576]{0,1:T(8,128)(2,1)} %param.24) | copy-start | bytes 7077892
  6.5 3.0 %copy-start.16 = (s32[2]{0:T(128)S(1)}, s32[2]{0:T(128)}, u32[]{:S(2)}) copy-start(s32[2]{0:T(128)} %param.38) | copy-start | bytes 28
  6.5 3.4 %copy-start.12 = (f32[2048]{0:T(1024)S(1)}, f32[2048]{0:T(1024)}, u32[]{:S(2)}) copy-start(f32[2048]{0:T(1024)} %param.22) | copy-start | bytes 24580
  6.5 58.1 %all-gather.2.cloned.1.call-start = ((), (), s32[]{:S(2)}) async-start(), calls=%async_computation.4 | async-start | bytes 2228224 | tf_op jit(solution)/shard_map/all_gather | solution.py:178
  10.1 2.6 %copy-start.9 = (bf16[1,128,512]{2,1,0:T(8,128)(2,1)S(1)}, bf16[1,128,512]{2,1,0:T(8,128)(2,1)}, u32[]{:S(2)}) copy-start(bf16[1,128,512]{2,1,0:T(8,128)(2,1)} %param.26) | copy-start | bytes 393220
  12.7 9.9 %copy-start.14 = (s32[4,2,8]{2,1,0:T(2,128)S(1)}, s32[4,2,8]{2,1,0:T(2,128)}, u32[]{:S(2)}) copy-start(s32[4,2,8]{2,1,0:T(2,128)} %param.39) | copy-start | bytes 772
  12.8 10.0 %copy-start.15 = (f32[512]{0:T(512)S(1)}, f32[512]{0:T(512)}, u32[]{:S(2)}) copy-start(f32[512]{0:T(512)} %param.25) | copy-start | bytes 6148
  12.9 10.2 %collective-permute-start = (bf16[64,576]{1,0:T(8,128)(2,1)S(1)}, bf16[64,576]{1,0:T(8,128)(2,1)S(1)}, u32[]{:S(2)}, u32[]{:S(2)}) collective-permute-start(bf16[64,576]{1,0:T(8,128)(2,1)S(1)} %pad_maximum_fusion.1), channel_id=1, source_target_pairs={{0,32},{32,64},{64,96},{96,0},{1,33},{33,65},{65,97},{97,1},{2,34}... | collective-permute-start | bytes 221192 | tf_op jit(solution)/shard_map/ppermute | solution.py:33
  14.5 8.6 %collective-permute-start.1 = (bf16[64,576]{1,0:T(8,128)(2,1)S(1)}, bf16[64,576]{1,0:T(8,128)(2,1)S(1)}, u32[]{:S(2)}, u32[]{:S(2)}) collective-permute-start(bf16[64,576]{1,0:T(8,128)(2,1)S(1)} %pad_maximum_fusion.1), channel_id=1, source_target_pairs={{0,64},{32,96},{64,0},{96,32},{1,65},{33,97},{65,1},{97,33},{2,66}... | collective-permute-start | bytes 221192 | tf_op jit(solution)/shard_map/ppermute | solution.py:33
  17.2 5.9 %collective-permute-start.2 = (bf16[64,576]{1,0:T(8,128)(2,1)S(1)}, bf16[64,576]{1,0:T(8,128)(2,1)S(1)}, u32[]{:S(2)}, u32[]{:S(2)}) collective-permute-start(bf16[64,576]{1,0:T(8,128)(2,1)S(1)} %pad_maximum_fusion.1), channel_id=1, source_target_pairs={{0,96},{32,0},{64,32},{96,64},{1,97},{33,1},{65,33},{97,65},{2,98}... | collective-permute-start | bytes 221192 | tf_op jit(solution)/shard_map/ppermute | solution.py:33
  22.6 42.1 %copy-start.5 = (s32[2,8,64]{2,1,0:T(8,128)S(1)}, s32[2,8,64]{2,1,0:T(8,128)}, u32[]{:S(2)}) copy-start(s32[2,8,64]{2,1,0:T(8,128)} %table_ref.1) | copy-start | bytes 12292
  23.2 12.7 %collective-permute-start.3 = (bf16[4,64,576]{2,1,0:T(8,128)(2,1)S(1)}, bf16[4,64,576]{2,1,0:T(8,128)(2,1)S(1)}, u32[]{:S(2)}, u32[]{:S(2)}) collective-permute-start(bf16[4,64,576]{2,1,0:T(8,128)(2,1)S(1)} %pad_maximum_fusion), channel_id=1, source_target_pairs={{0,8},{8,16},{16,24},{24,0},{1,9},{9,17},{17,25},{25,1},{2,10},{10... | collective-permute-start | bytes 884744 | tf_op jit(solution)/shard_map/ppermute | solution.py:33
  25.2 18.6 %collective-permute-start.4 = (bf16[4,64,576]{2,1,0:T(8,128)(2,1)S(1)}, bf16[4,64,576]{2,1,0:T(8,128)(2,1)S(1)}, u32[]{:S(2)}, u32[]{:S(2)}) collective-permute-start(bf16[4,64,576]{2,1,0:T(8,128)(2,1)S(1)} %pad_maximum_fusion), channel_id=1, source_target_pairs={{0,16},{8,24},{16,0},{24,8},{1,17},{9,25},{17,1},{25,9},{2,18},{10... | collective-permute-start | bytes 884744 | tf_op jit(solution)/shard_map/ppermute | solution.py:33
  28.8 15.1 %collective-permute-start.5 = (bf16[4,64,576]{2,1,0:T(8,128)(2,1)S(1)}, bf16[4,64,576]{2,1,0:T(8,128)(2,1)S(1)}, u32[]{:S(2)}, u32[]{:S(2)}) collective-permute-start(bf16[4,64,576]{2,1,0:T(8,128)(2,1)S(1)} %pad_maximum_fusion), channel_id=1, source_target_pairs={{0,24},{8,0},{16,8},{24,16},{1,25},{9,1},{17,9},{25,17},{2,26},{10... | collective-permute-start | bytes 884744 | tf_op jit(solution)/shard_map/ppermute | solution.py:33
  44.0 1.0 copy-start.3
  64.7 1.5 copy-start.1
  66.2 1.6 copy-start.2
  67.8 1.3 copy-start.4
  69.1 19.1 %copy-start.8 = (bf16[128,2048]{1,0:T(8,128)(2,1)S(1)}, bf16[128,2048]{1,0:T(8,128)(2,1)}, u32[]{:S(2)}) copy-start(bf16[128,2048]{1,0:T(8,128)(2,1)} %param.28) | copy-start | bytes 1572868
  74.3 27.3 %copy-start.13 = (f32[2048]{0:T(1024)S(1)}, f32[2048]{0:T(1024)}, u32[]{:S(2)}) copy-start(f32[2048]{0:T(1024)} %param.29) | copy-start | bytes 24580
  89.2 12.1 %all-to-all-start.1 = ((bf16[16,4,2048]{2,1,0:T(4,128)(2,1)}), bf16[16,4,2048]{2,1,0:T(4,128)(2,1)S(1)}, u32[]{:S(2)}, u32[]{:S(2)}) async-start(bf16[16,4,2048]{2,1,0:T(4,128)(2,1)} %reshape.224), calls=%async_computation.1 | async-start | bytes 524288 | tf_op jit(solution)/shard_map/all_to_all | solution.py:221
  104.1 7.4 %copy-start.10 = (f32[4,128,6]{1,0,2:T(4,128)S(1)}, f32[4,128,6]{1,0,2:T(4,128)}, u32[]{:S(2)}) copy-start(f32[4,128,6]{1,0,2:T(4,128)} %param.41) | copy-start | bytes 36868
  104.1 7.4 %copy-start.11 = (s32[4,128,6]{1,0,2:T(4,128)S(1)}, s32[4,128,6]{1,0,2:T(4,128)}, u32[]{:S(2)}) copy-start(s32[4,128,6]{1,0,2:T(4,128)} %param.40) | copy-start | bytes 36868
  104.1 36.5 %all-to-all-start.2 = ((bf16[128,4,2048]{2,1,0:T(4,128)(2,1)}), bf16[128,4,2048]{2,1,0:T(4,128)(2,1)}, u32[]{:S(2)}, u32[]{:S(2)}) async-start(bf16[128,4,2048]{2,1,0:T(4,128)(2,1)} %broadcast_in_dim.18), calls=%async_computation.2 | async-start | bytes 4194304 | tf_op jit(solution)/shard_map/all_to_all | solution.py:227
  144.5 3.9 %copy-start.6 = (bf16[512,2048]{1,0:T(8,128)(2,1)S(1)}, bf16[512,2048]{1,0:T(8,128)(2,1)}, u32[]{:S(2)}) copy-start(bf16[512,2048]{1,0:T(8,128)(2,1)} %reshape.225) | copy-start | bytes 6291460
  144.5 3.9 %copy-start.17 = (bf16[2,2048,352]{1,2,0:T(8,128)(2,1)S(1)}, bf16[2,2048,352]{1,2,0:T(8,128)(2,1)}, u32[]{:S(2)}) copy-start(bf16[2,2048,352]{1,2,0:T(8,128)(2,1)} %param.33) | copy-start | bytes 8650756
  148.5 1.8 copy-start.7
Sparse Core Ops, SparseCore 0:
  9.5 55.1 all-gather.1

commit v2 on v1

v2 whole, which is shorter than its diff:
```python
import functools

import jax
import jax.numpy as jnp
import numpy as np
from jax import lax
from jax.experimental import pallas as pl
from jax.experimental.pallas import tpu as pltpu
from jax.sharding import Mesh, PartitionSpec as P

FFE = 1408
THETA = 50000.0
EPS = 1e-06
NEG = -1e30
CAPACITY = 24
SLOTS = 4 * CAPACITY
OWN_ROWS = 64

BLK = ("x", "z")
BEAM = ("y", "core")
OUT_ORDER = BLK + BEAM
CORES = [(0, 1), (1, 0)]

f32, bf16 = jnp.float32, jnp.bfloat16
LAST = (((1,), (1,)), ((), ()))


def lanes(shape):
    return lax.broadcasted_iota(jnp.int32, shape, len(shape) - 1)


def sublanes(shape):
    return lax.broadcasted_iota(jnp.int32, shape, len(shape) - 2)


def kernel_call(body, name, outs, scratch, cost, smem, *args):
    vmem = pl.BlockSpec(memory_space=pltpu.VMEM)
    first = [pl.BlockSpec(memory_space=pltpu.SMEM)] if smem else []
    return pl.pallas_call(
        body,
        out_shape=[jax.ShapeDtypeStruct(shape, dtype) for shape, dtype in outs],
        in_specs=first + [vmem] * (len(args) - len(first)),
        out_specs=[vmem] * len(outs),
        scratch_shapes=scratch,
        compiler_params=pltpu.CompilerParams(vmem_limit_bytes=24 << 20),
        cost_estimate=pl.CostEstimate(flops=cost[0], bytes_accessed=cost[1], transcendentals=cost[2]),
        name=name,
    )(*args)


def shifted(value, axis, by):
    size = lax.axis_size(axis)
    return lax.ppermute(value, axis, [(i, (i + by) % size) for i in range(size)])


def gather_blk(value, near, far):
    first = jnp.stack([value] + [shifted(value, near, s) for s in range(1, 4)])
    return [first] + [shifted(first, far, s) for s in range(1, 4)]


def rope_parts(cos_ref, rows):
    cosine, sine = cos_ref[:, :64], cos_ref[:, 64:]
    wide = lambda v: jnp.concatenate([jnp.broadcast_to(v[k : k + 1], (8, 64)) for k in range(rows // 8)], axis=0)
    return wide(cosine), wide(sine)


def turned(values, precision=None):
    i, j = sublanes((64, 64)), lanes((64, 64))
    turn = jnp.where(i == j - 32, 1.0, 0.0) - jnp.where(i == j + 32, 1.0, 0.0)
    return jnp.dot(values, turn.astype(values.dtype), precision=precision, preferred_element_type=f32)


def query_kernel(embeds_ref, gain_ref, query_ref, key_up_ref, cos_ref, first_ref, second_ref, normed_ref):
    steps, _, width = embeds_ref.shape
    tokens = [embeds_ref[t].astype(f32) for t in range(steps)]
    tokens = jnp.concatenate([tokens[t][8 * g : 8 * g + 8] for g in range(2) for t in range(steps)], axis=0)
    mean_sq = jnp.sum(tokens * tokens, axis=1, keepdims=True) * (1.0 / width)
    normed = (tokens * lax.rsqrt(mean_sq + EPS) * gain_ref[...]).astype(bf16)
    normed_ref[...] = normed
    queries = lax.dot_general(normed, query_ref[...], LAST, preferred_element_type=f32).astype(bf16)
    latent = jnp.dot(queries[:, :128], key_up_ref[0], preferred_element_type=f32).astype(bf16)
    rope = queries[:, 128:]
    cosine, sine = rope_parts(cos_ref, 64)
    rope = (rope.astype(f32) * cosine + turned(rope) * sine).astype(bf16)
    for g, ref in enumerate((first_ref, second_ref)):
        ref[:, :512] = latent[32 * g : 32 * g + 32]
        ref[:, 512:] = rope[32 * g : 32 * g + 32]


def entry_kernel(normed_ref, latent_ref, gain_ref, cos_ref, out_ref):
    projected = lax.dot_general(normed_ref[...], latent_ref[...], LAST, preferred_element_type=f32)
    latent, rope = projected[:, :512], projected[:, 512:]
    mean_sq = jnp.sum(latent * latent, axis=1, keepdims=True) * (1.0 / 512)
    out_ref[:, :512] = (latent * lax.rsqrt(mean_sq + EPS) * gain_ref[...]).astype(bf16)
    cosine, sine = rope_parts(cos_ref, 64)
    out_ref[:, 512:] = (rope * cosine + turned(rope, lax.Precision.HIGHEST) * sine).astype(bf16)


def split_terms(line):
    first = line.astype(bf16).astype(f32)
    second = (line - first).astype(bf16).astype(f32)
    third = line - first - second
    place = sublanes((16, line.shape[1]))
    tile = jnp.where(place == 0, first, 0.0)
    tile = jnp.where(place == 1, second, tile)
    return jnp.where(place == 2, third, tile).astype(bf16)


def joined_terms(tile):
    tile = tile.astype(f32)
    return tile[0:1] + tile[1:2] + tile[2:3]


def as_line(column, offset=0):
    shape = (column.shape[0], 128)
    return jnp.sum(jnp.where(lanes(shape) == sublanes(shape) + offset, column, 0.0), axis=0, keepdims=True)


def as_column(line, count, offset=0):
    shape = (count, 128)
    return jnp.sum(jnp.where(lanes(shape) == sublanes(shape) + offset, line, 0.0), axis=1, keepdims=True)


def attend_kernel(g, info_ref, *refs):
    q_refs = refs[:4]
    cache_ref, entry_ref, parent_ref, table_ref = refs[4:8]
    out_refs = refs[8:]
    near, rows, width = q_refs[0].shape
    heads = 4 * near
    beams = table_ref.shape[1]
    steps = rows // beams
    pool, _, block_len = cache_ref.shape[1:]
    latent = out_refs[0].shape[1]
    scale = (width - latent + 128) ** (-0.5)
    blk = info_ref[0]
    shape = (beams, 128)
    origin = (lanes(shape) == sublanes(shape)).astype(f32)
    kept = []
    for t in range(steps):
        choose = (lanes((beams, beams)) == parent_ref[g, :, t : t + 1]).astype(f32)
        origin = jnp.dot(choose, origin, preferred_element_type=f32)
        origin = origin + (lanes(shape) == sublanes(shape) + beams * (1 + t)).astype(f32)
        kept.append(origin)
    origin = jnp.concatenate(kept, axis=0)
    table = table_ref[g]
    live = lanes(table.shape) < info_ref[1 + g]
    used = jnp.zeros((beams, 128), f32)
    for p in range(pool):
        hit = jnp.where((table == blk * pool + p) & live, 1.0, 0.0)
        hit = jnp.max(hit, axis=1, keepdims=True)
        used = used + jnp.where(lanes(used.shape) == p, hit, 0.0)
    used = jnp.dot(origin[:, :beams], used, preferred_element_type=f32)
    bias = jnp.concatenate(
        [jnp.broadcast_to(used[:, p : p + 1], (rows, block_len)) for p in range(pool)], axis=1
    )
    bias = jnp.where(bias > 0.5, 0.0, NEG)
    seen = origin[:, beams : beams + rows]
    recent_bias = jnp.where((seen > 0.5) & (blk == 0), 0.0, NEG)

    q = jnp.concatenate([ref[...] for ref in q_refs], axis=0).reshape(heads * rows, width)
    keys = jnp.concatenate([cache_ref[g, p] for p in range(pool)], axis=1)
    entry = entry_ref[g * rows : (g + 1) * rows]
    scores = jnp.dot(q, keys, preferred_element_type=f32)
    scores = scores.reshape(heads, rows, pool * block_len) * scale + bias[None]
    recent = lax.dot_general(q, entry, LAST, preferred_element_type=f32)
    recent = recent.reshape(heads, rows, rows) * scale + recent_bias[None]
    top = jnp.maximum(
        jnp.max(scores, axis=-1, keepdims=True), jnp.max(recent, axis=-1, keepdims=True)
    )
    weights = jnp.exp(scores - top)
    recent = jnp.exp(recent - top)
    total = jnp.sum(weights, axis=-1, keepdims=True) + jnp.sum(recent, axis=-1, keepdims=True)
    weights = weights.astype(bf16).reshape(heads * rows, pool * block_len)
    recent = recent.astype(bf16).reshape(heads * rows, rows)
    lat = lax.dot_general(weights, keys[:latent], LAST, preferred_element_type=f32)
    lat = lat + jnp.dot(recent, entry[:, :latent], preferred_element_type=f32)
    lat = (lat.reshape(heads, rows, latent) / total).astype(bf16)
    lse = jnp.where(top > 0.1 * NEG, top + jnp.log(total), NEG)
    for s, ref in enumerate(out_refs):
        for f in range(4):
            ref[f * rows : (f + 1) * rows, :] = lat[f * near + s]
        column = jnp.concatenate([lse[f * near + s] for f in range(4)], axis=0)
        ref[4 * rows :, :128] = split_terms(as_line(column))
        ref[4 * rows :, 128:] = jnp.zeros((16, latent - 128), bf16)


def shares(sums):
    best = functools.reduce(jnp.maximum, sums)
    parts = [jnp.exp(v - best) for v in sums]
    whole = functools.reduce(jnp.add, parts)
    return [p / whole for p in parts], best + jnp.log(whole)


def merge_kernel(*refs):
    parts, outs = refs[:4], refs[4:]
    part_share, whole = shares([joined_terms(ref[128:, :128]) for ref in parts])
    merged = sum(as_column(p, 128) * ref[:128, :].astype(f32) for p, ref in zip(part_share, parts))
    merged = merged.astype(bf16)
    tile = split_terms(whole)
    for f, ref in enumerate(outs):
        ref[:32, :] = merged[32 * f : 32 * f + 32]
        ref[32:, :128] = tile
        ref[32:, 128:] = jnp.zeros((16, ref.shape[1] - 128), bf16)


def output_kernel(*refs):
    value_ref, out_ref, result_ref = refs[8:]
    joined = []
    for g in range(2):
        parts = refs[4 * g : 4 * g + 4]
        lines = [joined_terms(ref[32:, :128]) for ref in parts]
        columns = [as_column(line, 32, 32 * f) for f, line in enumerate(lines)]
        part_share, _ = shares(columns)
        joined.append(sum(p * ref[:32, :].astype(f32) for p, ref in zip(part_share, parts)))
    attended = jnp.concatenate(joined, axis=0).astype(bf16)
    head_out = jnp.dot(attended, value_ref[0], preferred_element_type=f32).astype(bf16)
    line, row = sublanes((128, 64)), lanes((128, 64))
    source = 32 * (line >> 6) + 8 * ((line >> 1) & 3) + ((line >> 3) & 7)
    result = None
    for q in range(2):
        take = jnp.where((source == row) & ((line & 1) == q), 1.0, 0.0).astype(bf16)
        rows = jnp.dot(take, head_out, preferred_element_type=f32).astype(bf16)
        term = jnp.dot(rows, out_ref[:, q * 1024 : (q + 1) * 1024], preferred_element_type=f32)
        result = term if result is None else result + term
    result_ref[...] = result.astype(bf16)


def norm_kernel(info_ref, parts_ref, embeds_ref, gain_ref, spread_ref, resid_ref):
    blk = info_ref[1]
    steps, rows, width = embeds_ref.shape
    half = width // 2
    line = sublanes((2 * steps, half))
    resid = jnp.sum(parts_ref[...].astype(f32), axis=0)
    gain = jnp.zeros((2 * steps, half), f32)
    for q in range(2):
        columns = slice(q * half, (q + 1) * half)
        gain = gain + jnp.where((line & 1) == q, gain_ref[:, columns], 0.0)
        for t in range(steps):
            token = jnp.where(sublanes((rows, half)) == blk, embeds_ref[t, :, columns].astype(f32), 0.0)
            token = jnp.sum(token, axis=0, keepdims=True)
            resid = resid + jnp.where(line == 2 * t + q, token, 0.0)
    resid_ref[...] = resid
    sums = jnp.broadcast_to(jnp.sum(resid * resid, axis=1, keepdims=True), (2 * steps, 128))
    pair = jnp.where((sublanes((8, 8)) >> 1) == (lanes((8, 8)) >> 1), 1.0, 0.0)
    sums = jnp.dot(pair, sums, precision=lax.Precision.HIGHEST, preferred_element_type=f32)
    normed = (resid * lax.rsqrt(sums[:, :1] * (1.0 / width) + EPS) * gain).astype(bf16)
    spread_ref[...] = jnp.broadcast_to(normed[None], spread_ref.shape)


def line_row(line, core):
    chip = (line >> 3) & 63
    return 32 * (chip >> 4) + 16 * ((line >> 9) ^ core) + (chip & 15)


def route_kernel(info_ref, ids_ref, weights_ref, out_ref):
    core = info_ref[0]
    top, steps, rows = ids_ref.shape
    line = lanes((rows, out_ref.shape[1]))
    row = line_row(line, core)
    earlier = jnp.where(sublanes((rows, rows)) < lanes((rows, rows)), 1.0, 0.0).astype(bf16)
    slots, weights = [], []
    for e in range(2):
        expert = info_ref[3 + e]
        weight = jnp.zeros((steps, rows), f32)
        routed = jnp.zeros((steps, rows), f32)
        for k in range(top):
            match = ids_ref[k] == expert
            weight = weight + jnp.where(match, weights_ref[k], 0.0)
            routed = routed + jnp.where(match, 1.0, 0.0)
        wide = jnp.concatenate([routed, jnp.zeros((8 - steps, rows), f32)], axis=0).astype(bf16)
        rank = jnp.dot(wide, earlier, preferred_element_type=f32)[:steps]
        first = (sublanes((steps, rows)) * CAPACITY + 1).astype(f32)
        slots.append(jnp.where(routed > 0.5, rank + first, 0.0))
        weights.append(weight)
    total = jnp.zeros(out_ref.shape, f32)
    for t in range(steps):
        place = sublanes((8, rows))
        values = jnp.zeros((8, rows), f32)
        for k, value in enumerate(slots + weights):
            values = jnp.where(place == k, value[t : t + 1], values)
        take = jnp.where((sublanes(line.shape) == row) & (((line >> 1) & 3) == t), 1.0, 0.0)
        total = total + jnp.dot(values, take, precision=lax.Precision.HIGHEST, preferred_element_type=f32)
    out_ref[...] = total


def moe_kernel(
    info_ref,
    mine_ref,
    other_ref,
    route_ref,
    resid_ref,
    gate_ref,
    up_ref,
    down_ref,
    shared_gate_ref,
    shared_up_ref,
    shared_down_ref,
    own_out_ref,
    other_out_ref,
    x_ref,
    y_ref,
):
    f32, bf16 = jnp.float32, jnp.bfloat16
    core, blk, y = info_ref[0], info_ref[1], info_ref[2]
    lines, half = mine_ref.shape
    experts, units, width = gate_ref.shape
    slots, own_rows = SLOTS, OWN_ROWS
    total = experts * slots + own_rows
    line = lanes((1, 2 * lines))
    step = (line >> 1) & 3
    row = line_row(line, core)
    place = ((row & 1) ^ core) * (lines // 2) + (row >> 1) * 4 + step
    first = (line & 1) == 0

    hits = []
    for e in range(experts):
        slot = sublanes((slots, 2 * lines)) + 1
        hits.append(slot == route_ref[e : e + 1, :].astype(jnp.int32))
    own_line = jnp.where(line < lines, (line >> 1) - y * own_rows, -1)
    hits.append(sublanes((own_rows, 2 * lines)) == own_line)
    weights = [
        jnp.sum(jnp.where(hits[e] & first, route_ref[experts + e : experts + e + 1, :], 0.0), axis=1, keepdims=True)
        for e in range(experts)
    ]
    hit = jnp.concatenate([jnp.where(h, 1.0, 0.0) for h in hits], axis=0)
    for q in range(2):
        pick = jnp.where((line & 1) == q, hit, 0.0).astype(bf16)
        rows = jnp.dot(pick[:, :lines], mine_ref[...], preferred_element_type=f32)
        rows = rows + jnp.dot(pick[:, lines:], other_ref[...], preferred_element_type=f32)
        x_ref[:, q * half : (q + 1) * half] = rows.astype(bf16)
    parts = place + 1
    parts = jnp.where(sublanes((8, 2 * lines)) == 0, parts >> 4, parts & 15).astype(f32)
    parts = jnp.where(first, parts, 0.0).astype(bf16)
    spot = lax.dot_general(parts, hit.astype(bf16), LAST, preferred_element_type=f32)
    spot = (spot[0:1] * 16.0 + spot[1:2] - 1.0).astype(jnp.int32)

    def gated(x, gate, up):
        gate_val = lax.dot_general(x, gate, LAST, preferred_element_type=f32)
        up_val = lax.dot_general(x, up, LAST, preferred_element_type=f32)
        return (gate_val / (1.0 + jnp.exp(-gate_val)) * up_val).astype(bf16)

    for e in range(experts):
        part = slice(e * slots, (e + 1) * slots)
        act = gated(x_ref[part, :], gate_ref[e], up_ref[e])
        down = jnp.dot(act, down_ref[e], preferred_element_type=f32)
        y_ref[part, :] = (down * weights[e]).astype(bf16)
    part = slice(experts * slots, total)
    act = gated(x_ref[part, :], shared_gate_ref[...], shared_up_ref[...])
    own = jnp.dot(act, shared_down_ref[...], preferred_element_type=f32)
    for t in range(4):
        whole = jnp.concatenate([resid_ref[2 * t + q : 2 * t + q + 1, :] for q in range(2)], axis=1)
        own = own + jnp.where(sublanes((own_rows, 1)) == blk * 4 + t, whole, 0.0)
    y_ref[part, :] = own.astype(bf16)

    for side, ref in ((0, own_out_ref), (1, other_out_ref)):
        out_line = sublanes((lines, 1))
        out_place = (out_line >> 1) + side * (lines // 2)
        put = jnp.where(out_place == spot, 1.0, 0.0)
        result = None
        for q in range(2):
            put_q = jnp.where((out_line & 1) == q, put, 0.0).astype(bf16)
            term = jnp.dot(put_q, y_ref[:, q * half : (q + 1) * half], preferred_element_type=f32)
            result = term if result is None else result + term
        ref[...] = result.astype(bf16)


def per_device(
    embeds,
    attn_gain,
    w_query,
    w_latent,
    latent_gain,
    w_key_up,
    w_value_up,
    w_out,
    ffn_gain,
    w_shared_gate,
    w_shared_up,
    w_shared_down,
    w_expert_gate,
    w_expert_up,
    w_expert_down,
    cache_pool,
    block_tables,
    block_counts,
    parents,
    expert_ids,
    expert_weights,
):
    steps, row_dev, width = embeds.shape
    groups, beams, _ = block_tables.shape
    latent = w_key_up.shape[2]
    block_len, entry_width = cache_pool.shape[2:]
    rope = entry_width - latent
    pair_dev, _, unit_dev = w_expert_gate.shape
    half = width // 2
    chips = expert_ids.shape[1] // 2
    lines = chips * 2 * steps
    y, core = lax.axis_index("y"), lax.axis_index("core")
    blk, beam = lax.axis_index(BLK), lax.axis_index(BEAM)
    expert = blk * pair_dev * 2 + beam * unit_dev // FFE
    place = jnp.stack([core, blk, y, expert, expert + 2]).astype(jnp.int32)
    counts = jnp.concatenate([blk[None], block_counts]).astype(jnp.int32)

    position = (block_counts * block_len).astype(f32)[:, None] + jnp.arange(steps, dtype=f32)
    frequency = np.float64(THETA) ** (-np.arange(rope // 2) * 2.0 / rope)
    frequency = np.tile(frequency.astype(np.float32), 4)
    turn = np.repeat(np.array([0.0, 1.0], np.float32), rope)
    angles = position.reshape(-1, 1) * frequency
    cosines = jnp.where(turn == 0.0, jnp.cos(angles), jnp.sin(angles))
    rows_group = steps * beams
    rows_all = groups * rows_group
    query = ((rows_group, entry_width), bf16)
    first, second, normed = kernel_call(
        query_kernel,
        "query",
        [query, query, ((rows_all, width), bf16)],
        [],
        (60_000_000, 1_500_000, 0),
        False,
        embeds,
        attn_gain.reshape(1, width),
        w_query.T,
        w_key_up,
        cosines,
    )
    queries = (gather_blk(first, "x", "z"), gather_blk(second, "z", "x"))
    (entries,) = kernel_call(
        entry_kernel,
        "entry",
        [((rows_all, entry_width), bf16)],
        [],
        (150_000_000, 2_700_000, 0),
        False,
        normed,
        w_latent.T,
        latent_gain.reshape(1, latent),
        cosines,
    )
    (route,) = kernel_call(
        route_kernel,
        "route",
        [((8, 2 * lines), f32)],
        [],
        (60_000_000, 60_000, 0),
        True,
        place,
        expert_ids.transpose(2, 0, 1),
        expert_weights.transpose(2, 0, 1),
    )
    cache = cache_pool.transpose(0, 1, 3, 2)
    ancestry = parents.transpose(1, 2, 0)
    part = ((4 * rows_group + 16, latent), bf16)
    last = ((rows_group + 16, latent), bf16)
    final = []
    for g, (near, far) in enumerate((("x", "z"), ("z", "x"))):
        parts = kernel_call(
            functools.partial(attend_kernel, g),
            "attend",
            [part] * 4,
            [],
            (900_000_000, 2_500_000, 400_000),
            True,
            counts,
            *queries[g],
            cache,
            entries,
            ancestry,
            block_tables,
        )
        parts = [parts[0]] + [shifted(parts[s], near, -s) for s in range(1, 4)]
        merged = kernel_call(merge_kernel, "merge", [last] * 4, [], (2_000_000, 800_000, 1_000), False, *parts)
        final += [merged[0]] + [shifted(merged[f], far, -f) for f in range(1, 4)]
    (attn_part,) = kernel_call(
        output_kernel,
        "output",
        [((row_dev * 2 * steps, half), bf16)],
        [],
        (80_000_000, 1_500_000, 1_000),
        False,
        *final,
        w_value_up,
        w_out,
    )
    attn_part = lax.all_to_all(attn_part.reshape(row_dev, 2 * steps, half), BLK, 0, 0)
    spread, resid = kernel_call(
        norm_kernel,
        "norm",
        [((chips, 2 * steps, half), bf16), ((2 * steps, half), f32)],
        [],
        (1_000_000, 1_700_000, 0),
        True,
        place,
        attn_part,
        embeds,
        ffn_gain.reshape(1, width),
    )

    mine = lax.all_to_all(spread, ("y", "x", "z"), 0, 0).reshape(lines, half)
    other = lax.ppermute(mine, "core", CORES)
    total = pair_dev * SLOTS + OWN_ROWS
    own_out, other_out = kernel_call(
        moe_kernel,
        "moe",
        [((lines, half), bf16)] * 2,
        [pltpu.VMEM((total, width), bf16)] * 2,
        (4_000_000_000, 15_000_000, 300_000),
        True,
        place,
        mine,
        other,
        route,
        resid,
        w_expert_gate.transpose(0, 2, 1),
        w_expert_up.transpose(0, 2, 1),
        w_expert_down,
        w_shared_gate.T,
        w_shared_up.T,
        w_shared_down,
    )
    own_out = own_out.astype(f32) + lax.ppermute(other_out, "core", CORES).astype(f32)
    own_out = own_out.astype(bf16).reshape(chips, 2 * steps, half)
    result = jnp.sum(lax.all_to_all(own_out, ("x", "z", "y"), 0, 0).astype(f32), axis=0)
    return result.reshape(steps, 1, width)


def solution(mesh):
    devices = mesh.devices.reshape(4, 4, 4, 2)
    split = Mesh(devices, ("x", "z", "y", "core"))
    placed = (
        P(None, BEAM, None),
        P(),
        P(None, BLK),
        P(),
        P(),
        P(BLK, None, None),
        P(BLK, None, None),
        P(BLK, None),
        P(),
        P(None, BLK),
        P(None, BLK),
        P(BLK, None),
        P(BLK, None, BEAM),
        P(BLK, None, BEAM),
        P(BLK, BEAM, None),
        P(BEAM, BLK, None, None),
        P(BEAM, None, None),
        P(BEAM),
        P(None, BEAM, None),
        P(),
        P(),
    )
    return jax.shard_map(
        per_device,
        mesh=split,
        in_specs=placed,
        out_specs=P(None, OUT_ORDER, None),
        check_vma=False,
    )
```

time: 223 us -> 139 us (0.62)
  waiting for transfers between devices: 70.6 us -> 19.2 us
  matrix products: 25.9 us -> 0 us
  starting transfers between devices: 23.3 us -> 40.1 us
  between operations: 13.7 us -> 0.27 us
  Pallas kernels: 5.14 us -> 18.2 us
  local copies, waits for them, and re-layouts: 23.2 us -> 12.4 us
  other arithmetic: 10.5 us -> 2.89 us
  blocking collectives: 48.9 us -> 44.9 us
    all_to_all x2 -> x1, waiting for transfers between devices: 36.2 us -> 8.32 us  [per_device(): lax.all_to_all(attn_part.reshape(row_dev, 2 * steps, half), BLK, 0, 0)]
    dot_general x10 -> x0, matrix products: 25.9 us -> none  [the longest x2 14.9 us: per_device(): down = jnp.dot(activation, w_expert_down[e], preferred_element_type=f32)]
    ppermute x6 -> x24, starting transfers between devices: 12.3 us -> 36.3 us  [shifted(): lax.ppermute(value, axis, [(i, (i + by) % size) for i in range(size)])]
    all_gather x1 -> x0, waiting for transfers between devices: 19.7 us -> none  [per_device(): w_value = lax.all_gather(w_value_up, BLK, axis=0, tiled=True)]
    pallas_call x1 -> x10, Pallas kernels: 5.14 us -> 18.2 us  [kernel_call(): pl.pallas_call(body, out_shape=[jax.ShapeDtypeStruct(shape, dtype) for sh...]
    reshape x4 -> x1, local copies, waits for them, and re-layouts: 8.98 us -> 0.66 us  [per_device(): return result.reshape(steps, 1, width)]
    all_to_all x2 -> x1, starting transfers between devices: 11 us -> 3.53 us  [per_device(): lax.all_to_all(attn_part.reshape(row_dev, 2 * steps, half), BLK, 0, 0)]
    ppermute x6 -> x24, waiting for transfers between devices: 14 us -> 7.43 us  [shifted(): lax.ppermute(value, axis, [(i, (i + by) % size) for i in range(size)])]
  transfers between devices with their start and end apart: 9 -> 27, of which waited for: 5 -> 8; matrix products, arithmetic and copies ran while one was open for 5% -> 1% of each run, Pallas kernels for 0% -> 6%
where the time goes in v2:
time: 139 us; the launch traced here: 138 us
  blocking collectives  44.9 us (32%)
  starting transfers between devices  40.1 us (29%)
  waiting for transfers between devices  19.2 us (14%)
  Pallas kernels  18.2 us (13%)
  local copies, waits for them, and re-layouts  12.4 us (9%)
  other arithmetic  2.89 us (2%)
    ppermute x24, starting transfers between devices, shifted(): lax.ppermute(value, axis, [(i, (i + by) % size) for i in range(size)])  36.3 us
    all_to_all x1, blocking collectives, per_device(): lax.all_to_all(own_out, ('x', 'z', 'y'), 0, 0).astype(f32)  23.3 us
    all_to_all x1, blocking collectives, per_device(): mine = lax.all_to_all(spread, ('y', 'x', 'z'), 0, 0).reshape(lines, half)  21.5 us
    pallas_call x10, Pallas kernels, kernel_call(): pl.pallas_call(body, out_shape=[jax.ShapeDtypeStruct(shape, dtype) for sh...  18.2 us
    unnamed x41, local copies, waits for them, and re-layouts  11.6 us
    all_to_all x1, waiting for transfers between devices, per_device(): lax.all_to_all(attn_part.reshape(row_dev, 2 * steps, half), BLK, 0, 0)  8.32 us
    ppermute x24, waiting for transfers between devices, shifted(): lax.ppermute(value, axis, [(i, (i + by) % size) for i in range(size)])  7.43 us
    all_to_all x1, starting transfers between devices, per_device(): lax.all_to_all(attn_part.reshape(row_dev, 2 * steps, half), BLK, 0, 0)  3.53 us
  transfers between devices with their start and end apart: 27, of which 8 were waited for; matrix products, arithmetic and copies ran while one was open for 1% of the time, Pallas kernels for 6%

profile of v2, /device:TPU:0, one launch (start us, length us, event | category | flops | bytes accessed | tf_op | source)
XLA Modules:
  0.0 137.9 jit_solution(3130662579936343872)
XLA Ops:
  0.0 0.7 multiply_convert_fusion
  0.8 0.8 fusion.1.cos_ref
  1.6 0.9 copy-done.1
  2.6 1.1 copy-done.3
  3.7 0.9 copy-done.5
  4.6 0.7 copy-done.7
  5.9 4.2 %collective-permute-start.14 = (bf16[32,576]{1,0:T(8,128)(2,1)S(1)}, bf16[32,576]{1,0:T(8,128)(2,1)S(1)}, u32[]{:S(2)}, u32[]{:S(2)}) collective-permute-start(bf16[32,576]{1,0:T(8,128)(2,1)S(1)} %get-tuple-element.38), channel_id=1, source_target_pairs={{0,24},{8,0},{16,8},{24,16},{1,25},{9,1},{17,9},{25,17},{2,26},{10... | collective-permute-start | bytes 110600 | tf_op jit(solution)/shard_map/ppermute | solution.py:53
  10.0 1.3 collective-permute-start.12
  11.3 2.8 %collective-permute-start.2 = (bf16[32,576]{1,0:T(8,128)(2,1)S(1)}, bf16[32,576]{1,0:T(8,128)(2,1)S(1)}, u32[]{:S(2)}, u32[]{:S(2)}) collective-permute-start(bf16[32,576]{1,0:T(8,128)(2,1)S(1)} %get-tuple-element.28), channel_id=1, source_target_pairs={{0,96},{32,0},{64,32},{96,64},{1,97},{33,1},{65,33},{97,65},{2,98}... | collective-permute-start | bytes 110600 | tf_op jit(solution)/shard_map/ppermute | solution.py:53
  14.1 0.8 collective-permute-start.1
  14.9 0.9 collective-permute-start
  15.8 2.8 %collective-permute-start.17 = (bf16[4,32,576]{2,1,0:T(8,128)(2,1)S(1)}, bf16[4,32,576]{2,1,0:T(8,128)(2,1)S(1)}, u32[]{:S(2)}, u32[]{:S(2)}) collective-permute-start(bf16[4,32,576]{2,1,0:T(8,128)(2,1)S(1)} %pad_maximum_fusion.1.refs_0_), channel_id=1, source_target_pairs={{0,96},{32,0},{64,32},{96,64},{1,97},{33,1},{65,33},{97,65},{2,98}... | collective-permute-start | bytes 442376 | tf_op jit(solution)/shard_map/ppermute | solution.py:53
  18.6 1.2 collective-permute-start.16
  20.3 0.7 pad_add_fusion.info_ref
  21.0 0.8 copy.24
  21.8 1.7 %copy-done = bf16[2048,576]{0,1:T(8,128)(2,1)S(1)} copy-done((bf16[2048,576]{0,1:T(8,128)(2,1)S(1)}, bf16[2048,576]{0,1:T(8,128)(2,1)}, u32[]{:S(2)}) %copy-start) | copy-done | bytes 2359320
  23.4 0.7 copy-done.9
  24.1 1.0 entry.1.refs_5_
  25.1 1.5 %collective-permute-start.5 = (bf16[4,32,576]{2,1,0:T(8,128)(2,1)S(1)}, bf16[4,32,576]{2,1,0:T(8,128)(2,1)S(1)}, u32[]{:S(2)}, u32[]{:S(2)}) collective-permute-start(bf16[4,32,576]{2,1,0:T(8,128)(2,1)S(1)} %pad_maximum_fusion.refs_0_), channel_id=1, source_target_pairs={{0,24},{8,0},{16,8},{24,16},{1,25},{9,1},{17,9},{25,17},{2,26},{10... | collective-permute-start | bytes 442376 | tf_op jit(solution)/shard_map/ppermute | solution.py:53
  26.7 2.3 %collective-permute-start.4 = (bf16[4,32,576]{2,1,0:T(8,128)(2,1)S(1)}, bf16[4,32,576]{2,1,0:T(8,128)(2,1)S(1)}, u32[]{:S(2)}, u32[]{:S(2)}) collective-permute-start(bf16[4,32,576]{2,1,0:T(8,128)(2,1)S(1)} %pad_maximum_fusion.refs_0_), channel_id=1, source_target_pairs={{0,16},{8,24},{16,0},{24,8},{1,17},{9,25},{17,1},{25,9},{2,18},{10... | collective-permute-start | bytes 442376 | tf_op jit(solution)/shard_map/ppermute | solution.py:53
  29.0 2.8 %attend.3 = (bf16[144,512]{1,0:T(8,128)(2,1)S(1)}, bf16[144,512]{1,0:T(8,128)(2,1)S(1)}, bf16[144,512]{1,0:T(8,128)(2,1)S(1)}, bf16[144,512]{1,0:T(8,128)(2,1)S(1)}) custom-call(s32[3]{0:T(128)S(1)} %pad_add_fusion.info_ref, bf16[4,32,576]{2,1,0:T(8,128)(2,1)S(1)} %pad_maximum_fusion.1.refs_0_, bf16[4,32,576]{2,1,0:T(8,128)(2,1)S(1)} %collective-permute-done.15.refs_1_, ...), custom_call_target="tpu_custom_call" | custom-call | flops 900000000 | bytes 2500000 | tf_op jit(solution)/shard_map/attend/pallas_call | solution.py:39
  31.9 3.3 %collective-permute-start.18 = (bf16[144,512]{1,0:T(8,128)(2,1)S(1)}, bf16[144,512]{1,0:T(8,128)(2,1)S(1)}, u32[]{:S(2)}, u32[]{:S(2)}) collective-permute-start(bf16[144,512]{1,0:T(8,128)(2,1)S(1)} %get-tuple-element.40), channel_id=1, source_target_pairs={{0,24},{8,0},{16,8},{24,16},{1,25},{9,1},{17,9},{25,17},{2,26},{10... | collective-permute-start | bytes 442376 | tf_op jit(solution)/shard_map/ppermute | solution.py:53
  35.2 0.9 collective-permute-start.20
  36.1 2.8 %attend.2 = (bf16[144,512]{1,0:T(8,128)(2,1)S(1)}, bf16[144,512]{1,0:T(8,128)(2,1)S(1)}, bf16[144,512]{1,0:T(8,128)(2,1)S(1)}, bf16[144,512]{1,0:T(8,128)(2,1)S(1)}) custom-call(s32[3]{0:T(128)S(1)} %pad_add_fusion.info_ref, bf16[4,32,576]{2,1,0:T(8,128)(2,1)S(1)} %pad_maximum_fusion.refs_0_, bf16[4,32,576]{2,1,0:T(8,128)(2,1)S(1)} %collective-permute-done.3.refs_1_, ...), custom_call_target="tpu_custom_call" | custom-call | flops 900000000 | bytes 2500000 | tf_op jit(solution)/shard_map/attend/pallas_call | solution.py:39
  39.0 4.5 %collective-permute-start.6 = (bf16[144,512]{1,0:T(8,128)(2,1)S(1)}, bf16[144,512]{1,0:T(8,128)(2,1)S(1)}, u32[]{:S(2)}, u32[]{:S(2)}) collective-permute-start(bf16[144,512]{1,0:T(8,128)(2,1)S(1)} %get-tuple-element.31), channel_id=1, source_target_pairs={{0,96},{32,0},{64,32},{96,64},{1,97},{33,1},{65,33},{97,65},{2,98}... | collective-permute-start | bytes 442376 | tf_op jit(solution)/shard_map/ppermute | solution.py:53
  43.5 0.8 collective-permute-start.7
  44.6 3.2 %collective-permute-start.21 = (bf16[48,512]{1,0:T(8,128)(2,1)S(1)}, bf16[48,512]{1,0:T(8,128)(2,1)S(1)}, u32[]{:S(2)}, u32[]{:S(2)}) collective-permute-start(bf16[48,512]{1,0:T(8,128)(2,1)S(1)} %get-tuple-element.44), channel_id=1, source_target_pairs={{0,96},{32,0},{64,32},{96,64},{1,97},{33,1},{65,33},{97,65},{2,98}... | collective-permute-start | bytes 147464 | tf_op jit(solution)/shard_map/ppermute | solution.py:53
  47.8 1.5 %collective-permute-start.22 = (bf16[48,512]{1,0:T(8,128)(2,1)S(1)}, bf16[48,512]{1,0:T(8,128)(2,1)S(1)}, u32[]{:S(2)}, u32[]{:S(2)}) collective-permute-start(bf16[48,512]{1,0:T(8,128)(2,1)S(1)} %get-tuple-element.45), channel_id=1, source_target_pairs={{0,64},{32,96},{64,0},{96,32},{1,65},{33,97},{65,1},{97,33},{2,66}... | collective-permute-start | bytes 147464 | tf_op jit(solution)/shard_map/ppermute | solution.py:53
  49.3 0.9 collective-permute-done.7.refs_2_
  50.2 1.5 %collective-permute-done.8.refs_3_ = bf16[144,512]{1,0:T(8,128)(2,1)S(1)} collective-permute-done((bf16[144,512]{1,0:T(8,128)(2,1)S(1)}, bf16[144,512]{1,0:T(8,128)(2,1)S(1)}, u32[]{:S(2)}, u32[]{:S(2)}) %collective-permute-start.8) | collective-permute-done | bytes 147488 | tf_op jit(solution)/shard_map/ppermute | solution.py:53
  51.9 1.4 %collective-permute-start.9 = (bf16[48,512]{1,0:T(8,128)(2,1)S(1)}, bf16[48,512]{1,0:T(8,128)(2,1)S(1)}, u32[]{:S(2)}, u32[]{:S(2)}) collective-permute-start(bf16[48,512]{1,0:T(8,128)(2,1)S(1)} %get-tuple-element.35), channel_id=1, source_target_pairs={{0,24},{8,0},{16,8},{24,16},{1,25},{9,1},{17,9},{25,17},{2,26},{10... | collective-permute-start | bytes 147464 | tf_op jit(solution)/shard_map/ppermute | solution.py:53
  53.3 2.0 %collective-permute-start.10 = (bf16[48,512]{1,0:T(8,128)(2,1)S(1)}, bf16[48,512]{1,0:T(8,128)(2,1)S(1)}, u32[]{:S(2)}, u32[]{:S(2)}) collective-permute-start(bf16[48,512]{1,0:T(8,128)(2,1)S(1)} %get-tuple-element.36), channel_id=1, source_target_pairs={{0,16},{8,24},{16,0},{24,8},{1,17},{9,25},{17,1},{25,9},{2,18},{10... | collective-permute-start | bytes 147464 | tf_op jit(solution)/shard_map/ppermute | solution.py:53
  56.1 2.9 %collective-permute-done.10.refs_2_ = bf16[48,512]{1,0:T(8,128)(2,1)S(1)} collective-permute-done((bf16[48,512]{1,0:T(8,128)(2,1)S(1)}, bf16[48,512]{1,0:T(8,128)(2,1)S(1)}, u32[]{:S(2)}, u32[]{:S(2)}) %collective-permute-start.10) | collective-permute-done | bytes 49184 | tf_op jit(solution)/shard_map/ppermute | solution.py:53
  58.9 1.8 %collective-permute-done.11.refs_3_ = bf16[48,512]{1,0:T(8,128)(2,1)S(1)} collective-permute-done((bf16[48,512]{1,0:T(8,128)(2,1)S(1)}, bf16[48,512]{1,0:T(8,128)(2,1)S(1)}, u32[]{:S(2)}, u32[]{:S(2)}) %collective-permute-start.11) | collective-permute-done | bytes 49184 | tf_op jit(solution)/shard_map/ppermute | solution.py:53
  60.7 1.4 %output.1 = bf16[128,1024]{1,0:T(8,128)(2,1)} custom-call(bf16[48,512]{1,0:T(8,128)(2,1)S(1)} %get-tuple-element.34.refs_0_, bf16[48,512]{1,0:T(8,128)(2,1)S(1)} %collective-permute-done.9.refs_1_, bf16[48,512]{1,0:T(8,128)(2,1)S(1)} %collective-permute-done.10.refs_2_, bf16[48,512]{1,0:T(8,128)(2,1)S(1)} %collective-permute-done.11.refs_3_, ...), custom_call_target="tpu_custom_call" | custom-call | flops 80000000 | bytes 1500000 | tf_op jit(solution)/shard_map/output/pallas_call | solution.py:39
  62.1 3.5 %all-to-all-start = ((bf16[16,8,1024]{2,1,0:T(8,128)(2,1)}), bf16[16,8,1024]{2,1,0:T(8,128)(2,1)S(1)}, u32[]{:S(2)}, u32[]{:S(2)}) async-start(bf16[16,8,1024]{2,1,0:T(8,128)(2,1)} %bitcast.19), calls=%async_computation | async-start | bytes 524288 | tf_op jit(solution)/shard_map/all_to_all | solution.py:485
  65.8 8.3 %all-to-all-done.parts_ref = bf16[16,8,1024]{2,1,0:T(8,128)(2,1)S(1)} async-done(((bf16[16,8,1024]{2,1,0:T(8,128)(2,1)}), bf16[16,8,1024]{2,1,0:T(8,128)(2,1)S(1)}, u32[]{:S(2)}, u32[]{:S(2)}) %all-to-all-start) | async-done | bytes 262176 | tf_op jit(solution)/shard_map/all_to_all | solution.py:485
  74.1 1.1 norm.1
  75.2 21.5 %all_to_all.15 = bf16[64,8,1024]{2,1,0:T(8,128)(2,1)S(1)} all-to-all(bf16[64,8,1024]{2,1,0:T(8,128)(2,1)S(1)} %get-tuple-element.47), channel_id=1, replica_groups=mesh['x'=4,'z'=4,'y'=4,'core'=2] {'y','x','z'}, dimensions={0} | all-to-all | bytes 2097152 | tf_op jit(solution)/shard_map/all_to_all | solution.py:499
  96.7 1.7 %route.1.route_ref = f32[8,1024]{1,0:T(8,128)S(1)} custom-call(s32[5]{0:T(128)S(1)} %stack.53.info_ref, s32[6,4,128]{2,1,0:T(4,128)S(1)} %bitcast.47, f32[6,4,128]{2,1,0:T(4,128)S(1)} %bitcast.48), custom_call_target="tpu_custom_call" | custom-call | flops 60000000 | bytes 60000 | tf_op jit(solution)/shard_map/route/pallas_call | solution.py:39
  98.4 0.9 collective-permute-done.24.other_ref
  99.4 1.8 %copy-done.11 = bf16[2,2048,352]{1,2,0:T(8,128)(2,1)S(1)} copy-done((bf16[2,2048,352]{1,2,0:T(8,128)(2,1)S(1)}, bf16[2,2048,352]{1,2,0:T(8,128)(2,1)}, u32[]{:S(2)}) %copy-start.11) | copy-done | bytes 2883608
  101.2 1.8 %copy-done.12 = bf16[2,352,2048]{2,1,0:T(8,128)(2,1)S(1)} copy-done((bf16[2,352,2048]{2,1,0:T(8,128)(2,1)S(1)}, bf16[2,352,2048]{2,1,0:T(8,128)(2,1)}, u32[]{:S(2)}) %copy-start.12) | copy-done | bytes 2883608
  103.0 1.1 copy-done.16
  104.1 6.4 %moe.1 = (bf16[512,1024]{1,0:T(8,128)(2,1)S(1)}, bf16[512,1024]{1,0:T(8,128)(2,1)S(1)}) custom-call(s32[5]{0:T(128)S(1)} %stack.53.info_ref, bf16[512,1024]{1,0:T(8,128)(2,1)S(1)} %bitcast.32, bf16[512,1024]{1,0:T(8,128)(2,1)S(1)} %collective-permute-done.24.other_ref, f32[8,1024]{1,0:T(8,128)S(1)} %route.1.route_ref, ...), custom_call_target="tpu_custom_call" | custom-call | flops 4000000000 | bytes 15000000 | tf_op jit(solution)/shard_map/moe/pallas_call | solution.py:39
  110.8 2.5 %collective-permute-done.25 = bf16[512,1024]{1,0:T(8,128)(2,1)S(1)} collective-permute-done((bf16[512,1024]{1,0:T(8,128)(2,1)S(1)}, bf16[512,1024]{1,0:T(8,128)(2,1)S(1)}, u32[]{:S(2)}, u32[]{:S(2)}) %collective-permute-start.25) | collective-permute-done | bytes 1048608 | tf_op jit(solution)/shard_map/ppermute | solution.py:521
  113.7 23.3 %all_to_all.16 = bf16[64,8,1024]{2,1,0:T(8,128)(2,1)S(1)} all-to-all(bf16[64,8,1024]{2,1,0:T(8,128)(2,1)S(1)} %fusion), channel_id=1, replica_groups=mesh['x'=4,'z'=4,'y'=4,'core'=2] {'x','z','y'}, dimensions={0} | all-to-all | bytes 2097152 | tf_op jit(solution)/shard_map/all_to_all | solution.py:523
  137.2 0.7 reshape.44
  (70 shorter events, 3.5 us)
Async XLA Ops:
  1.6 1.0 copy-start.1
  2.6 1.1 copy-start.3
  3.7 0.9 copy-start.5
  4.6 0.7 copy-start.7
  5.3 23.7 %copy-start.19 = (s32[2,8,64]{2,1,0:T(8,128)S(1)}, s32[2,8,64]{2,1,0:T(8,128)}, u32[]{:S(2)}) copy-start(s32[2,8,64]{2,1,0:T(8,128)} %refs_7_.3) | copy-start | bytes 12292
  5.9 9.0 %collective-permute-start.14 = (bf16[32,576]{1,0:T(8,128)(2,1)S(1)}, bf16[32,576]{1,0:T(8,128)(2,1)S(1)}, u32[]{:S(2)}, u32[]{:S(2)}) collective-permute-start(bf16[32,576]{1,0:T(8,128)(2,1)S(1)} %get-tuple-element.38), channel_id=1, source_target_pairs={{0,24},{8,0},{16,8},{24,16},{1,25},{9,1},{17,9},{25,17},{2,26},{10... | collective-permute-start | bytes 110600 | tf_op jit(solution)/shard_map/ppermute | solution.py:53
  10.0 5.7 %collective-permute-start.13 = (bf16[32,576]{1,0:T(8,128)(2,1)S(1)}, bf16[32,576]{1,0:T(8,128)(2,1)S(1)}, u32[]{:S(2)}, u32[]{:S(2)}) collective-permute-start(bf16[32,576]{1,0:T(8,128)(2,1)S(1)} %get-tuple-element.38), channel_id=1, source_target_pairs={{0,16},{8,24},{16,0},{24,8},{1,17},{9,25},{17,1},{25,9},{2,18},{10... | collective-permute-start | bytes 110600 | tf_op jit(solution)/shard_map/ppermute | solution.py:53
  10.0 5.7 %collective-permute-start.12 = (bf16[32,576]{1,0:T(8,128)(2,1)S(1)}, bf16[32,576]{1,0:T(8,128)(2,1)S(1)}, u32[]{:S(2)}, u32[]{:S(2)}) collective-permute-start(bf16[32,576]{1,0:T(8,128)(2,1)S(1)} %get-tuple-element.38), channel_id=1, source_target_pairs={{0,8},{8,16},{16,24},{24,0},{1,9},{9,17},{17,25},{25,1},{2,10},{10... | collective-permute-start | bytes 110600 | tf_op jit(solution)/shard_map/ppermute | solution.py:53
  11.3 8.4 %collective-permute-start.2 = (bf16[32,576]{1,0:T(8,128)(2,1)S(1)}, bf16[32,576]{1,0:T(8,128)(2,1)S(1)}, u32[]{:S(2)}, u32[]{:S(2)}) collective-permute-start(bf16[32,576]{1,0:T(8,128)(2,1)S(1)} %get-tuple-element.28), channel_id=1, source_target_pairs={{0,96},{32,0},{64,32},{96,64},{1,97},{33,1},{65,33},{97,65},{2,98}... | collective-permute-start | bytes 110600 | tf_op jit(solution)/shard_map/ppermute | solution.py:53
  14.1 11.0 %collective-permute-start.1 = (bf16[32,576]{1,0:T(8,128)(2,1)S(1)}, bf16[32,576]{1,0:T(8,128)(2,1)S(1)}, u32[]{:S(2)}, u32[]{:S(2)}) collective-permute-start(bf16[32,576]{1,0:T(8,128)(2,1)S(1)} %get-tuple-element.28), channel_id=1, source_target_pairs={{0,64},{32,96},{64,0},{96,32},{1,65},{33,97},{65,1},{97,33},{2,66}... | collective-permute-start | bytes 110600 | tf_op jit(solution)/shard_map/ppermute | solution.py:53
  14.9 10.2 %collective-permute-start = (bf16[32,576]{1,0:T(8,128)(2,1)S(1)}, bf16[32,576]{1,0:T(8,128)(2,1)S(1)}, u32[]{:S(2)}, u32[]{:S(2)}) collective-permute-start(bf16[32,576]{1,0:T(8,128)(2,1)S(1)} %get-tuple-element.28), channel_id=1, source_target_pairs={{0,32},{32,64},{64,96},{96,0},{1,33},{33,65},{65,97},{97,1},{2,34}... | collective-permute-start | bytes 110600 | tf_op jit(solution)/shard_map/ppermute | solution.py:53
  15.8 13.2 %collective-permute-start.17 = (bf16[4,32,576]{2,1,0:T(8,128)(2,1)S(1)}, bf16[4,32,576]{2,1,0:T(8,128)(2,1)S(1)}, u32[]{:S(2)}, u32[]{:S(2)}) collective-permute-start(bf16[4,32,576]{2,1,0:T(8,128)(2,1)S(1)} %pad_maximum_fusion.1.refs_0_), channel_id=1, source_target_pairs={{0,96},{32,0},{64,32},{96,64},{1,97},{33,1},{65,33},{97,65},{2,98}... | collective-permute-start | bytes 442376 | tf_op jit(solution)/shard_map/ppermute | solution.py:53
  18.6 10.4 %collective-permute-start.16 = (bf16[4,32,576]{2,1,0:T(8,128)(2,1)S(1)}, bf16[4,32,576]{2,1,0:T(8,128)(2,1)S(1)}, u32[]{:S(2)}, u32[]{:S(2)}) collective-permute-start(bf16[4,32,576]{2,1,0:T(8,128)(2,1)S(1)} %pad_maximum_fusion.1.refs_0_), channel_id=1, source_target_pairs={{0,64},{32,96},{64,0},{96,32},{1,65},{33,97},{65,1},{97,33},{2,66}... | collective-permute-start | bytes 442376 | tf_op jit(solution)/shard_map/ppermute | solution.py:53
  19.7 9.3 %collective-permute-start.15 = (bf16[4,32,576]{2,1,0:T(8,128)(2,1)S(1)}, bf16[4,32,576]{2,1,0:T(8,128)(2,1)S(1)}, u32[]{:S(2)}, u32[]{:S(2)}) collective-permute-start(bf16[4,32,576]{2,1,0:T(8,128)(2,1)S(1)} %pad_maximum_fusion.1.refs_0_), channel_id=1, source_target_pairs={{0,32},{32,64},{64,96},{96,0},{1,33},{33,65},{65,97},{97,1},{2,34}... | collective-permute-start | bytes 442376 | tf_op jit(solution)/shard_map/ppermute | solution.py:53
  21.8 1.7 %copy-start = (bf16[2048,576]{0,1:T(8,128)(2,1)S(1)}, bf16[2048,576]{0,1:T(8,128)(2,1)}, u32[]{:S(2)}) copy-start(bf16[2048,576]{0,1:T(8,128)(2,1)} %param.26) | copy-start | bytes 7077892
  23.4 0.7 copy-start.9
  24.1 4.9 %copy-start.13 = (bf16[2,6,128,576]{2,3,1,0:T(8,128)(2,1)S(1)}, bf16[2,6,128,576]{2,3,1,0:T(8,128)(2,1)}, u32[]{:S(2)}) copy-start(bf16[2,6,128,576]{2,3,1,0:T(8,128)(2,1)} %param.38) | copy-start | bytes 5308420
  25.1 10.0 %collective-permute-start.5 = (bf16[4,32,576]{2,1,0:T(8,128)(2,1)S(1)}, bf16[4,32,576]{2,1,0:T(8,128)(2,1)S(1)}, u32[]{:S(2)}, u32[]{:S(2)}) collective-permute-start(bf16[4,32,576]{2,1,0:T(8,128)(2,1)S(1)} %pad_maximum_fusion.refs_0_), channel_id=1, source_target_pairs={{0,24},{8,0},{16,8},{24,16},{1,25},{9,1},{17,9},{25,17},{2,26},{10... | collective-permute-start | bytes 442376 | tf_op jit(solution)/shard_map/ppermute | solution.py:53
  26.7 9.4 %collective-permute-start.4 = (bf16[4,32,576]{2,1,0:T(8,128)(2,1)S(1)}, bf16[4,32,576]{2,1,0:T(8,128)(2,1)S(1)}, u32[]{:S(2)}, u32[]{:S(2)}) collective-permute-start(bf16[4,32,576]{2,1,0:T(8,128)(2,1)S(1)} %pad_maximum_fusion.refs_0_), channel_id=1, source_target_pairs={{0,16},{8,24},{16,0},{24,8},{1,17},{9,25},{17,1},{25,9},{2,18},{10... | collective-permute-start | bytes 442376 | tf_op jit(solution)/shard_map/ppermute | solution.py:53
  29.0 7.1 %collective-permute-start.3 = (bf16[4,32,576]{2,1,0:T(8,128)(2,1)S(1)}, bf16[4,32,576]{2,1,0:T(8,128)(2,1)S(1)}, u32[]{:S(2)}, u32[]{:S(2)}) collective-permute-start(bf16[4,32,576]{2,1,0:T(8,128)(2,1)S(1)} %pad_maximum_fusion.refs_0_), channel_id=1, source_target_pairs={{0,8},{8,16},{16,24},{24,0},{1,9},{9,17},{17,25},{25,1},{2,10},{10... | collective-permute-start | bytes 442376 | tf_op jit(solution)/shard_map/ppermute | solution.py:53
  31.9 12.4 %collective-permute-start.18 = (bf16[144,512]{1,0:T(8,128)(2,1)S(1)}, bf16[144,512]{1,0:T(8,128)(2,1)S(1)}, u32[]{:S(2)}, u32[]{:S(2)}) collective-permute-start(bf16[144,512]{1,0:T(8,128)(2,1)S(1)} %get-tuple-element.40), channel_id=1, source_target_pairs={{0,24},{8,0},{16,8},{24,16},{1,25},{9,1},{17,9},{25,17},{2,26},{10... | collective-permute-start | bytes 442376 | tf_op jit(solution)/shard_map/ppermute | solution.py:53
  35.2 9.3 %collective-permute-start.19 = (bf16[144,512]{1,0:T(8,128)(2,1)S(1)}, bf16[144,512]{1,0:T(8,128)(2,1)S(1)}, u32[]{:S(2)}, u32[]{:S(2)}) collective-permute-start(bf16[144,512]{1,0:T(8,128)(2,1)S(1)} %get-tuple-element.41), channel_id=1, source_target_pairs={{0,16},{8,24},{16,0},{24,8},{1,17},{9,25},{17,1},{25,9},{2,18},{10... | collective-permute-start | bytes 442376 | tf_op jit(solution)/shard_map/ppermute | solution.py:53
  35.2 25.5 %copy-start.4 = (bf16[128,2048]{1,0:T(8,128)(2,1)S(1)}, bf16[128,2048]{1,0:T(8,128)(2,1)}, u32[]{:S(2)}) copy-start(bf16[128,2048]{1,0:T(8,128)(2,1)} %refs_9_.1) | copy-start | bytes 1572868
  35.2 25.5 %copy-start.6 = (bf16[1,512,128]{2,1,0:T(8,128)(2,1)S(1)}, bf16[1,512,128]{2,1,0:T(8,128)(2,1)}, u32[]{:S(2)}) copy-start(bf16[1,512,128]{2,1,0:T(8,128)(2,1)} %refs_8_.1) | copy-start | bytes 393220
  35.2 9.3 %collective-permute-start.20 = (bf16[144,512]{1,0:T(8,128)(2,1)S(1)}, bf16[144,512]{1,0:T(8,128)(2,1)S(1)}, u32[]{:S(2)}, u32[]{:S(2)}) collective-permute-start(bf16[144,512]{1,0:T(8,128)(2,1)S(1)} %get-tuple-element.42), channel_id=1, source_target_pairs={{0,8},{8,16},{16,24},{24,0},{1,9},{9,17},{17,25},{25,1},{2,10},{10... | collective-permute-start | bytes 442376 | tf_op jit(solution)/shard_map/ppermute | solution.py:53
  39.0 35.2 %copy-start.2 = (bf16[4,16,2048]{2,1,0:T(8,128)(2,1)S(1)}, bf16[4,16,2048]{2,1,0:T(8,128)(2,1)}, u32[]{:S(2)}) copy-start(bf16[4,16,2048]{2,1,0:T(8,128)(2,1)} %embeds_ref.3) | copy-start | bytes 786436
  39.0 35.1 %copy-start.8 = (f32[2048]{0:T(1024)S(1)}, f32[2048]{0:T(1024)}, u32[]{:S(2)}) copy-start(f32[2048]{0:T(1024)} %param.31) | copy-start | bytes 24580
  39.0 10.3 %collective-permute-start.6 = (bf16[144,512]{1,0:T(8,128)(2,1)S(1)}, bf16[144,512]{1,0:T(8,128)(2,1)S(1)}, u32[]{:S(2)}, u32[]{:S(2)}) collective-permute-start(bf16[144,512]{1,0:T(8,128)(2,1)S(1)} %get-tuple-element.31), channel_id=1, source_target_pairs={{0,96},{32,0},{64,32},{96,64},{1,97},{33,1},{65,33},{97,65},{2,98}... | collective-permute-start | bytes 442376 | tf_op jit(solution)/shard_map/ppermute | solution.py:53
  43.5 6.8 %collective-permute-start.7 = (bf16[144,512]{1,0:T(8,128)(2,1)S(1)}, bf16[144,512]{1,0:T(8,128)(2,1)S(1)}, u32[]{:S(2)}, u32[]{:S(2)}) collective-permute-start(bf16[144,512]{1,0:T(8,128)(2,1)S(1)} %get-tuple-element.32), channel_id=1, source_target_pairs={{0,64},{32,96},{64,0},{96,32},{1,65},{33,97},{65,1},{97,33},{2,66}... | collective-permute-start | bytes 442376 | tf_op jit(solution)/shard_map/ppermute | solution.py:53
  44.3 7.4 %collective-permute-start.8 = (bf16[144,512]{1,0:T(8,128)(2,1)S(1)}, bf16[144,512]{1,0:T(8,128)(2,1)S(1)}, u32[]{:S(2)}, u32[]{:S(2)}) collective-permute-start(bf16[144,512]{1,0:T(8,128)(2,1)S(1)} %get-tuple-element.33), channel_id=1, source_target_pairs={{0,32},{32,64},{64,96},{96,0},{1,33},{33,65},{65,97},{97,1},{2,34}... | collective-permute-start | bytes 442376 | tf_op jit(solution)/shard_map/ppermute | solution.py:53
  44.6 10.7 %collective-permute-start.21 = (bf16[48,512]{1,0:T(8,128)(2,1)S(1)}, bf16[48,512]{1,0:T(8,128)(2,1)S(1)}, u32[]{:S(2)}, u32[]{:S(2)}) collective-permute-start(bf16[48,512]{1,0:T(8,128)(2,1)S(1)} %get-tuple-element.44), channel_id=1, source_target_pairs={{0,96},{32,0},{64,32},{96,64},{1,97},{33,1},{65,33},{97,65},{2,98}... | collective-permute-start | bytes 147464 | tf_op jit(solution)/shard_map/ppermute | solution.py:53
  47.8 7.9 %collective-permute-start.22 = (bf16[48,512]{1,0:T(8,128)(2,1)S(1)}, bf16[48,512]{1,0:T(8,128)(2,1)S(1)}, u32[]{:S(2)}, u32[]{:S(2)}) collective-permute-start(bf16[48,512]{1,0:T(8,128)(2,1)S(1)} %get-tuple-element.45), channel_id=1, source_target_pairs={{0,64},{32,96},{64,0},{96,32},{1,65},{33,97},{65,1},{97,33},{2,66}... | collective-permute-start | bytes 147464 | tf_op jit(solution)/shard_map/ppermute | solution.py:53
  49.3 6.4 %collective-permute-start.23 = (bf16[48,512]{1,0:T(8,128)(2,1)S(1)}, bf16[48,512]{1,0:T(8,128)(2,1)S(1)}, u32[]{:S(2)}, u32[]{:S(2)}) collective-permute-start(bf16[48,512]{1,0:T(8,128)(2,1)S(1)} %get-tuple-element.46), channel_id=1, source_target_pairs={{0,32},{32,64},{64,96},{96,0},{1,33},{33,65},{65,97},{97,1},{2,34}... | collective-permute-start | bytes 147464 | tf_op jit(solution)/shard_map/ppermute | solution.py:53
  51.9 4.2 %collective-permute-start.9 = (bf16[48,512]{1,0:T(8,128)(2,1)S(1)}, bf16[48,512]{1,0:T(8,128)(2,1)S(1)}, u32[]{:S(2)}, u32[]{:S(2)}) collective-permute-start(bf16[48,512]{1,0:T(8,128)(2,1)S(1)} %get-tuple-element.35), channel_id=1, source_target_pairs={{0,24},{8,0},{16,8},{24,16},{1,25},{9,1},{17,9},{25,17},{2,26},{10... | collective-permute-start | bytes 147464 | tf_op jit(solution)/shard_map/ppermute | solution.py:53
  53.3 5.6 %collective-permute-start.10 = (bf16[48,512]{1,0:T(8,128)(2,1)S(1)}, bf16[48,512]{1,0:T(8,128)(2,1)S(1)}, u32[]{:S(2)}, u32[]{:S(2)}) collective-permute-start(bf16[48,512]{1,0:T(8,128)(2,1)S(1)} %get-tuple-element.36), channel_id=1, source_target_pairs={{0,16},{8,24},{16,0},{24,8},{1,17},{9,25},{17,1},{25,9},{2,18},{10... | collective-permute-start | bytes 147464 | tf_op jit(solution)/shard_map/ppermute | solution.py:53
  55.4 5.3 %collective-permute-start.11 = (bf16[48,512]{1,0:T(8,128)(2,1)S(1)}, bf16[48,512]{1,0:T(8,128)(2,1)S(1)}, u32[]{:S(2)}, u32[]{:S(2)}) collective-permute-start(bf16[48,512]{1,0:T(8,128)(2,1)S(1)} %get-tuple-element.37), channel_id=1, source_target_pairs={{0,8},{8,16},{16,24},{24,0},{1,9},{9,17},{17,25},{25,1},{2,10},{10... | collective-permute-start | bytes 147464 | tf_op jit(solution)/shard_map/ppermute | solution.py:53
  60.7 36.0 %copy-start.17 = (s32[4,128,6]{1,0,2:T(4,128)S(1)}, s32[4,128,6]{1,0,2:T(4,128)}, u32[]{:S(2)}) copy-start(s32[4,128,6]{1,0,2:T(4,128)} %param.42) | copy-start | bytes 36868
  60.7 36.0 %copy-start.18 = (f32[4,128,6]{1,0,2:T(4,128)S(1)}, f32[4,128,6]{1,0,2:T(4,128)}, u32[]{:S(2)}) copy-start(f32[4,128,6]{1,0,2:T(4,128)} %param.43) | copy-start | bytes 36868
  60.7 38.6 %copy-start.10 = (bf16[2,2048,352]{1,2,0:T(8,128)(2,1)S(1)}, bf16[2,2048,352]{1,2,0:T(8,128)(2,1)}, u32[]{:S(2)}) copy-start(bf16[2,2048,352]{1,2,0:T(8,128)(2,1)} %param.35) | copy-start | bytes 8650756
  62.1 12.0 %all-to-all-start = ((bf16[16,8,1024]{2,1,0:T(8,128)(2,1)}), bf16[16,8,1024]{2,1,0:T(8,128)(2,1)S(1)}, u32[]{:S(2)}, u32[]{:S(2)}) async-start(bf16[16,8,1024]{2,1,0:T(8,128)(2,1)} %bitcast.19), calls=%async_computation | async-start | bytes 524288 | tf_op jit(solution)/shard_map/all_to_all | solution.py:485
  74.1 25.3 %copy-start.14 = (bf16[2048,176]{0,1:T(8,128)(2,1)S(1)}, bf16[2048,176]{0,1:T(8,128)(2,1)}, u32[]{:S(2)}) copy-start(bf16[2048,176]{0,1:T(8,128)(2,1)} %param.32) | copy-start | bytes 2162692
  74.1 25.3 %copy-start.15 = (bf16[2048,176]{0,1:T(8,128)(2,1)S(1)}, bf16[2048,176]{0,1:T(8,128)(2,1)}, u32[]{:S(2)}) copy-start(bf16[2048,176]{0,1:T(8,128)(2,1)} %param.33) | copy-start | bytes 2162692
  96.7 2.7 %collective-permute-start.24 = (bf16[512,1024]{1,0:T(8,128)(2,1)S(1)}, bf16[512,1024]{1,0:T(8,128)(2,1)S(1)}, u32[]{:S(2)}, u32[]{:S(2)}) collective-permute-start(bf16[512,1024]{1,0:T(8,128)(2,1)S(1)} %bitcast.31), channel_id=1, source_target_pairs={{0,1},{1,0},{2,3},{3,2},{4,5},{5,4},{6,7},{7,6},{8,9},{9,8},{10,11... | collective-permute-start | bytes 3145736 | tf_op jit(solution)/shard_map/ppermute | solution.py:500
  99.4 1.8 %copy-start.11 = (bf16[2,2048,352]{1,2,0:T(8,128)(2,1)S(1)}, bf16[2,2048,352]{1,2,0:T(8,128)(2,1)}, u32[]{:S(2)}) copy-start(bf16[2,2048,352]{1,2,0:T(8,128)(2,1)} %param.36) | copy-start | bytes 8650756
  101.2 1.8 %copy-start.12 = (bf16[2,352,2048]{2,1,0:T(8,128)(2,1)S(1)}, bf16[2,352,2048]{2,1,0:T(8,128)(2,1)}, u32[]{:S(2)}) copy-start(bf16[2,352,2048]{2,1,0:T(8,128)(2,1)} %down_ref.1) | copy-start | bytes 8650756
  103.0 1.1 copy-start.16
  110.5 2.7 %collective-permute-start.25 = (bf16[512,1024]{1,0:T(8,128)(2,1)S(1)}, bf16[512,1024]{1,0:T(8,128)(2,1)S(1)}, u32[]{:S(2)}, u32[]{:S(2)}) collective-permute-start(bf16[512,1024]{1,0:T(8,128)(2,1)S(1)} %get-tuple-element.50), channel_id=1, source_target_pairs={{0,1},{1,0},{2,3},{3,2},{4,5},{5,4},{6,7},{7,6},{8,9},{9,8},{10,11... | collective-permute-start | bytes 3145736 | tf_op jit(solution)/shard_map/ppermute | solution.py:521

commit v3 on v2

v3 whole, which is shorter than its diff:
```python
import functools

import jax
import jax.numpy as jnp
import numpy as np
from jax import lax
from jax.experimental import pallas as pl
from jax.experimental.pallas import tpu as pltpu
from jax.sharding import Mesh, PartitionSpec as P

FFE = 1408
THETA = 50000.0
EPS = 1e-06
NEG = -1e30
CAPACITY = 24
SLOTS = 4 * CAPACITY
OWN_ROWS = 64

BLK = ("x", "z")
BEAM = ("y", "core")
OUT_ORDER = BLK + BEAM
CORES = [(0, 1), (1, 0)]
SCALARS = (pltpu.SMEM,)

f32, bf16 = jnp.float32, jnp.bfloat16
LAST = (((1,), (1,)), ((), ()))


def lanes(shape):
    return lax.broadcasted_iota(jnp.int32, shape, len(shape) - 1)


def sublanes(shape):
    return lax.broadcasted_iota(jnp.int32, shape, len(shape) - 2)


def kernel_call(body, name, outs, scratch, cost, first, *args):
    vmem = pl.BlockSpec(memory_space=pltpu.VMEM)
    first = [pl.BlockSpec(memory_space=space) for space in first]
    return pl.pallas_call(
        body,
        out_shape=[jax.ShapeDtypeStruct(shape, dtype) for shape, dtype in outs],
        in_specs=first + [vmem] * (len(args) - len(first)),
        out_specs=[vmem] * len(outs),
        scratch_shapes=scratch,
        compiler_params=pltpu.CompilerParams(vmem_limit_bytes=24 << 20),
        cost_estimate=pl.CostEstimate(flops=cost[0], bytes_accessed=cost[1], transcendentals=cost[2]),
        name=name,
    )(*args)


def fetch(sources, targets, sems):
    copies = [pltpu.make_async_copy(a, b, sems.at[k]) for k, (a, b) in enumerate(zip(sources, targets))]
    for copy in copies:
        copy.start()
    return copies


def in_hbm(*arrays):
    return [pltpu.with_memory_space_constraint(a, pltpu.HBM) for a in arrays]


def room_for(arrays):
    return [pltpu.VMEM(a.shape, a.dtype) for a in arrays] + [pltpu.SemaphoreType.DMA((len(arrays),))]


def shifted(value, axis, by):
    size = lax.axis_size(axis)
    return lax.ppermute(value, axis, [(i, (i + by) % size) for i in range(size)])


def gather(value, axis):
    arrived = {s: shifted(value, axis, s) for s in (1, 3, 2)}
    return [value] + [arrived[s] for s in range(1, 4)]


def rope_parts(cos_ref, rows):
    cosine, sine = cos_ref[:, :64], cos_ref[:, 64:]
    wide = lambda v: jnp.concatenate([jnp.broadcast_to(v[k : k + 1], (8, 64)) for k in range(rows // 8)], axis=0)
    return wide(cosine), wide(sine)


def turned(values, precision=None):
    i, j = sublanes((64, 64)), lanes((64, 64))
    turn = jnp.where(i == j - 32, 1.0, 0.0) - jnp.where(i == j + 32, 1.0, 0.0)
    return jnp.dot(values, turn.astype(values.dtype), precision=precision, preferred_element_type=f32)


def query_kernel(
    embeds_hbm, query_hbm, key_up_hbm, gain_hbm, frequency_hbm, counts_hbm,
    first_ref, second_ref, normed_ref, cos_ref,
    embeds_ref, query_ref, key_up_ref, gain_ref, frequency_ref, counts_ref, sems,
):
    steps, _, width = embeds_ref.shape
    copies = fetch(
        (embeds_hbm, query_hbm, key_up_hbm, gain_hbm, frequency_hbm, counts_hbm),
        (embeds_ref, query_ref, key_up_ref, gain_ref, frequency_ref, counts_ref),
        sems,
    )
    copies[4].wait()
    copies[5].wait()
    line = sublanes((8, 128))
    position = jnp.where(line < steps, counts_ref[0], counts_ref[1]) * 128 + (line & (steps - 1))
    angles = position.astype(f32) * frequency_ref[...]
    cos_ref[...] = jnp.where(lanes((8, 128)) < 64, jnp.cos(angles), jnp.sin(angles))
    copies[0].wait()
    copies[3].wait()
    tokens = [embeds_ref[t].astype(f32) for t in range(steps)]
    tokens = jnp.concatenate([tokens[t][8 * g : 8 * g + 8] for g in range(2) for t in range(steps)], axis=0)
    mean_sq = jnp.sum(tokens * tokens, axis=1, keepdims=True) * (1.0 / width)
    normed = (tokens * lax.rsqrt(mean_sq + EPS) * gain_ref[...]).astype(bf16)
    normed_ref[...] = normed
    copies[1].wait()
    queries = lax.dot_general(normed, query_ref[...], LAST, preferred_element_type=f32).astype(bf16)
    copies[2].wait()
    latent = jnp.dot(queries[:, :128], key_up_ref[0], preferred_element_type=f32).astype(bf16)
    rope = queries[:, 128:]
    cosine, sine = rope_parts(cos_ref, 64)
    rope = (rope.astype(f32) * cosine + turned(rope) * sine).astype(bf16)
    for g, ref in enumerate((first_ref, second_ref)):
        ref[:, :512] = latent[32 * g : 32 * g + 32]
        ref[:, 512:] = rope[32 * g : 32 * g + 32]


def entry_kernel(normed_ref, latent_ref, gain_ref, cos_ref, out_ref):
    projected = lax.dot_general(normed_ref[...], latent_ref[...], LAST, preferred_element_type=f32)
    latent, rope = projected[:, :512], projected[:, 512:]
    mean_sq = jnp.sum(latent * latent, axis=1, keepdims=True) * (1.0 / 512)
    out_ref[:, :512] = (latent * lax.rsqrt(mean_sq + EPS) * gain_ref[...]).astype(bf16)
    cosine, sine = rope_parts(cos_ref, 64)
    out_ref[:, 512:] = (rope * cosine + turned(rope, lax.Precision.HIGHEST) * sine).astype(bf16)


def split_terms(line):
    first = line.astype(bf16).astype(f32)
    second = (line - first).astype(bf16).astype(f32)
    third = line - first - second
    place = sublanes((8, line.shape[1]))
    tile = jnp.where(place == 0, first, 0.0)
    tile = jnp.where(place == 1, second, tile)
    return jnp.where(place == 2, third, tile).astype(bf16)


def joined_terms(tile):
    tile = tile.astype(f32)
    return tile[0:1] + tile[1:2] + tile[2:3]


def as_line(column, offset=0):
    shape = (column.shape[0], 128)
    return jnp.sum(jnp.where(lanes(shape) == sublanes(shape) + offset, column, 0.0), axis=0, keepdims=True)


def as_column(line, count, offset=0):
    shape = (count, 128)
    return jnp.sum(jnp.where(lanes(shape) == sublanes(shape) + offset, line, 0.0), axis=1, keepdims=True)


def attend_kernel(info_ref, *refs):
    q_refs = (refs[:4], refs[4:8])
    cache_ref, entry_ref, parent_ref, table_ref, out_ref, sum_ref = refs[8:]
    near, rows, width = q_refs[0][0].shape
    heads = 4 * near
    groups, beams, _ = table_ref.shape
    pool, _, block_len = cache_ref.shape[1:]
    latent = out_ref.shape[2]
    steps = rows // beams
    scale = (width - latent + 128) ** (-0.5)
    blk = info_ref[0]
    for g in range(groups):
        shape = (beams, 128)
        origin = (lanes(shape) == sublanes(shape)).astype(f32)
        kept = []
        for t in range(steps):
            diagonal = lanes((beams, beams)) == sublanes((beams, beams))
            parent = jnp.where(diagonal, parent_ref[t, g : g + 1, :].astype(f32), 0.0)
            parent = jnp.sum(parent, axis=1, keepdims=True).astype(jnp.int32)
            choose = (lanes((beams, beams)) == parent).astype(f32)
            origin = jnp.dot(choose, origin, preferred_element_type=f32)
            origin = origin + (lanes(shape) == sublanes(shape) + beams * (1 + t)).astype(f32)
            kept.append(origin)
        origin = jnp.concatenate(kept, axis=0)
        table = table_ref[g]
        live = lanes(table.shape) < info_ref[1 + g]
        used = jnp.zeros((beams, 128), f32)
        for p in range(pool):
            hit = jnp.where((table == blk * pool + p) & live, 1.0, 0.0)
            hit = jnp.max(hit, axis=1, keepdims=True)
            used = used + jnp.where(lanes(used.shape) == p, hit, 0.0)
        used = jnp.dot(origin[:, :beams], used, preferred_element_type=f32)
        bias = jnp.concatenate(
            [jnp.broadcast_to(used[:, p : p + 1], (rows, block_len)) for p in range(pool)], axis=1
        )
        bias = jnp.where(bias > 0.5, 0.0, NEG)
        seen = origin[:, beams : beams + rows]
        recent_bias = jnp.where((seen > 0.5) & (blk == 0), 0.0, NEG)

        part = slice(g * rows, (g + 1) * rows)
        q = jnp.concatenate([ref[...] for ref in q_refs[g]], axis=0).reshape(heads * rows, width)
        keys = jnp.concatenate([cache_ref[g, p] for p in range(pool)], axis=1)
        entry = entry_ref[part]
        scores = jnp.dot(q, keys, preferred_element_type=f32)
        scores = scores.reshape(heads, rows, pool * block_len) * scale + bias[None]
        recent = lax.dot_general(q, entry, LAST, preferred_element_type=f32)
        recent = recent.reshape(heads, rows, rows) * scale + recent_bias[None]
        top = jnp.maximum(
            jnp.max(scores, axis=-1, keepdims=True), jnp.max(recent, axis=-1, keepdims=True)
        )
        weights = jnp.exp(scores - top)
        recent = jnp.exp(recent - top)
        total = jnp.sum(weights, axis=-1, keepdims=True) + jnp.sum(recent, axis=-1, keepdims=True)
        weights = weights.astype(bf16).reshape(heads * rows, pool * block_len)
        recent = recent.astype(bf16).reshape(heads * rows, rows)
        lat = lax.dot_general(weights, keys[:latent], LAST, preferred_element_type=f32)
        lat = lat + jnp.dot(recent, entry[:, :latent], preferred_element_type=f32)
        lat = (lat.reshape(heads, rows, latent) / total).astype(bf16)
        lse = jnp.where(top > 0.1 * NEG, top + jnp.log(total), NEG)
        lse = jnp.broadcast_to(lse, (heads, rows, 128))
        for f in range(4):
            for s in range(near):
                dx, dz = (s, f) if g == 0 else (f, s)
                home = (((blk >> 2) - dx) & 3) * 4 + ((blk - dz) & 3)
                out_ref[home, part, :] = lat[f * near + s]
                sum_ref[home, part, :] = lse[f * near + s]
    for h in range(heads):
        tile = split_terms(as_line(sum_ref[h]))
        out_ref[h, groups * rows :, :128] = tile
        out_ref[h, groups * rows :, 128:] = jnp.zeros((8, latent - 128), bf16)


def output_kernel(parts_ref, value_ref, out_ref, result_ref):
    count, rows = parts_ref.shape[0], 64
    sums = [joined_terms(parts_ref[k, rows:, :128]) for k in range(count)]
    best = functools.reduce(jnp.maximum, sums)
    shares = [jnp.exp(v - best) for v in sums]
    whole = functools.reduce(jnp.add, shares)
    joined = sum(as_column(p / whole, rows) * parts_ref[k, :rows, :].astype(f32) for k, p in enumerate(shares))
    head_out = jnp.dot(joined.astype(bf16), value_ref[0], preferred_element_type=f32).astype(bf16)
    line, row = sublanes((128, rows)), lanes((128, rows))
    source = 32 * (line >> 6) + 8 * ((line >> 1) & 3) + ((line >> 3) & 7)
    result = None
    for q in range(2):
        take = jnp.where((source == row) & ((line & 1) == q), 1.0, 0.0).astype(bf16)
        picked_rows = jnp.dot(take, head_out, preferred_element_type=f32).astype(bf16)
        term = jnp.dot(picked_rows, out_ref[:, q * 1024 : (q + 1) * 1024], preferred_element_type=f32)
        result = term if result is None else result + term
    result_ref[...] = result.astype(bf16)


def norm_kernel(info_ref, parts_ref, embeds_ref, gain_ref, spread_ref, resid_ref):
    blk = info_ref[1]
    steps, rows, width = embeds_ref.shape
    half = width // 2
    line = sublanes((2 * steps, half))
    resid = jnp.sum(parts_ref[...].astype(f32), axis=0)
    gain = jnp.zeros((2 * steps, half), f32)
    for q in range(2):
        columns = slice(q * half, (q + 1) * half)
        gain = gain + jnp.where((line & 1) == q, gain_ref[:, columns], 0.0)
        for t in range(steps):
            token = jnp.where(sublanes((rows, half)) == blk, embeds_ref[t, :, columns].astype(f32), 0.0)
            token = jnp.sum(token, axis=0, keepdims=True)
            resid = resid + jnp.where(line == 2 * t + q, token, 0.0)
    resid_ref[...] = resid
    sums = jnp.broadcast_to(jnp.sum(resid * resid, axis=1, keepdims=True), (2 * steps, 128))
    pair = jnp.where((sublanes((8, 8)) >> 1) == (lanes((8, 8)) >> 1), 1.0, 0.0)
    sums = jnp.dot(pair, sums, precision=lax.Precision.HIGHEST, preferred_element_type=f32)
    normed = (resid * lax.rsqrt(sums[:, :1] * (1.0 / width) + EPS) * gain).astype(bf16)
    spread_ref[...] = jnp.broadcast_to(normed[None], spread_ref.shape)


def line_row(line, core):
    chip = (line >> 3) & 63
    return 32 * (chip >> 4) + 16 * ((line >> 9) ^ core) + (chip & 15)


def route_kernel(info_ref, ids_ref, weights_ref, out_ref):
    core = info_ref[0]
    top, steps, rows = ids_ref.shape
    line = lanes((rows, out_ref.shape[1]))
    row = line_row(line, core)
    earlier = jnp.where(sublanes((rows, rows)) < lanes((rows, rows)), 1.0, 0.0).astype(bf16)
    slots, weights = [], []
    for e in range(2):
        expert = info_ref[3 + e]
        weight = jnp.zeros((steps, rows), f32)
        routed = jnp.zeros((steps, rows), f32)
        for k in range(top):
            match = ids_ref[k] == expert
            weight = weight + jnp.where(match, weights_ref[k], 0.0)
            routed = routed + jnp.where(match, 1.0, 0.0)
        wide = jnp.concatenate([routed, jnp.zeros((8 - steps, rows), f32)], axis=0).astype(bf16)
        rank = jnp.dot(wide, earlier, preferred_element_type=f32)[:steps]
        first = (sublanes((steps, rows)) * CAPACITY + 1).astype(f32)
        slots.append(jnp.where(routed > 0.5, rank + first, 0.0))
        weights.append(weight)
    total = jnp.zeros(out_ref.shape, f32)
    for t in range(steps):
        place = sublanes((8, rows))
        values = jnp.zeros((8, rows), f32)
        for k, value in enumerate(slots + weights):
            values = jnp.where(place == k, value[t : t + 1], values)
        take = jnp.where((sublanes(line.shape) == row) & (((line >> 1) & 3) == t), 1.0, 0.0)
        total = total + jnp.dot(values, take, precision=lax.Precision.HIGHEST, preferred_element_type=f32)
    out_ref[...] = total


def line_places(line, core, lines):
    row = line_row(line, core)
    return ((row & 1) ^ core) * (lines // 2) + (row >> 1) * 4 + ((line >> 1) & 3)


def picked(source_ref, hit, line, place, weights):
    halves = []
    for q in range(2):
        pick = jnp.where((line & 1) == q, hit, 0.0).astype(bf16)
        halves.append(jnp.dot(pick, source_ref[...], preferred_element_type=f32))
    first = jnp.where((line & 1) == 0, 1.0, 0.0)
    scale = [
        jnp.sum(hit[e * SLOTS : (e + 1) * SLOTS] * (first * weights[e]), axis=1, keepdims=True)
        for e in range(len(weights))
    ]
    parts = jnp.where(sublanes((8, line.shape[1])) == 0, (place + 1) >> 4, (place + 1) & 15).astype(f32)
    spot = lax.dot_general((parts * first).astype(bf16), hit.astype(bf16), LAST, preferred_element_type=f32)
    return halves, jnp.concatenate(scale, axis=0), spot


def pick_kernel(info_ref, mine_ref, route_ref, x_ref, scale_ref, spot_ref):
    core, y = info_ref[0], info_ref[2]
    lines, half = mine_ref.shape
    line = lanes((1, lines))
    hits = [sublanes((SLOTS, lines)) + 1 == route_ref[e : e + 1, :lines].astype(jnp.int32) for e in range(2)]
    hits.append(sublanes((OWN_ROWS, lines)) == (line >> 1) - y * OWN_ROWS)
    hit = jnp.concatenate([jnp.where(h, 1.0, 0.0) for h in hits], axis=0)
    place = line_places(line, core, lines)
    halves, scale, spot = picked(mine_ref, hit, line, place, [route_ref[2 + e : 3 + e, :lines] for e in range(2)])
    for q in range(2):
        x_ref[:, q * half : (q + 1) * half] = halves[q].astype(bf16)
    scale_ref[...] = jnp.broadcast_to(scale, scale_ref.shape)
    spot_ref[...] = spot


def put(ref, y_ref, spot, side):
    lines, half = ref.shape
    line = sublanes((lines, 1))
    found = jnp.where((line >> 1) + side * (lines // 2) == spot, 1.0, 0.0)
    result = None
    for q in range(2):
        found_q = jnp.where((line & 1) == q, found, 0.0).astype(bf16)
        term = jnp.dot(found_q, y_ref[:, q * half : (q + 1) * half], preferred_element_type=f32)
        result = term if result is None else result + term
    ref[...] = result.astype(bf16)


def expert_kernel(
    info_ref, shared_down_hbm, mine_x_ref, mine_scale_ref, mine_spot_ref, other_ref, route_ref, resid_ref,
    gate_ref, up_ref, down_ref, shared_gate_ref, shared_up_ref,
    other_out_ref, y_ref, spot_ref,
    x_ref, shared_down_ref, sems,
):
    core, blk = info_ref[0], info_ref[1]
    lines, half = other_ref.shape
    (copy,) = fetch((shared_down_hbm,), (shared_down_ref,), sems)
    line = lanes((1, lines)) + lines
    hits = [sublanes((SLOTS, lines)) + 1 == route_ref[e : e + 1, lines:].astype(jnp.int32) for e in range(2)]
    hit = jnp.concatenate([jnp.where(h, 1.0, 0.0) for h in hits], axis=0)
    place = line_places(line, core, lines)
    halves, scale, spot = picked(other_ref, hit, line, place, [route_ref[2 + e : 3 + e, lines:] for e in range(2)])
    routed = 2 * SLOTS
    for q in range(2):
        columns = slice(q * half, (q + 1) * half)
        x_ref[:, columns] = (mine_x_ref[:routed, columns].astype(f32) + halves[q]).astype(bf16)
    scale = scale + mine_scale_ref[:, :1]
    spot = jnp.concatenate([spot, jnp.zeros((8, OWN_ROWS), f32)], axis=1) + mine_spot_ref[...]
    spot = (spot[0:1] * 16.0 + spot[1:2] - 1.0).astype(jnp.int32)
    spot_ref[...] = jnp.broadcast_to(spot, spot_ref.shape)

    def gated(x, gate, up):
        gate_val = lax.dot_general(x, gate, LAST, preferred_element_type=f32)
        up_val = lax.dot_general(x, up, LAST, preferred_element_type=f32)
        return (gate_val / (1.0 + jnp.exp(-gate_val)) * up_val).astype(bf16)

    for e in range(2):
        part = slice(e * SLOTS, (e + 1) * SLOTS)
        act = gated(x_ref[part, :], gate_ref[e], up_ref[e])
        down = jnp.dot(act, down_ref[e], preferred_element_type=f32)
        y_ref[part, :] = (down * scale[part]).astype(bf16)
    act = gated(mine_x_ref[routed:, :], shared_gate_ref[...], shared_up_ref[...])
    copy.wait()
    own = jnp.dot(act, shared_down_ref[...], preferred_element_type=f32)
    for t in range(4):
        whole = jnp.concatenate([resid_ref[2 * t + q : 2 * t + q + 1, :] for q in range(2)], axis=1)
        own = own + jnp.where(sublanes((OWN_ROWS, 1)) == blk * 4 + t, whole, 0.0)
    y_ref[routed:, :] = own.astype(bf16)
    put(other_out_ref, y_ref, spot, 1)


def put_kernel(y_ref, spot_ref, out_ref):
    put(out_ref, y_ref, spot_ref[0:1], 0)


def per_device(
    embeds,
    attn_gain,
    w_query,
    w_latent,
    latent_gain,
    w_key_up,
    w_value_up,
    w_out,
    ffn_gain,
    w_shared_gate,
    w_shared_up,
    w_shared_down,
    w_expert_gate,
    w_expert_up,
    w_expert_down,
    cache_pool,
    block_tables,
    block_counts,
    parents,
    expert_ids,
    expert_weights,
):
    steps, row_dev, width = embeds.shape
    groups, beams, _ = block_tables.shape
    latent = w_key_up.shape[2]
    block_len, entry_width = cache_pool.shape[2:]
    rope = entry_width - latent
    pair_dev, _, unit_dev = w_expert_gate.shape
    half = width // 2
    chips = expert_ids.shape[1] // 2
    lines = chips * 2 * steps
    y, core = lax.axis_index("y"), lax.axis_index("core")
    blk, beam = lax.axis_index(BLK), lax.axis_index(BEAM)
    expert = blk * pair_dev * 2 + beam * unit_dev // FFE
    place = jnp.stack([core, blk, y, expert, expert + 2]).astype(jnp.int32)
    counts = jnp.concatenate([blk[None], block_counts]).astype(jnp.int32)

    frequency = np.float64(THETA) ** (-np.arange(rope // 2) * 2.0 / rope)
    frequency = np.tile(frequency.astype(np.float32), 4).reshape(1, 128)
    rows_all = groups * steps * beams
    blk_size = lax.axis_size("x") * lax.axis_size("z")
    sources = (embeds, w_query.T, w_key_up, attn_gain.reshape(1, width), jnp.asarray(frequency), block_counts)
    query = ((steps * beams, entry_width), bf16)
    first, second, normed, cosines = kernel_call(
        query_kernel,
        "query",
        [query, query, ((rows_all, width), bf16), ((8, 128), f32)],
        [pltpu.VMEM(a.shape, a.dtype) for a in sources[:-1]]
        + [pltpu.SMEM(block_counts.shape, jnp.int32), pltpu.SemaphoreType.DMA((len(sources),))],
        (60_000_000, 20_000_000, 0),
        (pltpu.HBM,) * len(sources),
        *in_hbm(*sources),
    )
    first, second = jnp.stack(gather(first, "x")), jnp.stack(gather(second, "z"))
    queries = gather(first, "z") + gather(second, "x")
    (entries,) = kernel_call(
        entry_kernel,
        "entry",
        [((rows_all, entry_width), bf16)],
        [],
        (150_000_000, 40_000_000, 0),
        (),
        normed,
        w_latent.T,
        latent_gain.reshape(1, latent),
        cosines,
    )
    cache = cache_pool.transpose(0, 1, 3, 2)
    (parts,) = kernel_call(
        attend_kernel,
        "attend",
        [((blk_size, rows_all + 8, latent), bf16)],
        [pltpu.VMEM((blk_size, rows_all, 128), f32)],
        (1_800_000_000, 5_000_000, 800_000),
        SCALARS,
        counts,
        *queries,
        cache,
        entries,
        parents,
        block_tables,
    )
    expert_ids, parts = lax.optimization_barrier((expert_ids, parts))
    parts = lax.all_to_all(parts, BLK, 0, 0)
    (route,) = kernel_call(
        route_kernel,
        "route",
        [((8, 2 * lines), f32)],
        [],
        (60_000_000, 60_000, 0),
        SCALARS,
        place,
        expert_ids.transpose(2, 0, 1),
        expert_weights.transpose(2, 0, 1),
    )
    parts, route = lax.optimization_barrier((parts, route))
    (attn_part,) = kernel_call(
        output_kernel,
        "output",
        [((row_dev * 2 * steps, half), bf16)],
        [],
        (80_000_000, 90_000_000, 1_000),
        (),
        parts,
        w_value_up,
        w_out,
    )
    attn_part = lax.all_to_all(attn_part.reshape(row_dev, 2 * steps, half), BLK, 0, 0)
    spread, resid = kernel_call(
        norm_kernel,
        "norm",
        [((chips, 2 * steps, half), bf16), ((2 * steps, half), f32)],
        [],
        (1_000_000, 90_000_000, 0),
        SCALARS,
        place,
        attn_part,
        embeds,
        ffn_gain.reshape(1, width),
    )

    mine = lax.all_to_all(spread, ("y", "x", "z"), 0, 0).reshape(lines, half)
    other = lax.ppermute(mine, "core", CORES)
    routed = pair_dev * SLOTS
    total = routed + OWN_ROWS
    slots = [((total, width), bf16), ((routed, 128), f32), ((8, total), f32)]
    x_mine, scale, spot = kernel_call(
        pick_kernel,
        "pick",
        slots,
        [],
        (1_000_000_000, 20_000_000, 0),
        SCALARS,
        place,
        mine,
        route,
    )
    other_out, outs, spot = kernel_call(
        expert_kernel,
        "experts",
        [((lines, half), bf16), ((total, width), bf16), ((8, total), jnp.int32)],
        [pltpu.VMEM((routed, width), bf16)] + room_for((w_shared_down,)),
        (3_000_000_000, 15_000_000, 300_000),
        SCALARS + (pltpu.HBM,),
        place,
        *in_hbm(w_shared_down),
        x_mine,
        scale,
        spot,
        other,
        route,
        resid,
        w_expert_gate.transpose(0, 2, 1),
        w_expert_up.transpose(0, 2, 1),
        w_expert_down,
        w_shared_gate.T,
        w_shared_up.T,
    )
    arrived = lax.ppermute(other_out, "core", CORES)
    (own_out,) = kernel_call(
        put_kernel, "put", [((lines, half), bf16)], [], (500_000_000, 2_000_000, 0), (), outs, spot
    )
    own_out = own_out.astype(f32) + arrived.astype(f32)
    own_out = own_out.astype(bf16).reshape(chips, 2 * steps, half)
    result = jnp.sum(lax.all_to_all(own_out, ("x", "z", "y"), 0, 0).astype(f32), axis=0)
    return result.reshape(steps, 1, width)


def solution(mesh):
    devices = mesh.devices.reshape(4, 4, 4, 2)
    split = Mesh(devices, ("x", "z", "y", "core"))
    placed = (
        P(None, BEAM, None),
        P(),
        P(None, BLK),
        P(),
        P(),
        P(BLK, None, None),
        P(BLK, None, None),
        P(BLK, None),
        P(),
        P(None, BLK),
        P(None, BLK),
        P(BLK, None),
        P(BLK, None, BEAM),
        P(BLK, None, BEAM),
        P(BLK, BEAM, None),
        P(BEAM, BLK, None, None),
        P(BEAM, None, None),
        P(BEAM),
        P(None, BEAM, None),
        P(),
        P(),
    )
    return jax.shard_map(
        per_device,
        mesh=split,
        in_specs=placed,
        out_specs=P(None, OUT_ORDER, None),
        check_vma=False,
    )
```

time: 139 us -> 125 us (0.90)
  starting transfers between devices: 40.1 us -> 26.3 us
  blocking collectives: 44.9 us -> 57.1 us
  local copies, waits for them, and re-layouts: 12.4 us -> 5.19 us
  waiting for transfers between devices: 19.2 us -> 15.5 us
  other arithmetic: 2.89 us -> 0.72 us
  Pallas kernels: 18.2 us -> 19.7 us
    ppermute x24 -> x12, starting transfers between devices: 36.3 us -> 20.1 us  [shifted(): lax.ppermute(value, axis, [(i, (i + by) % size) for i in range(size)])]
    all_to_all x0 -> x1, blocking collectives: none -> 12 us  [per_device(): lax.all_to_all(attn_part.reshape(row_dev, 2 * steps, half), BLK, 0, 0)]
    unnamed x41 -> x38, local copies, waits for them, and re-layouts: 11.6 us -> 4.44 us
    ppermute x24 -> x12, waiting for transfers between devices: 7.43 us -> 1.54 us  [shifted(): lax.ppermute(value, axis, [(i, (i + by) % size) for i in range(size)])]
    all_to_all x1, waiting for transfers between devices: 8.32 us -> 10.8 us  [per_device(): parts = lax.all_to_all(parts, BLK, 0, 0)]
    all_to_all x1, starting transfers between devices: 3.53 us -> 5.91 us  [per_device(): parts = lax.all_to_all(parts, BLK, 0, 0)]
    pallas_call x10 -> x9, Pallas kernels: 18.2 us -> 19.7 us  [kernel_call(): pl.pallas_call(body, out_shape=[jax.ShapeDtypeStruct(shape, dtype) for sh...]
  transfers between devices with their start and end apart: 27 -> 15, of which waited for: 8 -> 4; matrix products, arithmetic and copies ran while one was open for 1% -> 0% of each run, Pallas kernels for 6% -> 4%
where the time goes in v3:
time: 125 us
  blocking collectives  57.1 us (46%)
  starting transfers between devices  26.3 us (21%)
  Pallas kernels  19.7 us (16%)
  waiting for transfers between devices  15.5 us (12%)
  local copies, waits for them, and re-layouts  5.19 us (4%)
    all_to_all x1, blocking collectives, per_device(): lax.all_to_all(own_out, ('x', 'z', 'y'), 0, 0).astype(f32)  23.3 us
    all_to_all x1, blocking collectives, per_device(): mine = lax.all_to_all(spread, ('y', 'x', 'z'), 0, 0).reshape(lines, half)  21.8 us
    ppermute x12, starting transfers between devices, shifted(): lax.ppermute(value, axis, [(i, (i + by) % size) for i in range(size)])  20.1 us
    pallas_call x9, Pallas kernels, kernel_call(): pl.pallas_call(body, out_shape=[jax.ShapeDtypeStruct(shape, dtype) for sh...  19.7 us
    all_to_all x1, blocking collectives, per_device(): lax.all_to_all(attn_part.reshape(row_dev, 2 * steps, half), BLK, 0, 0)  12 us
    all_to_all x1, waiting for transfers between devices, per_device(): parts = lax.all_to_all(parts, BLK, 0, 0)  10.8 us
    all_to_all x1, starting transfers between devices, per_device(): parts = lax.all_to_all(parts, BLK, 0, 0)  5.91 us
    unnamed x38, local copies, waits for them, and re-layouts  4.44 us
  transfers between devices with their start and end apart: 15, of which 4 were waited for; matrix products, arithmetic and copies ran while one was open for 0% of the time, Pallas kernels for 4%

profile of v3, /device:TPU:0, one launch (start us, length us, event | category | flops | bytes accessed | tf_op | source)
XLA Modules:
  0.0 124.7 jit_solution(1810604947968064521)
XLA Ops:
  0.0 2.0 %query.1 = (bf16[32,576]{1,0:T(8,128)(2,1)S(1)}, bf16[32,576]{1,0:T(8,128)(2,1)S(1)}, bf16[64,2048]{1,0:T(8,128)(2,1)S(1)}, f32[8,128]{1,0:T(8,128)S(1)}) custom-call(bf16[4,16,2048]{2,1,0:T(8,128)(2,1)} %embeds_ref.1, bf16[192,2048]{1,0:T(8,128)(2,1)} %bitcast.44, bf16[1,128,512]{2,1,0:T(8,128)(2,1)} %key_up_hbm.1, f32[1,2048]{1,0:T(1,128)} %bitcast.51, ...), custom_call_target="tpu_custom_call" | custom-call | flops 60000000 | bytes 20000000 | tf_op jit(solution)/shard_map/query/pallas_call | solution.py:40
  2.0 4.2 %collective-permute-start.8 = (bf16[32,576]{1,0:T(8,128)(2,1)S(1)}, bf16[32,576]{1,0:T(8,128)(2,1)S(1)}, u32[]{:S(2)}, u32[]{:S(2)}) collective-permute-start(bf16[32,576]{1,0:T(8,128)(2,1)S(1)} %get-tuple-element.22), channel_id=1, source_target_pairs={{0,24},{8,0},{16,8},{24,16},{1,25},{9,1},{17,9},{25,17},{2,26},{10... | collective-permute-start | bytes 110600 | tf_op jit(solution)/shard_map/ppermute | solution.py:69
  6.2 0.0 collective-permute-start.7
  6.2 1.3 %collective-permute-start.6 = (bf16[32,576]{1,0:T(8,128)(2,1)S(1)}, bf16[32,576]{1,0:T(8,128)(2,1)S(1)}, u32[]{:S(2)}, u32[]{:S(2)}) collective-permute-start(bf16[32,576]{1,0:T(8,128)(2,1)S(1)} %get-tuple-element.22), channel_id=1, source_target_pairs={{0,8},{8,16},{16,24},{24,0},{1,9},{9,17},{17,25},{25,1},{2,10},{10... | collective-permute-start | bytes 110600 | tf_op jit(solution)/shard_map/ppermute | solution.py:69
  7.5 2.8 %collective-permute-start.2 = (bf16[32,576]{1,0:T(8,128)(2,1)S(1)}, bf16[32,576]{1,0:T(8,128)(2,1)S(1)}, u32[]{:S(2)}, u32[]{:S(2)}) collective-permute-start(bf16[32,576]{1,0:T(8,128)(2,1)S(1)} %get-tuple-element.21), channel_id=1, source_target_pairs={{0,96},{32,0},{64,32},{96,64},{1,97},{33,1},{65,33},{97,65},{2,98}... | collective-permute-start | bytes 110600 | tf_op jit(solution)/shard_map/ppermute | solution.py:69
  10.2 0.8 collective-permute-start.1
  11.0 0.0 collective-permute-done.8
  11.0 0.9 collective-permute-start
  11.9 0.0 collective-permute-done.7
  11.9 0.0 collective-permute-done.6
  12.0 2.8 %collective-permute-start.11 = (bf16[4,32,576]{2,1,0:T(8,128)(2,1)S(1)}, bf16[4,32,576]{2,1,0:T(8,128)(2,1)S(1)}, u32[]{:S(2)}, u32[]{:S(2)}) collective-permute-start(bf16[4,32,576]{2,1,0:T(8,128)(2,1)S(1)} %pad_maximum_fusion.1.refs_4_), channel_id=1, source_target_pairs={{0,96},{32,0},{64,32},{96,64},{1,97},{33,1},{65,33},{97,65},{2,98}... | collective-permute-start | bytes 442376 | tf_op jit(solution)/shard_map/ppermute | solution.py:69
  14.7 1.2 collective-permute-start.10
  15.9 0.5 collective-permute-start.9
  16.5 1.9 %collective-permute-start.5 = (bf16[4,32,576]{2,1,0:T(8,128)(2,1)S(1)}, bf16[4,32,576]{2,1,0:T(8,128)(2,1)S(1)}, u32[]{:S(2)}, u32[]{:S(2)}) collective-permute-start(bf16[4,32,576]{2,1,0:T(8,128)(2,1)S(1)} %pad_maximum_fusion.refs_0_), channel_id=1, source_target_pairs={{0,24},{8,0},{16,8},{24,16},{1,25},{9,1},{17,9},{25,17},{2,26},{10... | collective-permute-start | bytes 442376 | tf_op jit(solution)/shard_map/ppermute | solution.py:69
  18.3 2.3 %collective-permute-start.4 = (bf16[4,32,576]{2,1,0:T(8,128)(2,1)S(1)}, bf16[4,32,576]{2,1,0:T(8,128)(2,1)S(1)}, u32[]{:S(2)}, u32[]{:S(2)}) collective-permute-start(bf16[4,32,576]{2,1,0:T(8,128)(2,1)S(1)} %pad_maximum_fusion.refs_0_), channel_id=1, source_target_pairs={{0,16},{8,24},{16,0},{24,8},{1,17},{9,25},{17,1},{25,9},{2,18},{10... | collective-permute-start | bytes 442376 | tf_op jit(solution)/shard_map/ppermute | solution.py:69
  20.6 1.6 %collective-permute-start.3 = (bf16[4,32,576]{2,1,0:T(8,128)(2,1)S(1)}, bf16[4,32,576]{2,1,0:T(8,128)(2,1)S(1)}, u32[]{:S(2)}, u32[]{:S(2)}) collective-permute-start(bf16[4,32,576]{2,1,0:T(8,128)(2,1)S(1)} %pad_maximum_fusion.refs_0_), channel_id=1, source_target_pairs={{0,8},{8,16},{16,24},{24,0},{1,9},{9,17},{17,25},{25,1},{2,10},{10... | collective-permute-start | bytes 442376 | tf_op jit(solution)/shard_map/ppermute | solution.py:69
  22.2 1.7 %copy-done.3 = bf16[2048,576]{0,1:T(8,128)(2,1)S(1)} copy-done((bf16[2048,576]{0,1:T(8,128)(2,1)S(1)}, bf16[2048,576]{0,1:T(8,128)(2,1)}, u32[]{:S(2)}) %copy-start.3) | copy-done | bytes 2359320
  23.9 0.7 copy-done.12
  24.6 1.0 entry.1.refs_9_
  25.6 0.1 pad_add_fusion.info_ref
  25.7 1.5 %collective-permute-done.3.refs_1_ = bf16[4,32,576]{2,1,0:T(8,128)(2,1)S(1)} collective-permute-done((bf16[4,32,576]{2,1,0:T(8,128)(2,1)S(1)}, bf16[4,32,576]{2,1,0:T(8,128)(2,1)S(1)}, u32[]{:S(2)}, u32[]{:S(2)}) %collective-permute-start.3) | collective-permute-done | bytes 147488 | tf_op jit(solution)/shard_map/ppermute | solution.py:69
  27.2 6.0 %attend.1 = bf16[16,72,512]{2,1,0:T(8,128)(2,1)} custom-call(s32[3]{0:T(128)S(1)} %pad_add_fusion.info_ref, bf16[4,32,576]{2,1,0:T(8,128)(2,1)S(1)} %pad_maximum_fusion.refs_0_, bf16[4,32,576]{2,1,0:T(8,128)(2,1)S(1)} %collective-permute-done.3.refs_1_, bf16[4,32,576]{2,1,0:T(8,128)(2,1)S(1)} %collective-permute-done.4.refs_2_, ...), custom_call_target="tpu_custom_call" | custom-call | flops 1800000000 | bytes 5000000 | tf_op jit(solution)/shard_map/attend/pallas_call | solution.py:40
  33.2 0.0 copy-start.5
  33.2 0.0 copy-start.6
  33.2 5.9 %all-to-all-start = ((bf16[16,72,512]{2,1,0:T(8,128)(2,1)}), bf16[16,72,512]{2,1,0:T(8,128)(2,1)S(1)}, u32[]{:S(2)}, u32[]{:S(2)}) async-start(bf16[16,72,512]{2,1,0:T(8,128)(2,1)} %attend.1), calls=%async_computation | async-start | bytes 2359296 | tf_op jit(solution)/shard_map/all_to_all | solution.py:486
  39.2 0.1 stack.53.info_ref
  39.2 0.7 copy-done.14
  40.0 0.7 copy-done.15
  40.7 1.7 %route.1.route_ref = f32[8,1024]{1,0:T(8,128)S(1)} custom-call(s32[5]{0:T(128)S(1)} %stack.53.info_ref, s32[6,4,128]{2,1,0:T(4,128)S(1)} %bitcast.42, f32[6,4,128]{2,1,0:T(4,128)S(1)} %bitcast.43), custom_call_target="tpu_custom_call" | custom-call | flops 60000000 | bytes 60000 | tf_op jit(solution)/shard_map/route/pallas_call | solution.py:40
  42.4 0.6 copy-done.9
  43.0 10.8 %all-to-all-done.parts_ref = bf16[16,72,512]{2,1,0:T(8,128)(2,1)S(1)} async-done(((bf16[16,72,512]{2,1,0:T(8,128)(2,1)}), bf16[16,72,512]{2,1,0:T(8,128)(2,1)S(1)}, u32[]{:S(2)}, u32[]{:S(2)}) %all-to-all-start) | async-done | bytes 1179680 | tf_op jit(solution)/shard_map/all_to_all | solution.py:486
  53.8 0.8 output.1
  54.7 0.0 copy-start.10
  54.7 12.0 %all_to_all.20.parts_ref = bf16[16,8,1024]{2,1,0:T(8,128)(2,1)S(1)} all-to-all(bf16[16,8,1024]{2,1,0:T(8,128)(2,1)S(1)} %bitcast.34), channel_id=1, replica_groups=mesh['x'=4,'z'=4,'y'=4,'core'=2] {'x','z'}, dimensions={0} | all-to-all | bytes 524288 | tf_op jit(solution)/shard_map/all_to_all | solution.py:510
  66.7 1.1 norm.1
  67.8 0.0 copy-start.1
  67.8 21.8 %all_to_all.21 = bf16[64,8,1024]{2,1,0:T(8,128)(2,1)S(1)} all-to-all(bf16[64,8,1024]{2,1,0:T(8,128)(2,1)S(1)} %get-tuple-element.28), channel_id=1, replica_groups=mesh['x'=4,'z'=4,'y'=4,'core'=2] {'y','x','z'}, dimensions={0} | all-to-all | bytes 2097152 | tf_op jit(solution)/shard_map/all_to_all | solution.py:524
  89.6 0.0 collective-permute-start.12
  89.6 1.3 %pick.1 = (bf16[256,2048]{1,0:T(8,128)(2,1)S(1)}, f32[192,128]{1,0:T(8,128)S(1)}, f32[8,256]{1,0:T(8,128)S(1)}) custom-call(s32[5]{0:T(128)S(1)} %stack.53.info_ref, bf16[512,1024]{1,0:T(8,128)(2,1)S(1)} %bitcast.33, f32[8,1024]{1,0:T(8,128)S(1)} %copy-done.10), custom_call_target="tpu_custom_call" | custom-call | flops 1000000000 | bytes 20000000 | tf_op jit(solution)/shard_map/pick/pallas_call | solution.py:40
  90.9 1.3 %collective-permute-done.12.other_ref = bf16[512,1024]{1,0:T(8,128)(2,1)S(1)} collective-permute-done((bf16[512,1024]{1,0:T(8,128)(2,1)S(1)}, bf16[512,1024]{1,0:T(8,128)(2,1)S(1)}, u32[]{:S(2)}, u32[]{:S(2)}) %collective-permute-start.12) | collective-permute-done | bytes 1048608 | tf_op jit(solution)/shard_map/ppermute | solution.py:525
  92.2 5.1 %experts.1 = (bf16[512,1024]{1,0:T(8,128)(2,1)S(1)}, bf16[256,2048]{1,0:T(8,128)(2,1)S(1)}, s32[8,256]{1,0:T(8,128)S(1)}) custom-call(s32[5]{0:T(128)S(1)} %stack.53.info_ref, bf16[176,2048]{1,0:T(8,128)(2,1)} %shared_down_hbm.1, bf16[256,2048]{1,0:T(8,128)(2,1)S(1)} %get-tuple-element.30.mine_x_ref, f32[192,128]{1,0:T(8,128)S(1)} %get-tuple-element.31.mine_scale_ref, ...), custom_call_target="tpu_custom_call" | custom-call | flops 3000000000 | bytes 15000000 | tf_op jit(solution)/shard_map/experts/pallas_call | solution.py:40
  97.3 0.2 collective-permute-start.13
  97.5 0.7 put.1
  98.3 1.8 %collective-permute-done.13 = bf16[512,1024]{1,0:T(8,128)(2,1)S(1)} collective-permute-done((bf16[512,1024]{1,0:T(8,128)(2,1)S(1)}, bf16[512,1024]{1,0:T(8,128)(2,1)S(1)}, u32[]{:S(2)}, u32[]{:S(2)}) %collective-permute-start.13) | collective-permute-done | bytes 1048608 | tf_op jit(solution)/shard_map/ppermute | solution.py:561
  100.1 0.4 fusion
  100.5 23.3 %all_to_all.22 = bf16[64,8,1024]{2,1,0:T(8,128)(2,1)S(1)} all-to-all(bf16[64,8,1024]{2,1,0:T(8,128)(2,1)S(1)} %fusion), channel_id=1, replica_groups=mesh['x'=4,'z'=4,'y'=4,'core'=2] {'x','z','y'}, dimensions={0} | all-to-all | bytes 2097152 | tf_op jit(solution)/shard_map/all_to_all | solution.py:567
  123.8 0.2 convert_reduce_fusion
  124.0 0.7 reshape.27
  (39 shorter events, 0.1 us)
Async XLA Ops:
  0.0 25.6 %copy-start.18 = (s32[2]{0:T(128)S(1)}, s32[2]{0:T(128)}, u32[]{:S(2)}) copy-start(s32[2]{0:T(128)} %counts_hbm.1) | copy-start | bytes 28
  0.0 27.2 %copy-start.13 = (bf16[2,6,128,576]{2,3,1,0:T(8,128)(2,1)S(1)}, bf16[2,6,128,576]{2,3,1,0:T(8,128)(2,1)}, u32[]{:S(2)}) copy-start(bf16[2,6,128,576]{2,3,1,0:T(8,128)(2,1)} %param.37) | copy-start | bytes 5308420
  0.0 27.2 %copy-start.16 = (s32[2,8,64]{2,1,0:T(8,128)S(1)}, s32[2,8,64]{2,1,0:T(8,128)}, u32[]{:S(2)}) copy-start(s32[2,8,64]{2,1,0:T(8,128)} %refs_11_.1) | copy-start | bytes 12292
  0.0 27.2 %copy-start.17 = (s32[4,2,8]{2,1,0:T(2,128)S(1)}, s32[4,2,8]{2,1,0:T(2,128)}, u32[]{:S(2)}) copy-start(s32[4,2,8]{2,1,0:T(2,128)} %refs_10_.1) | copy-start | bytes 772
  2.0 9.0 %collective-permute-start.8 = (bf16[32,576]{1,0:T(8,128)(2,1)S(1)}, bf16[32,576]{1,0:T(8,128)(2,1)S(1)}, u32[]{:S(2)}, u32[]{:S(2)}) collective-permute-start(bf16[32,576]{1,0:T(8,128)(2,1)S(1)} %get-tuple-element.22), channel_id=1, source_target_pairs={{0,24},{8,0},{16,8},{24,16},{1,25},{9,1},{17,9},{25,17},{2,26},{10... | collective-permute-start | bytes 110600 | tf_op jit(solution)/shard_map/ppermute | solution.py:69
  6.2 5.7 %collective-permute-start.7 = (bf16[32,576]{1,0:T(8,128)(2,1)S(1)}, bf16[32,576]{1,0:T(8,128)(2,1)S(1)}, u32[]{:S(2)}, u32[]{:S(2)}) collective-permute-start(bf16[32,576]{1,0:T(8,128)(2,1)S(1)} %get-tuple-element.22), channel_id=1, source_target_pairs={{0,16},{8,24},{16,0},{24,8},{1,17},{9,25},{17,1},{25,9},{2,18},{10... | collective-permute-start | bytes 110600 | tf_op jit(solution)/shard_map/ppermute | solution.py:69
  6.2 5.7 %collective-permute-start.6 = (bf16[32,576]{1,0:T(8,128)(2,1)S(1)}, bf16[32,576]{1,0:T(8,128)(2,1)S(1)}, u32[]{:S(2)}, u32[]{:S(2)}) collective-permute-start(bf16[32,576]{1,0:T(8,128)(2,1)S(1)} %get-tuple-element.22), channel_id=1, source_target_pairs={{0,8},{8,16},{16,24},{24,0},{1,9},{9,17},{17,25},{25,1},{2,10},{10... | collective-permute-start | bytes 110600 | tf_op jit(solution)/shard_map/ppermute | solution.py:69
  7.5 8.4 %collective-permute-start.2 = (bf16[32,576]{1,0:T(8,128)(2,1)S(1)}, bf16[32,576]{1,0:T(8,128)(2,1)S(1)}, u32[]{:S(2)}, u32[]{:S(2)}) collective-permute-start(bf16[32,576]{1,0:T(8,128)(2,1)S(1)} %get-tuple-element.21), channel_id=1, source_target_pairs={{0,96},{32,0},{64,32},{96,64},{1,97},{33,1},{65,33},{97,65},{2,98}... | collective-permute-start | bytes 110600 | tf_op jit(solution)/shard_map/ppermute | solution.py:69
  10.2 6.2 %collective-permute-start.1 = (bf16[32,576]{1,0:T(8,128)(2,1)S(1)}, bf16[32,576]{1,0:T(8,128)(2,1)S(1)}, u32[]{:S(2)}, u32[]{:S(2)}) collective-permute-start(bf16[32,576]{1,0:T(8,128)(2,1)S(1)} %get-tuple-element.21), channel_id=1, source_target_pairs={{0,64},{32,96},{64,0},{96,32},{1,65},{33,97},{65,1},{97,33},{2,66}... | collective-permute-start | bytes 110600 | tf_op jit(solution)/shard_map/ppermute | solution.py:69
  11.0 5.4 %collective-permute-start = (bf16[32,576]{1,0:T(8,128)(2,1)S(1)}, bf16[32,576]{1,0:T(8,128)(2,1)S(1)}, u32[]{:S(2)}, u32[]{:S(2)}) collective-permute-start(bf16[32,576]{1,0:T(8,128)(2,1)S(1)} %get-tuple-element.21), channel_id=1, source_target_pairs={{0,32},{32,64},{64,96},{96,0},{1,33},{33,65},{65,97},{97,1},{2,34}... | collective-permute-start | bytes 110600 | tf_op jit(solution)/shard_map/ppermute | solution.py:69
  12.0 8.7 %collective-permute-start.11 = (bf16[4,32,576]{2,1,0:T(8,128)(2,1)S(1)}, bf16[4,32,576]{2,1,0:T(8,128)(2,1)S(1)}, u32[]{:S(2)}, u32[]{:S(2)}) collective-permute-start(bf16[4,32,576]{2,1,0:T(8,128)(2,1)S(1)} %pad_maximum_fusion.1.refs_4_), channel_id=1, source_target_pairs={{0,96},{32,0},{64,32},{96,64},{1,97},{33,1},{65,33},{97,65},{2,98}... | collective-permute-start | bytes 442376 | tf_op jit(solution)/shard_map/ppermute | solution.py:69
  14.7 10.9 %collective-permute-start.10 = (bf16[4,32,576]{2,1,0:T(8,128)(2,1)S(1)}, bf16[4,32,576]{2,1,0:T(8,128)(2,1)S(1)}, u32[]{:S(2)}, u32[]{:S(2)}) collective-permute-start(bf16[4,32,576]{2,1,0:T(8,128)(2,1)S(1)} %pad_maximum_fusion.1.refs_4_), channel_id=1, source_target_pairs={{0,64},{32,96},{64,0},{96,32},{1,65},{33,97},{65,1},{97,33},{2,66}... | collective-permute-start | bytes 442376 | tf_op jit(solution)/shard_map/ppermute | solution.py:69
  15.9 9.7 %collective-permute-start.9 = (bf16[4,32,576]{2,1,0:T(8,128)(2,1)S(1)}, bf16[4,32,576]{2,1,0:T(8,128)(2,1)S(1)}, u32[]{:S(2)}, u32[]{:S(2)}) collective-permute-start(bf16[4,32,576]{2,1,0:T(8,128)(2,1)S(1)} %pad_maximum_fusion.1.refs_4_), channel_id=1, source_target_pairs={{0,32},{32,64},{64,96},{96,0},{1,33},{33,65},{65,97},{97,1},{2,34}... | collective-permute-start | bytes 442376 | tf_op jit(solution)/shard_map/ppermute | solution.py:69
  16.5 9.2 %collective-permute-start.5 = (bf16[4,32,576]{2,1,0:T(8,128)(2,1)S(1)}, bf16[4,32,576]{2,1,0:T(8,128)(2,1)S(1)}, u32[]{:S(2)}, u32[]{:S(2)}) collective-permute-start(bf16[4,32,576]{2,1,0:T(8,128)(2,1)S(1)} %pad_maximum_fusion.refs_0_), channel_id=1, source_target_pairs={{0,24},{8,0},{16,8},{24,16},{1,25},{9,1},{17,9},{25,17},{2,26},{10... | collective-permute-start | bytes 442376 | tf_op jit(solution)/shard_map/ppermute | solution.py:69
  18.3 7.3 %collective-permute-start.4 = (bf16[4,32,576]{2,1,0:T(8,128)(2,1)S(1)}, bf16[4,32,576]{2,1,0:T(8,128)(2,1)S(1)}, u32[]{:S(2)}, u32[]{:S(2)}) collective-permute-start(bf16[4,32,576]{2,1,0:T(8,128)(2,1)S(1)} %pad_maximum_fusion.refs_0_), channel_id=1, source_target_pairs={{0,16},{8,24},{16,0},{24,8},{1,17},{9,25},{17,1},{25,9},{2,18},{10... | collective-permute-start | bytes 442376 | tf_op jit(solution)/shard_map/ppermute | solution.py:69
  20.6 6.5 %collective-permute-start.3 = (bf16[4,32,576]{2,1,0:T(8,128)(2,1)S(1)}, bf16[4,32,576]{2,1,0:T(8,128)(2,1)S(1)}, u32[]{:S(2)}, u32[]{:S(2)}) collective-permute-start(bf16[4,32,576]{2,1,0:T(8,128)(2,1)S(1)} %pad_maximum_fusion.refs_0_), channel_id=1, source_target_pairs={{0,8},{8,16},{16,24},{24,0},{1,9},{9,17},{17,25},{25,1},{2,10},{10... | collective-permute-start | bytes 442376 | tf_op jit(solution)/shard_map/ppermute | solution.py:69
  22.2 1.7 %copy-start.3 = (bf16[2048,576]{0,1:T(8,128)(2,1)S(1)}, bf16[2048,576]{0,1:T(8,128)(2,1)}, u32[]{:S(2)}) copy-start(bf16[2048,576]{0,1:T(8,128)(2,1)} %param.25) | copy-start | bytes 7077892
  23.9 0.7 copy-start.12
  33.2 20.6 %copy-start.7 = (bf16[128,2048]{1,0:T(8,128)(2,1)S(1)}, bf16[128,2048]{1,0:T(8,128)(2,1)}, u32[]{:S(2)}) copy-start(bf16[128,2048]{1,0:T(8,128)(2,1)} %out_ref.1) | copy-start | bytes 1572868
  33.2 20.6 %copy-start.8 = (bf16[1,512,128]{2,1,0:T(8,128)(2,1)S(1)}, bf16[1,512,128]{2,1,0:T(8,128)(2,1)}, u32[]{:S(2)}) copy-start(bf16[1,512,128]{2,1,0:T(8,128)(2,1)} %value_ref.1) | copy-start | bytes 393220
  33.2 33.5 %copy-start.4 = (bf16[4,16,2048]{2,1,0:T(8,128)(2,1)S(1)}, bf16[4,16,2048]{2,1,0:T(8,128)(2,1)}, u32[]{:S(2)}) copy-start(bf16[4,16,2048]{2,1,0:T(8,128)(2,1)} %embeds_ref.1) | copy-start | bytes 786436
  33.2 33.5 %copy-start.11 = (f32[2048]{0:T(1024)S(1)}, f32[2048]{0:T(1024)}, u32[]{:S(2)}) copy-start(f32[2048]{0:T(1024)} %param.30) | copy-start | bytes 24580
  33.2 59.0 %copy-start.5 = (bf16[2048,176]{0,1:T(8,128)(2,1)S(1)}, bf16[2048,176]{0,1:T(8,128)(2,1)}, u32[]{:S(2)}) copy-start(bf16[2048,176]{0,1:T(8,128)(2,1)} %param.31) | copy-start | bytes 2162692
  33.2 59.0 %copy-start.6 = (bf16[2048,176]{0,1:T(8,128)(2,1)S(1)}, bf16[2048,176]{0,1:T(8,128)(2,1)}, u32[]{:S(2)}) copy-start(bf16[2048,176]{0,1:T(8,128)(2,1)} %param.32) | copy-start | bytes 2162692
  33.2 20.6 %all-to-all-start = ((bf16[16,72,512]{2,1,0:T(8,128)(2,1)}), bf16[16,72,512]{2,1,0:T(8,128)(2,1)S(1)}, u32[]{:S(2)}, u32[]{:S(2)}) async-start(bf16[16,72,512]{2,1,0:T(8,128)(2,1)} %attend.1), calls=%async_computation | async-start | bytes 2359296 | tf_op jit(solution)/shard_map/all_to_all | solution.py:486
  39.2 0.7 copy-start.14
  39.9 0.7 copy-start.15
  42.4 0.6 copy-start.9
  53.8 38.4 %copy-start.2 = (bf16[2,352,2048]{2,1,0:T(8,128)(2,1)S(1)}, bf16[2,352,2048]{2,1,0:T(8,128)(2,1)}, u32[]{:S(2)}) copy-start(bf16[2,352,2048]{2,1,0:T(8,128)(2,1)} %down_ref.1) | copy-start | bytes 8650756
  54.7 34.9 %copy-start.10 = (f32[8,1024]{1,0:T(8,128)S(1)}, f32[8,1024]{1,0:T(8,128)}, u32[]{:S(2)}) copy-start(f32[8,1024]{1,0:T(8,128)} %copy-done.9) | copy-start | bytes 98308
  67.8 24.5 %copy-start.1 = (bf16[2,2048,352]{1,2,0:T(8,128)(2,1)S(1)}, bf16[2,2048,352]{1,2,0:T(8,128)(2,1)}, u32[]{:S(2)}) copy-start(bf16[2,2048,352]{1,2,0:T(8,128)(2,1)} %param.35) | copy-start | bytes 8650756
  89.6 2.7 %copy-start = (bf16[2,2048,352]{1,2,0:T(8,128)(2,1)S(1)}, bf16[2,2048,352]{1,2,0:T(8,128)(2,1)}, u32[]{:S(2)}) copy-start(bf16[2,2048,352]{1,2,0:T(8,128)(2,1)} %param.34) | copy-start | bytes 8650756
  89.6 2.7 %collective-permute-start.12 = (bf16[512,1024]{1,0:T(8,128)(2,1)S(1)}, bf16[512,1024]{1,0:T(8,128)(2,1)S(1)}, u32[]{:S(2)}, u32[]{:S(2)}) collective-permute-start(bf16[512,1024]{1,0:T(8,128)(2,1)S(1)} %bitcast.32), channel_id=1, source_target_pairs={{0,1},{1,0},{2,3},{3,2},{4,5},{5,4},{6,7},{7,6},{8,9},{9,8},{10,11... | collective-permute-start | bytes 3145736 | tf_op jit(solution)/shard_map/ppermute | solution.py:525
  97.3 2.7 %collective-permute-start.13 = (bf16[512,1024]{1,0:T(8,128)(2,1)S(1)}, bf16[512,1024]{1,0:T(8,128)(2,1)S(1)}, u32[]{:S(2)}, u32[]{:S(2)}) collective-permute-start(bf16[512,1024]{1,0:T(8,128)(2,1)S(1)} %get-tuple-element.36), channel_id=1, source_target_pairs={{0,1},{1,0},{2,3},{3,2},{4,5},{5,4},{6,7},{7,6},{8,9},{9,8},{10,11... | collective-permute-start | bytes 3145736 | tf_op jit(solution)/shard_map/ppermute | solution.py:561

commit v4 on v3

--- a/solution.py
+++ b/solution.py
@@ -21,6 +21,7 @@
 OUT_ORDER = BLK + BEAM
 CORES = [(0, 1), (1, 0)]
 SCALARS = (pltpu.SMEM,)
+VMEM_MIB = {"attend": 20, "pick": 16, "experts": 16, "put": 12}
 
 f32, bf16 = jnp.float32, jnp.bfloat16
 LAST = (((1,), (1,)), ((), ()))
@@ -43,7 +44,7 @@
         in_specs=first + [vmem] * (len(args) - len(first)),
         out_specs=[vmem] * len(outs),
         scratch_shapes=scratch,
-        compiler_params=pltpu.CompilerParams(vmem_limit_bytes=24 << 20),
+        compiler_params=pltpu.CompilerParams(vmem_limit_bytes=VMEM_MIB.get(name, 6) << 20),
         cost_estimate=pl.CostEstimate(flops=cost[0], bytes_accessed=cost[1], transcendentals=cost[2]),
         name=name,
     )(*args)
@@ -64,13 +65,19 @@
     return [pltpu.VMEM(a.shape, a.dtype) for a in arrays] + [pltpu.SemaphoreType.DMA((len(arrays),))]
 
 
-def shifted(value, axis, by):
-    size = lax.axis_size(axis)
-    return lax.ppermute(value, axis, [(i, (i + by) % size) for i in range(size)])
-
-
-def gather(value, axis):
-    arrived = {s: shifted(value, axis, s) for s in (1, 3, 2)}
+def shifted(value, turn, by):
+    pairs = []
+    for x in range(4):
+        for z in range(4):
+            for core in range(2):
+                along_x = core == turn
+                to = ((x + by) % 4, z) if along_x else (x, (z + by) % 4)
+                pairs.append((8 * x + 2 * z + core, 8 * to[0] + 2 * to[1] + core))
+    return lax.ppermute(value, ("x", "z", "core"), pairs)
+
+
+def gather(value, turn):
+    arrived = {s: shifted(value, turn, s) for s in (1, 3, 2)}
     return [value] + [arrived[s] for s in range(1, 4)]
 
 
@@ -87,14 +94,14 @@
 
 
 def query_kernel(
-    embeds_hbm, query_hbm, key_up_hbm, gain_hbm, frequency_hbm, counts_hbm,
-    first_ref, second_ref, normed_ref, cos_ref,
+    embeds_hbm, query_hbm, key_up_hbm, gain_hbm, frequency_hbm, counts_hbm, latent_hbm,
+    result_ref, normed_ref, cos_ref, latent_ref,
     embeds_ref, query_ref, key_up_ref, gain_ref, frequency_ref, counts_ref, sems,
 ):
     steps, _, width = embeds_ref.shape
     copies = fetch(
-        (embeds_hbm, query_hbm, key_up_hbm, gain_hbm, frequency_hbm, counts_hbm),
-        (embeds_ref, query_ref, key_up_ref, gain_ref, frequency_ref, counts_ref),
+        (embeds_hbm, query_hbm, key_up_hbm, gain_hbm, frequency_hbm, counts_hbm, latent_hbm),
+        (embeds_ref, query_ref, key_up_ref, gain_ref, frequency_ref, counts_ref, latent_ref),
         sems,
     )
     copies[4].wait()
@@ -117,9 +124,9 @@
     rope = queries[:, 128:]
     cosine, sine = rope_parts(cos_ref, 64)
     rope = (rope.astype(f32) * cosine + turned(rope) * sine).astype(bf16)
-    for g, ref in enumerate((first_ref, second_ref)):
-        ref[:, :512] = latent[32 * g : 32 * g + 32]
-        ref[:, 512:] = rope[32 * g : 32 * g + 32]
+    result_ref[:, :512] = latent
+    result_ref[:, 512:] = rope
+    copies[6].wait()
 
 
 def entry_kernel(normed_ref, latent_ref, gain_ref, cos_ref, out_ref):
@@ -131,18 +138,19 @@
     out_ref[:, 512:] = (rope * cosine + turned(rope, lax.Precision.HIGHEST) * sine).astype(bf16)
 
 
-def split_terms(line):
-    first = line.astype(bf16).astype(f32)
-    second = (line - first).astype(bf16).astype(f32)
-    third = line - first - second
-    place = sublanes((8, line.shape[1]))
-    tile = jnp.where(place == 0, first, 0.0)
-    tile = jnp.where(place == 1, second, tile)
-    return jnp.where(place == 2, third, tile).astype(bf16)
-
-
-def joined_terms(tile):
-    tile = tile.astype(f32)
+def split_terms(lines):
+    place = sublanes((8, lines[0].shape[1]))
+    tile = jnp.zeros(place.shape, f32)
+    for k, line in enumerate(lines):
+        first = line.astype(bf16).astype(f32)
+        second = (line - first).astype(bf16).astype(f32)
+        for j, term in enumerate((first, second, line - first - second)):
+            tile = jnp.where(place == 3 * k + j, term, tile)
+    return tile.astype(bf16)
+
+
+def joined_terms(tile, k):
+    tile = tile.astype(f32)[3 * k : 3 * k + 3]
     return tile[0:1] + tile[1:2] + tile[2:3]
 
 
@@ -157,13 +165,15 @@
 
 
 def attend_kernel(info_ref, *refs):
-    q_refs = (refs[:4], refs[4:8])
-    cache_ref, entry_ref, parent_ref, table_ref, out_ref, sum_ref = refs[8:]
-    near, rows, width = q_refs[0][0].shape
+    q_refs, out_refs = refs[:4], refs[8:12]
+    cache_ref, entry_ref, parent_ref, table_ref = refs[4:8]
+    sum_ref = refs[12]
+    near, rows_all, width = q_refs[0].shape
     heads = 4 * near
     groups, beams, _ = table_ref.shape
+    rows = rows_all // groups
     pool, _, block_len = cache_ref.shape[1:]
-    latent = out_ref.shape[2]
+    latent = out_refs[0].shape[1]
     steps = rows // beams
     scale = (width - latent + 128) ** (-0.5)
     blk = info_ref[0]
@@ -196,7 +206,7 @@
         recent_bias = jnp.where((seen > 0.5) & (blk == 0), 0.0, NEG)
 
         part = slice(g * rows, (g + 1) * rows)
-        q = jnp.concatenate([ref[...] for ref in q_refs[g]], axis=0).reshape(heads * rows, width)
+        q = jnp.concatenate([ref[:, part, :] for ref in q_refs], axis=0).reshape(heads * rows, width)
         keys = jnp.concatenate([cache_ref[g, p] for p in range(pool)], axis=1)
         entry = entry_ref[part]
         scores = jnp.dot(q, keys, preferred_element_type=f32)
@@ -216,25 +226,48 @@
         lat = (lat.reshape(heads, rows, latent) / total).astype(bf16)
         lse = jnp.where(top > 0.1 * NEG, top + jnp.log(total), NEG)
         lse = jnp.broadcast_to(lse, (heads, rows, 128))
-        for f in range(4):
-            for s in range(near):
-                dx, dz = (s, f) if g == 0 else (f, s)
-                home = (((blk >> 2) - dx) & 3) * 4 + ((blk - dz) & 3)
-                out_ref[home, part, :] = lat[f * near + s]
-                sum_ref[home, part, :] = lse[f * near + s]
-    for h in range(heads):
-        tile = split_terms(as_line(sum_ref[h]))
-        out_ref[h, groups * rows :, :128] = tile
-        out_ref[h, groups * rows :, 128:] = jnp.zeros((8, latent - 128), bf16)
-
-
-def output_kernel(parts_ref, value_ref, out_ref, result_ref):
-    count, rows = parts_ref.shape[0], 64
-    sums = [joined_terms(parts_ref[k, rows:, :128]) for k in range(count)]
+        for s in range(near):
+            for f in range(4):
+                first = f * rows_all + g * rows
+                out_refs[s][first : first + rows, :] = lat[f * near + s]
+                sum_ref[s, first : first + rows, :] = lse[f * near + s]
+    for s, ref in enumerate(out_refs):
+        lines = [as_line(sum_ref[s, 128 * k : 128 * k + 128, :]) for k in range(2)]
+        ref[4 * rows_all :, :128] = split_terms(lines)
+        ref[4 * rows_all :, 128:] = jnp.zeros((8, latent - 128), bf16)
+
+
+def shares(sums):
     best = functools.reduce(jnp.maximum, sums)
-    shares = [jnp.exp(v - best) for v in sums]
-    whole = functools.reduce(jnp.add, shares)
-    joined = sum(as_column(p / whole, rows) * parts_ref[k, :rows, :].astype(f32) for k, p in enumerate(shares))
+    parts = [jnp.exp(v - best) for v in sums]
+    whole = functools.reduce(jnp.add, parts)
+    return [p / whole for p in parts], best + jnp.log(whole)
+
+
+def merge_kernel(*refs):
+    parts, outs = refs[:4], refs[4:]
+    rows = 64
+    lines = []
+    for k in range(2):
+        part_share, whole = shares([joined_terms(ref[4 * rows :, :128], k) for ref in parts])
+        lines.append(whole)
+        own = slice(128 * k, 128 * k + 128)
+        merged = sum(as_column(p, 128) * ref[own, :].astype(f32) for p, ref in zip(part_share, parts))
+        merged = merged.astype(bf16)
+        for f in range(2):
+            outs[2 * k + f][:rows, :] = merged[rows * f : rows * f + rows]
+    tile = split_terms(lines)
+    for ref in outs:
+        ref[rows:, :128] = tile
+        ref[rows:, 128:] = jnp.zeros((8, ref.shape[1] - 128), bf16)
+
+
+def output_kernel(*refs):
+    parts, (value_ref, out_ref, result_ref) = refs[:4], refs[4:]
+    rows = 64
+    sums = [as_column(joined_terms(ref[rows:, :128], f // 2), rows, rows * (f % 2)) for f, ref in enumerate(parts)]
+    part_share, _ = shares(sums)
+    joined = sum(p * ref[:rows, :].astype(f32) for p, ref in zip(part_share, parts))
     head_out = jnp.dot(joined.astype(bf16), value_ref[0], preferred_element_type=f32).astype(bf16)
     line, row = sublanes((128, rows)), lanes((128, rows))
     source = 32 * (line >> 6) + 8 * ((line >> 1) & 3) + ((line >> 3) & 7)
@@ -271,7 +304,7 @@
 
 def line_row(line, core):
     chip = (line >> 3) & 63
-    return 32 * (chip >> 4) + 16 * ((line >> 9) ^ core) + (chip & 15)
+    return 32 * (chip >> 4) + 16 * ((line >> 9) ^ core) + 4 * (chip & 3) + ((chip >> 2) & 3)
 
 
 def route_kernel(info_ref, ids_ref, weights_ref, out_ref):
@@ -307,7 +340,8 @@
 
 def line_places(line, core, lines):
     row = line_row(line, core)
-    return ((row & 1) ^ core) * (lines // 2) + (row >> 1) * 4 + ((line >> 1) & 3)
+    chip = 16 * ((row >> 1) & 3) + 4 * ((row >> 3) & 3) + (row >> 5)
+    return ((row & 1) ^ core) * (lines // 2) + chip * 4 + ((line >> 1) & 3)
 
 
 def picked(source_ref, hit, line, place, weights):
@@ -325,9 +359,22 @@
     return halves, jnp.concatenate(scale, axis=0), spot
 
 
-def pick_kernel(info_ref, mine_ref, route_ref, x_ref, scale_ref, spot_ref):
-    core, y = info_ref[0], info_ref[2]
+def gated(x, gate, up):
+    gate_val = lax.dot_general(x, gate, LAST, preferred_element_type=f32)
+    up_val = lax.dot_general(x, up, LAST, preferred_element_type=f32)
+    return (gate_val / (1.0 + jnp.exp(-gate_val)) * up_val).astype(bf16)
+
+
+def pick_kernel(
+    info_ref, gate_hbm, up_hbm, down_hbm, mine_ref, route_ref, resid_ref,
+    x_ref, own_ref, scale_ref, spot_ref,
+    gate_ref, up_ref, down_ref, sems,
+):
+    core, blk, y = info_ref[0], info_ref[1], info_ref[2]
+    own_chip = 4 * (blk & 3) + (blk >> 2)
     lines, half = mine_ref.shape
+    routed = 2 * SLOTS
+    copies = fetch((gate_hbm, up_hbm, down_hbm), (gate_ref, up_ref, down_ref), sems)
     line = lanes((1, lines))
     hits = [sublanes((SLOTS, lines)) + 1 == route_ref[e : e + 1, :lines].astype(jnp.int32) for e in range(2)]
     hits.append(sublanes((OWN_ROWS, lines)) == (line >> 1) - y * OWN_ROWS)
@@ -335,9 +382,18 @@
     place = line_places(line, core, lines)
     halves, scale, spot = picked(mine_ref, hit, line, place, [route_ref[2 + e : 3 + e, :lines] for e in range(2)])
     for q in range(2):
-        x_ref[:, q * half : (q + 1) * half] = halves[q].astype(bf16)
+        x_ref[:, q * half : (q + 1) * half] = halves[q][:routed].astype(bf16)
     scale_ref[...] = jnp.broadcast_to(scale, scale_ref.shape)
     spot_ref[...] = spot
+    own_rows = jnp.concatenate([v[routed:].astype(bf16) for v in halves], axis=1)
+    for copy in copies:
+        copy.wait()
+    act = gated(own_rows, gate_ref[...], up_ref[...])
+    own = jnp.dot(act, down_ref[...], preferred_element_type=f32)
+    for t in range(4):
+        whole = jnp.concatenate([resid_ref[2 * t + q : 2 * t + q + 1, :] for q in range(2)], axis=1)
+        own = own + jnp.where(sublanes((OWN_ROWS, 1)) == own_chip * 4 + t, whole, 0.0)
+    own_ref[...] = own.astype(bf16)
 
 
 def put(ref, y_ref, spot, side):
@@ -353,14 +409,12 @@
 
 
 def expert_kernel(
-    info_ref, shared_down_hbm, mine_x_ref, mine_scale_ref, mine_spot_ref, other_ref, route_ref, resid_ref,
-    gate_ref, up_ref, down_ref, shared_gate_ref, shared_up_ref,
-    other_out_ref, y_ref, spot_ref,
-    x_ref, shared_down_ref, sems,
+    info_ref, mine_x_ref, own_ref, mine_scale_ref, mine_spot_ref, other_ref, route_ref,
+    gate_ref, up_ref, down_ref,
+    other_out_ref, y_ref, spot_ref, x_ref,
 ):
-    core, blk = info_ref[0], info_ref[1]
+    core = info_ref[0]
     lines, half = other_ref.shape
-    (copy,) = fetch((shared_down_hbm,), (shared_down_ref,), sems)
     line = lanes((1, lines)) + lines
     hits = [sublanes((SLOTS, lines)) + 1 == route_ref[e : e + 1, lines:].astype(jnp.int32) for e in range(2)]
     hit = jnp.concatenate([jnp.where(h, 1.0, 0.0) for h in hits], axis=0)
@@ -369,29 +423,18 @@
     routed = 2 * SLOTS
     for q in range(2):
         columns = slice(q * half, (q + 1) * half)
-        x_ref[:, columns] = (mine_x_ref[:routed, columns].astype(f32) + halves[q]).astype(bf16)
+        x_ref[:, columns] = (mine_x_ref[:, columns].astype(f32) + halves[q]).astype(bf16)
     scale = scale + mine_scale_ref[:, :1]
     spot = jnp.concatenate([spot, jnp.zeros((8, OWN_ROWS), f32)], axis=1) + mine_spot_ref[...]
     spot = (spot[0:1] * 16.0 + spot[1:2] - 1.0).astype(jnp.int32)
     spot_ref[...] = jnp.broadcast_to(spot, spot_ref.shape)
-
-    def gated(x, gate, up):
-        gate_val = lax.dot_general(x, gate, LAST, preferred_element_type=f32)
-        up_val = lax.dot_general(x, up, LAST, preferred_element_type=f32)
-        return (gate_val / (1.0 + jnp.exp(-gate_val)) * up_val).astype(bf16)
 
     for e in range(2):
         part = slice(e * SLOTS, (e + 1) * SLOTS)
         act = gated(x_ref[part, :], gate_ref[e], up_ref[e])
         down = jnp.dot(act, down_ref[e], preferred_element_type=f32)
         y_ref[part, :] = (down * scale[part]).astype(bf16)
-    act = gated(mine_x_ref[routed:, :], shared_gate_ref[...], shared_up_ref[...])
-    copy.wait()
-    own = jnp.dot(act, shared_down_ref[...], preferred_element_type=f32)
-    for t in range(4):
-        whole = jnp.concatenate([resid_ref[2 * t + q : 2 * t + q + 1, :] for q in range(2)], axis=1)
-        own = own + jnp.where(sublanes((OWN_ROWS, 1)) == blk * 4 + t, whole, 0.0)
-    y_ref[routed:, :] = own.astype(bf16)
+    y_ref[routed:, :] = own_ref[...]
     put(other_out_ref, y_ref, spot, 1)
 
 
@@ -425,7 +468,7 @@
     steps, row_dev, width = embeds.shape
     groups, beams, _ = block_tables.shape
     latent = w_key_up.shape[2]
-    block_len, entry_width = cache_pool.shape[2:]
+    entry_width = cache_pool.shape[3]
     rope = entry_width - latent
     pair_dev, _, unit_dev = w_expert_gate.shape
     half = width // 2
@@ -441,49 +484,33 @@
     frequency = np.tile(frequency.astype(np.float32), 4).reshape(1, 128)
     rows_all = groups * steps * beams
     blk_size = lax.axis_size("x") * lax.axis_size("z")
-    sources = (embeds, w_query.T, w_key_up, attn_gain.reshape(1, width), jnp.asarray(frequency), block_counts)
-    query = ((steps * beams, entry_width), bf16)
-    first, second, normed, cosines = kernel_call(
+    sources = (embeds, w_query.T, w_key_up, attn_gain.reshape(1, width), jnp.asarray(frequency), block_counts, w_latent.T)
+    query, normed, cosines, latent_weights = kernel_call(
         query_kernel,
         "query",
-        [query, query, ((rows_all, width), bf16), ((8, 128), f32)],
-        [pltpu.VMEM(a.shape, a.dtype) for a in sources[:-1]]
+        [((rows_all, entry_width), bf16), ((rows_all, width), bf16), ((8, 128), f32), ((entry_width, width), bf16)],
+        [pltpu.VMEM(a.shape, a.dtype) for a in sources[:-2]]
         + [pltpu.SMEM(block_counts.shape, jnp.int32), pltpu.SemaphoreType.DMA((len(sources),))],
         (60_000_000, 20_000_000, 0),
         (pltpu.HBM,) * len(sources),
         *in_hbm(*sources),
     )
-    first, second = jnp.stack(gather(first, "x")), jnp.stack(gather(second, "z"))
-    queries = gather(first, "z") + gather(second, "x")
+    query = jnp.stack(gather(query, 0))
+    queries = gather(query, 1)
+    _, normed, expert_ids = lax.optimization_barrier((query, normed, expert_ids))
     (entries,) = kernel_call(
         entry_kernel,
         "entry",
         [((rows_all, entry_width), bf16)],
         [],
-        (150_000_000, 40_000_000, 0),
+        (150_000_000, 3_000_000, 0),
         (),
         normed,
-        w_latent.T,
+        latent_weights,
         latent_gain.reshape(1, latent),
         cosines,
     )
     cache = cache_pool.transpose(0, 1, 3, 2)
-    (parts,) = kernel_call(
-        attend_kernel,
-        "attend",
-        [((blk_size, rows_all + 8, latent), bf16)],
-        [pltpu.VMEM((blk_size, rows_all, 128), f32)],
-        (1_800_000_000, 5_000_000, 800_000),
-        SCALARS,
-        counts,
-        *queries,
-        cache,
-        entries,
-        parents,
-        block_tables,
-    )
-    expert_ids, parts = lax.optimization_barrier((expert_ids, parts))
-    parts = lax.all_to_all(parts, BLK, 0, 0)
     (route,) = kernel_call(
         route_kernel,
         "route",
@@ -495,7 +522,28 @@
         expert_ids.transpose(2, 0, 1),
         expert_weights.transpose(2, 0, 1),
     )
-    parts, route = lax.optimization_barrier((parts, route))
+    counts, route = lax.optimization_barrier((counts, route))
+    part = ((4 * rows_all + 8, latent), bf16)
+    parts = kernel_call(
+        attend_kernel,
+        "attend",
+        [part] * 4,
+        [pltpu.VMEM((4, 4 * rows_all, 128), f32)],
+        (1_800_000_000, 5_000_000, 800_000),
+        SCALARS,
+        counts,
+        *queries,
+        cache,
+        entries,
+        parents,
+        block_tables,
+    )
+    moved = {s: shifted(parts[s], 0, -s) for s in (1, 3, 2)}
+    parts = [parts[0]] + [moved[s] for s in range(1, 4)]
+    last = ((rows_all + 8, latent), bf16)
+    parts = kernel_call(merge_kernel, "merge", [last] * 4, [], (4_000_000, 30_000_000, 2_000), (), *parts)
+    moved = {f: shifted(parts[f], 1, -f) for f in (1, 3, 2)}
+    parts = [parts[0]] + [moved[f] for f in range(1, 4)]
     (attn_part,) = kernel_call(
         output_kernel,
         "output",
@@ -503,7 +551,7 @@
         [],
         (80_000_000, 90_000_000, 1_000),
         (),
-        parts,
+        *parts,
         w_value_up,
         w_out,
     )
@@ -521,42 +569,42 @@
         ffn_gain.reshape(1, width),
     )
 
-    mine = lax.all_to_all(spread, ("y", "x", "z"), 0, 0).reshape(lines, half)
+    mine = lax.all_to_all(spread, ("y", "z", "x"), 0, 0).reshape(lines, half)
     other = lax.ppermute(mine, "core", CORES)
     routed = pair_dev * SLOTS
     total = routed + OWN_ROWS
-    slots = [((total, width), bf16), ((routed, 128), f32), ((8, total), f32)]
-    x_mine, scale, spot = kernel_call(
+    slots = [((routed, width), bf16), ((OWN_ROWS, width), bf16), ((routed, 128), f32), ((8, total), f32)]
+    fetched = (w_shared_gate.T, w_shared_up.T, w_shared_down)
+    x_mine, own, scale, spot = kernel_call(
         pick_kernel,
         "pick",
         slots,
-        [],
+        room_for(fetched),
         (1_000_000_000, 20_000_000, 0),
-        SCALARS,
+        SCALARS + (pltpu.HBM,) * len(fetched),
         place,
+        *in_hbm(*fetched),
         mine,
         route,
+        resid,
     )
     other_out, outs, spot = kernel_call(
         expert_kernel,
         "experts",
         [((lines, half), bf16), ((total, width), bf16), ((8, total), jnp.int32)],
-        [pltpu.VMEM((routed, width), bf16)] + room_for((w_shared_down,)),
+        [pltpu.VMEM((routed, width), bf16)],
         (3_000_000_000, 15_000_000, 300_000),
-        SCALARS + (pltpu.HBM,),
+        SCALARS,
         place,
-        *in_hbm(w_shared_down),
         x_mine,
+        own,
         scale,
         spot,
         other,
         route,
-        resid,
         w_expert_gate.transpose(0, 2, 1),
         w_expert_up.transpose(0, 2, 1),
         w_expert_down,
-        w_shared_gate.T,
-        w_shared_up.T,
     )
     arrived = lax.ppermute(other_out, "core", CORES)
     (own_out,) = kernel_call(
@@ -564,7 +612,7 @@
     )
     own_out = own_out.astype(f32) + arrived.astype(f32)
     own_out = own_out.astype(bf16).reshape(chips, 2 * steps, half)
-    result = jnp.sum(lax.all_to_all(own_out, ("x", "z", "y"), 0, 0).astype(f32), axis=0)
+    result = jnp.sum(lax.all_to_all(own_out, ("y", "z", "x"), 0, 0).astype(f32), axis=0)
     return result.reshape(steps, 1, width)
 
 

time: 125 us -> 124 us (level)
  waiting for transfers between devices: 15.5 us -> 28.9 us
  starting transfers between devices: 26.3 us -> 15.3 us
  local copies, waits for them, and re-layouts: 5.19 us -> 0.82 us
  Pallas kernels: 19.7 us -> 21 us
    ppermute x12, waiting for transfers between devices: 1.54 us -> 27.3 us  [shifted(): return lax.ppermute(value, ('x', 'z', 'core'), pairs)]
    all_to_all x1 -> x0, waiting for transfers between devices: 10.8 us -> none  [per_device(): parts = lax.all_to_all(parts, BLK, 0, 0)]
    all_to_all x1 -> x0, starting transfers between devices: 5.91 us -> none  [per_device(): parts = lax.all_to_all(parts, BLK, 0, 0)]
    ppermute x12, starting transfers between devices: 20.1 us -> 14.7 us  [shifted(): return lax.ppermute(value, ('x', 'z', 'core'), pairs)]
    unnamed x38 -> x28, local copies, waits for them, and re-layouts: 4.44 us -> 0.07 us
    ppermute x1, waiting for transfers between devices: 1.32 us -> 0.01 us  [per_device(): other = lax.ppermute(mine, 'core', CORES)]
    pallas_call x9 -> x10, Pallas kernels: 19.7 us -> 21 us  [kernel_call(): pl.pallas_call(body, out_shape=[jax.ShapeDtypeStruct(shape, dtype) for sh...]
  transfers between devices with their start and end apart: 15 -> 14, of which waited for: 4 -> 13; matrix products, arithmetic and copies ran while one was open for 0% -> 0% of each run, Pallas kernels for 4% -> 6%
where the time goes in v4:
time: 124 us
  blocking collectives  57.2 us (46%)
  waiting for transfers between devices  28.9 us (23%)
  Pallas kernels  21 us (17%)
  starting transfers between devices  15.3 us (12%)
    ppermute x12, waiting for transfers between devices, shifted(): return lax.ppermute(value, ('x', 'z', 'core'), pairs)  27.3 us
    all_to_all x1, blocking collectives, per_device(): lax.all_to_all(own_out, ('y', 'z', 'x'), 0, 0).astype(f32)  23.8 us
    all_to_all x1, blocking collectives, per_device(): mine = lax.all_to_all(spread, ('y', 'z', 'x'), 0, 0).reshape(lines, half)  22 us
    pallas_call x10, Pallas kernels, kernel_call(): pl.pallas_call(body, out_shape=[jax.ShapeDtypeStruct(shape, dtype) for sh...  21 us
    ppermute x12, starting transfers between devices, shifted(): return lax.ppermute(value, ('x', 'z', 'core'), pairs)  14.7 us
    all_to_all x1, blocking collectives, per_device(): lax.all_to_all(attn_part.reshape(row_dev, 2 * steps, half), BLK, 0, 0)  11.4 us
  transfers between devices with their start and end apart: 14, of which 13 were waited for; matrix products, arithmetic and copies ran while one was open for 0% of the time, Pallas kernels for 6%

profile of v4, /device:TPU:0, one launch (start us, length us, event | category | flops | bytes accessed | tf_op | source)
XLA Modules:
  0.0 124.1 jit_solution(12997835475295159465)
XLA Ops:
  0.0 2.2 %query.1 = (bf16[64,576]{1,0:T(8,128)(2,1)S(1)}, bf16[64,2048]{1,0:T(8,128)(2,1)S(1)}, f32[8,128]{1,0:T(8,128)S(1)}, bf16[576,2048]{1,0:T(8,128)(2,1)S(1)}) custom-call(bf16[4,16,2048]{2,1,0:T(8,128)(2,1)} %embeds_ref.1, bf16[192,2048]{1,0:T(8,128)(2,1)} %bitcast.37, bf16[1,128,512]{2,1,0:T(8,128)(2,1)} %key_up_hbm.1, f32[1,2048]{1,0:T(1,128)} %bitcast.41, ...), custom_call_target="tpu_custom_call" | custom-call | flops 60000000 | bytes 20000000 | tf_op jit(solution)/shard_map/query/pallas_call | solution.py:41
  2.2 0.0 copy-start.11
  2.2 0.0 copy-start.12
  2.2 2.9 %collective-permute-start.2 = (bf16[64,576]{1,0:T(8,128)(2,1)S(1)}, bf16[64,576]{1,0:T(8,128)(2,1)S(1)}, u32[]{:S(2)}, u32[]{:S(2)}) collective-permute-start(bf16[64,576]{1,0:T(8,128)(2,1)S(1)} %get-tuple-element.30), channel_id=1, source_target_pairs={{0,96},{1,25},{8,104},{9,1},{16,112},{17,9},{24,120},{25,17},{32,0... | collective-permute-start | bytes 221192 | tf_op jit(solution)/shard_map/ppermute | solution.py:76
  5.1 0.8 collective-permute-start.1
  5.9 0.9 collective-permute-start
  6.8 0.4 collective-permute-done.2
  7.2 3.9 %collective-permute-done.1 = bf16[64,576]{1,0:T(8,128)(2,1)S(1)} collective-permute-done((bf16[64,576]{1,0:T(8,128)(2,1)S(1)}, bf16[64,576]{1,0:T(8,128)(2,1)S(1)}, u32[]{:S(2)}, u32[]{:S(2)}) %collective-permute-start.1) | collective-permute-done | bytes 73760 | tf_op jit(solution)/shard_map/ppermute | solution.py:76
  11.1 0.8 collective-permute-done
  12.0 0.1 pad_maximum_fusion.refs_0_
  12.0 4.1 %collective-permute-start.5 = (bf16[4,64,576]{2,1,0:T(8,128)(2,1)S(1)}, bf16[4,64,576]{2,1,0:T(8,128)(2,1)S(1)}, u32[]{:S(2)}, u32[]{:S(2)}) collective-permute-start(bf16[4,64,576]{2,1,0:T(8,128)(2,1)S(1)} %pad_maximum_fusion.refs_0_), channel_id=1, source_target_pairs={{0,24},{1,97},{8,0},{9,105},{16,8},{17,113},{24,16},{25,121},{32,5... | collective-permute-start | bytes 884744 | tf_op jit(solution)/shard_map/ppermute | solution.py:76
  16.1 1.3 %collective-permute-start.3 = (bf16[4,64,576]{2,1,0:T(8,128)(2,1)S(1)}, bf16[4,64,576]{2,1,0:T(8,128)(2,1)}, u32[]{:S(2)}, u32[]{:S(2)}) collective-permute-start(bf16[4,64,576]{2,1,0:T(8,128)(2,1)S(1)} %pad_maximum_fusion.refs_0_), channel_id=1, source_target_pairs={{0,8},{1,33},{8,16},{9,41},{16,24},{17,49},{24,0},{25,57},{32,40},... | collective-permute-start | bytes 884744 | tf_op jit(solution)/shard_map/ppermute | solution.py:76
  17.4 0.1 stack.38.info_ref
  17.5 0.1 pad_add_fusion.info_ref
  17.6 1.7 %route.1.route_ref = f32[8,1024]{1,0:T(8,128)S(1)} custom-call(s32[5]{0:T(128)S(1)} %stack.38.info_ref, s32[6,4,128]{2,1,0:T(4,128)S(1)} %bitcast.34, f32[6,4,128]{2,1,0:T(4,128)S(1)} %bitcast.35), custom_call_target="tpu_custom_call" | custom-call | flops 60000000 | bytes 60000 | tf_op jit(solution)/shard_map/route/pallas_call | solution.py:41
  19.3 1.0 entry.1.refs_5_
  20.3 4.0 %collective-permute-done.5.refs_3_ = bf16[4,64,576]{2,1,0:T(8,128)(2,1)S(1)} collective-permute-done((bf16[4,64,576]{2,1,0:T(8,128)(2,1)S(1)}, bf16[4,64,576]{2,1,0:T(8,128)(2,1)S(1)}, u32[]{:S(2)}, u32[]{:S(2)}) %collective-permute-start.5) | collective-permute-done | bytes 294944 | tf_op jit(solution)/shard_map/ppermute | solution.py:76
  24.2 0.7 collective-permute-done.4.refs_2_
  24.9 3.1 %collective-permute-done.3.refs_1_ = bf16[4,64,576]{2,1,0:T(8,128)(2,1)} collective-permute-done((bf16[4,64,576]{2,1,0:T(8,128)(2,1)S(1)}, bf16[4,64,576]{2,1,0:T(8,128)(2,1)}, u32[]{:S(2)}, u32[]{:S(2)}) %collective-permute-start.3) | collective-permute-done | bytes 294944 | tf_op jit(solution)/shard_map/ppermute | solution.py:76
  28.0 0.0 copy-start.1
  28.1 0.0 copy-start.2
  28.1 5.6 %attend.1 = (bf16[264,512]{1,0:T(8,128)(2,1)S(1)}, bf16[264,512]{1,0:T(8,128)(2,1)S(1)}, bf16[264,512]{1,0:T(8,128)(2,1)S(1)}, bf16[264,512]{1,0:T(8,128)(2,1)S(1)}) custom-call(s32[3]{0:T(128)S(1)} %pad_add_fusion.info_ref, bf16[4,64,576]{2,1,0:T(8,128)(2,1)S(1)} %pad_maximum_fusion.refs_0_, bf16[4,64,576]{2,1,0:T(8,128)(2,1)} %collective-permute-done.3.refs_1_, ...), custom_call_target="tpu_custom_call" | custom-call | flops 1800000000 | bytes 5000000 | tf_op jit(solution)/shard_map/attend/pallas_call | solution.py:41
  33.6 0.0 copy-start
  33.7 0.6 collective-permute-start.6
  34.3 0.8 collective-permute-start.7
  35.1 1.2 collective-permute-start.8
  36.3 3.9 %collective-permute-done.6.refs_1_ = bf16[264,512]{1,0:T(8,128)(2,1)S(1)} collective-permute-done((bf16[264,512]{1,0:T(8,128)(2,1)S(1)}, bf16[264,512]{1,0:T(8,128)(2,1)S(1)}, u32[]{:S(2)}, u32[]{:S(2)}) %collective-permute-start.6) | collective-permute-done | bytes 270368 | tf_op jit(solution)/shard_map/ppermute | solution.py:76
  40.2 2.2 %collective-permute-done.7.refs_2_ = bf16[264,512]{1,0:T(8,128)(2,1)S(1)} collective-permute-done((bf16[264,512]{1,0:T(8,128)(2,1)S(1)}, bf16[264,512]{1,0:T(8,128)(2,1)S(1)}, u32[]{:S(2)}, u32[]{:S(2)}) %collective-permute-start.7) | collective-permute-done | bytes 270368 | tf_op jit(solution)/shard_map/ppermute | solution.py:76
  42.3 2.8 %collective-permute-done.8.refs_3_ = bf16[264,512]{1,0:T(8,128)(2,1)S(1)} collective-permute-done((bf16[264,512]{1,0:T(8,128)(2,1)S(1)}, bf16[264,512]{1,0:T(8,128)(2,1)S(1)}, u32[]{:S(2)}, u32[]{:S(2)}) %collective-permute-start.8) | collective-permute-done | bytes 270368 | tf_op jit(solution)/shard_map/ppermute | solution.py:76
  45.1 0.3 merge.1
  45.5 1.0 collective-permute-start.9
  46.4 1.1 collective-permute-start.11
  47.6 2.3 %collective-permute-done.9.refs_1_ = bf16[72,512]{1,0:T(8,128)(2,1)S(1)} collective-permute-done((bf16[72,512]{1,0:T(8,128)(2,1)S(1)}, bf16[72,512]{1,0:T(8,128)(2,1)S(1)}, u32[]{:S(2)}, u32[]{:S(2)}) %collective-permute-start.9) | collective-permute-done | bytes 73760 | tf_op jit(solution)/shard_map/ppermute | solution.py:76
  49.9 2.5 %collective-permute-done.10.refs_2_ = bf16[72,512]{1,0:T(8,128)(2,1)S(1)} collective-permute-done((bf16[72,512]{1,0:T(8,128)(2,1)S(1)}, bf16[72,512]{1,0:T(8,128)(2,1)S(1)}, u32[]{:S(2)}, u32[]{:S(2)}) %collective-permute-start.10) | collective-permute-done | bytes 73760 | tf_op jit(solution)/shard_map/ppermute | solution.py:76
  52.3 0.7 collective-permute-done.11.refs_3_
  53.1 0.7 output.1
  53.8 11.4 %all_to_all.15.parts_ref = bf16[16,8,1024]{2,1,0:T(8,128)(2,1)S(1)} all-to-all(bf16[16,8,1024]{2,1,0:T(8,128)(2,1)S(1)} %bitcast.25), channel_id=1, replica_groups=mesh['x'=4,'z'=4,'y'=4,'core'=2] {'x','z'}, dimensions={0} | all-to-all | bytes 524288 | tf_op jit(solution)/shard_map/all_to_all | solution.py:558
  65.2 1.1 norm.1
  66.3 22.0 %all_to_all.16 = bf16[64,8,1024]{2,1,0:T(8,128)(2,1)S(1)} all-to-all(bf16[64,8,1024]{2,1,0:T(8,128)(2,1)S(1)} %get-tuple-element.45), channel_id=1, replica_groups=mesh['x'=4,'z'=4,'y'=4,'core'=2] {'y','z','x'}, dimensions={0} | all-to-all | bytes 2097152 | tf_op jit(solution)/shard_map/all_to_all | solution.py:572
  88.3 3.6 %pick.1 = (bf16[192,2048]{1,0:T(8,128)(2,1)S(1)}, bf16[64,2048]{1,0:T(8,128)(2,1)S(1)}, f32[192,128]{1,0:T(8,128)S(1)}, f32[8,256]{1,0:T(8,128)S(1)}) custom-call(s32[5]{0:T(128)S(1)} %stack.38.info_ref, bf16[176,2048]{1,0:T(8,128)(2,1)} %bitcast.42, bf16[176,2048]{1,0:T(8,128)(2,1)} %bitcast.43, bf16[176,2048]{1,0:T(8,128)(2,1)} %down_hbm.1, ...), custom_call_target="tpu_custom_call" | custom-call | flops 1000000000 | bytes 20000000 | tf_op jit(solution)/shard_map/pick/pallas_call | solution.py:41
  91.9 4.2 %experts.1 = (bf16[512,1024]{1,0:T(8,128)(2,1)S(1)}, bf16[256,2048]{1,0:T(8,128)(2,1)S(1)}, s32[8,256]{1,0:T(8,128)S(1)}) custom-call(s32[5]{0:T(128)S(1)} %stack.38.info_ref, bf16[192,2048]{1,0:T(8,128)(2,1)S(1)} %get-tuple-element.48.mine_x_ref, bf16[64,2048]{1,0:T(8,128)(2,1)S(1)} %get-tuple-element.49.own_ref, ...), custom_call_target="tpu_custom_call" | custom-call | flops 3000000000 | bytes 15000000 | tf_op jit(solution)/shard_map/experts/pallas_call | solution.py:41
  96.1 0.6 collective-permute-start.13
  96.7 0.7 put.1
  97.4 1.6 %collective-permute-done.13 = bf16[512,1024]{1,0:T(8,128)(2,1)S(1)} collective-permute-done((bf16[512,1024]{1,0:T(8,128)(2,1)S(1)}, bf16[512,1024]{1,0:T(8,128)(2,1)S(1)}, u32[]{:S(2)}, u32[]{:S(2)}) %collective-permute-start.13) | collective-permute-done | bytes 1048608 | tf_op jit(solution)/shard_map/ppermute | solution.py:609
  99.0 0.4 fusion
  99.4 23.8 %all_to_all.17 = bf16[64,8,1024]{2,1,0:T(8,128)(2,1)S(1)} all-to-all(bf16[64,8,1024]{2,1,0:T(8,128)(2,1)S(1)} %fusion), channel_id=1, replica_groups=mesh['x'=4,'z'=4,'y'=4,'core'=2] {'y','z','x'}, dimensions={0} | all-to-all | bytes 2097152 | tf_op jit(solution)/shard_map/all_to_all | solution.py:615
  123.2 0.2 convert_reduce_fusion
  123.4 0.7 reshape.27
  (27 shorter events, 0.1 us)
Async XLA Ops:
  0.0 17.5 %copy-start.13 = (s32[2]{0:T(128)S(1)}, s32[2]{0:T(128)}, u32[]{:S(2)}) copy-start(s32[2]{0:T(128)} %counts_hbm.1) | copy-start | bytes 28
  0.0 17.6 %copy-start.9 = (s32[4,128,6]{1,0,2:T(4,128)S(1)}, s32[4,128,6]{1,0,2:T(4,128)}, u32[]{:S(2)}) copy-start(s32[4,128,6]{1,0,2:T(4,128)} %param.41) | copy-start | bytes 36868
  0.0 17.6 %copy-start.10 = (f32[4,128,6]{1,0,2:T(4,128)S(1)}, f32[4,128,6]{1,0,2:T(4,128)}, u32[]{:S(2)}) copy-start(f32[4,128,6]{1,0,2:T(4,128)} %param.42) | copy-start | bytes 36868
  0.0 19.3 %copy-start.4 = (f32[512]{0:T(512)S(1)}, f32[512]{0:T(512)}, u32[]{:S(2)}) copy-start(f32[512]{0:T(512)} %param.26) | copy-start | bytes 6148
  2.2 25.9 %copy-start.11 = (s32[2,8,64]{2,1,0:T(8,128)S(1)}, s32[2,8,64]{2,1,0:T(8,128)}, u32[]{:S(2)}) copy-start(s32[2,8,64]{2,1,0:T(8,128)} %refs_7_.1) | copy-start | bytes 12292
  2.2 25.9 %copy-start.12 = (s32[4,2,8]{2,1,0:T(2,128)S(1)}, s32[4,2,8]{2,1,0:T(2,128)}, u32[]{:S(2)}) copy-start(s32[4,2,8]{2,1,0:T(2,128)} %refs_6_.1) | copy-start | bytes 772
  2.2 5.0 %collective-permute-start.2 = (bf16[64,576]{1,0:T(8,128)(2,1)S(1)}, bf16[64,576]{1,0:T(8,128)(2,1)S(1)}, u32[]{:S(2)}, u32[]{:S(2)}) collective-permute-start(bf16[64,576]{1,0:T(8,128)(2,1)S(1)} %get-tuple-element.30), channel_id=1, source_target_pairs={{0,96},{1,25},{8,104},{9,1},{16,112},{17,9},{24,120},{25,17},{32,0... | collective-permute-start | bytes 221192 | tf_op jit(solution)/shard_map/ppermute | solution.py:76
  5.1 6.0 %collective-permute-start.1 = (bf16[64,576]{1,0:T(8,128)(2,1)S(1)}, bf16[64,576]{1,0:T(8,128)(2,1)S(1)}, u32[]{:S(2)}, u32[]{:S(2)}) collective-permute-start(bf16[64,576]{1,0:T(8,128)(2,1)S(1)} %get-tuple-element.30), channel_id=1, source_target_pairs={{0,64},{1,17},{8,72},{9,25},{16,80},{17,1},{24,88},{25,9},{32,96},... | collective-permute-start | bytes 221192 | tf_op jit(solution)/shard_map/ppermute | solution.py:76
  5.9 6.0 %collective-permute-start = (bf16[64,576]{1,0:T(8,128)(2,1)S(1)}, bf16[64,576]{1,0:T(8,128)(2,1)S(1)}, u32[]{:S(2)}, u32[]{:S(2)}) collective-permute-start(bf16[64,576]{1,0:T(8,128)(2,1)S(1)} %get-tuple-element.30), channel_id=1, source_target_pairs={{0,32},{1,9},{8,40},{9,17},{16,48},{17,25},{24,56},{25,1},{32,64},... | collective-permute-start | bytes 221192 | tf_op jit(solution)/shard_map/ppermute | solution.py:76
  12.0 12.2 %collective-permute-start.5 = (bf16[4,64,576]{2,1,0:T(8,128)(2,1)S(1)}, bf16[4,64,576]{2,1,0:T(8,128)(2,1)S(1)}, u32[]{:S(2)}, u32[]{:S(2)}) collective-permute-start(bf16[4,64,576]{2,1,0:T(8,128)(2,1)S(1)} %pad_maximum_fusion.refs_0_), channel_id=1, source_target_pairs={{0,24},{1,97},{8,0},{9,105},{16,8},{17,113},{24,16},{25,121},{32,5... | collective-permute-start | bytes 884744 | tf_op jit(solution)/shard_map/ppermute | solution.py:76
  16.1 8.8 %collective-permute-start.4 = (bf16[4,64,576]{2,1,0:T(8,128)(2,1)S(1)}, bf16[4,64,576]{2,1,0:T(8,128)(2,1)}, u32[]{:S(2)}, u32[]{:S(2)}) collective-permute-start(bf16[4,64,576]{2,1,0:T(8,128)(2,1)S(1)} %pad_maximum_fusion.refs_0_), channel_id=1, source_target_pairs={{0,16},{1,65},{8,24},{9,73},{16,0},{17,81},{24,8},{25,89},{32,48},... | collective-permute-start | bytes 884744 | tf_op jit(solution)/shard_map/ppermute | solution.py:76
  16.1 11.9 %collective-permute-start.3 = (bf16[4,64,576]{2,1,0:T(8,128)(2,1)S(1)}, bf16[4,64,576]{2,1,0:T(8,128)(2,1)}, u32[]{:S(2)}, u32[]{:S(2)}) collective-permute-start(bf16[4,64,576]{2,1,0:T(8,128)(2,1)S(1)} %pad_maximum_fusion.refs_0_), channel_id=1, source_target_pairs={{0,8},{1,33},{8,16},{9,41},{16,24},{17,49},{24,0},{25,57},{32,40},... | collective-permute-start | bytes 884744 | tf_op jit(solution)/shard_map/ppermute | solution.py:76
  17.5 10.6 %copy-start.8 = (bf16[2,6,128,576]{2,3,1,0:T(8,128)(2,1)S(1)}, bf16[2,6,128,576]{2,3,1,0:T(8,128)(2,1)}, u32[]{:S(2)}) copy-start(bf16[2,6,128,576]{2,3,1,0:T(8,128)(2,1)} %param.37) | copy-start | bytes 5308420
  28.0 25.0 %copy-start.1 = (bf16[128,2048]{1,0:T(8,128)(2,1)S(1)}, bf16[128,2048]{1,0:T(8,128)(2,1)}, u32[]{:S(2)}) copy-start(bf16[128,2048]{1,0:T(8,128)(2,1)} %refs_5_.1) | copy-start | bytes 1572868
  28.1 25.0 %copy-start.2 = (bf16[1,512,128]{2,1,0:T(8,128)(2,1)S(1)}, bf16[1,512,128]{2,1,0:T(8,128)(2,1)}, u32[]{:S(2)}) copy-start(bf16[1,512,128]{2,1,0:T(8,128)(2,1)} %refs_4_.1) | copy-start | bytes 393220
  33.6 31.5 %copy-start = (bf16[4,16,2048]{2,1,0:T(8,128)(2,1)S(1)}, bf16[4,16,2048]{2,1,0:T(8,128)(2,1)}, u32[]{:S(2)}) copy-start(bf16[4,16,2048]{2,1,0:T(8,128)(2,1)} %embeds_ref.1) | copy-start | bytes 786436
  33.6 31.5 %copy-start.3 = (f32[2048]{0:T(1024)S(1)}, f32[2048]{0:T(1024)}, u32[]{:S(2)}) copy-start(f32[2048]{0:T(1024)} %param.30) | copy-start | bytes 24580
  33.7 6.5 %collective-permute-start.6 = (bf16[264,512]{1,0:T(8,128)(2,1)S(1)}, bf16[264,512]{1,0:T(8,128)(2,1)S(1)}, u32[]{:S(2)}, u32[]{:S(2)}) collective-permute-start(bf16[264,512]{1,0:T(8,128)(2,1)S(1)} %get-tuple-element.38), channel_id=1, source_target_pairs={{0,96},{1,25},{8,104},{9,1},{16,112},{17,9},{24,120},{25,17},{32,0... | collective-permute-start | bytes 811016 | tf_op jit(solution)/shard_map/ppermute | solution.py:76
  34.3 8.1 %collective-permute-start.7 = (bf16[264,512]{1,0:T(8,128)(2,1)S(1)}, bf16[264,512]{1,0:T(8,128)(2,1)S(1)}, u32[]{:S(2)}, u32[]{:S(2)}) collective-permute-start(bf16[264,512]{1,0:T(8,128)(2,1)S(1)} %get-tuple-element.39), channel_id=1, source_target_pairs={{0,64},{1,17},{8,72},{9,25},{16,80},{17,1},{24,88},{25,9},{32,96},... | collective-permute-start | bytes 811016 | tf_op jit(solution)/shard_map/ppermute | solution.py:76
  35.1 10.1 %collective-permute-start.8 = (bf16[264,512]{1,0:T(8,128)(2,1)S(1)}, bf16[264,512]{1,0:T(8,128)(2,1)S(1)}, u32[]{:S(2)}, u32[]{:S(2)}) collective-permute-start(bf16[264,512]{1,0:T(8,128)(2,1)S(1)} %get-tuple-element.40), channel_id=1, source_target_pairs={{0,32},{1,9},{8,40},{9,17},{16,48},{17,25},{24,56},{25,1},{32,64},... | collective-permute-start | bytes 811016 | tf_op jit(solution)/shard_map/ppermute | solution.py:76
  45.1 46.8 %copy-start.7 = (bf16[2,352,2048]{2,1,0:T(8,128)(2,1)S(1)}, bf16[2,352,2048]{2,1,0:T(8,128)(2,1)}, u32[]{:S(2)}) copy-start(bf16[2,352,2048]{2,1,0:T(8,128)(2,1)} %down_ref.1) | copy-start | bytes 8650756
  45.5 4.4 %collective-permute-start.9 = (bf16[72,512]{1,0:T(8,128)(2,1)S(1)}, bf16[72,512]{1,0:T(8,128)(2,1)S(1)}, u32[]{:S(2)}, u32[]{:S(2)}) collective-permute-start(bf16[72,512]{1,0:T(8,128)(2,1)S(1)} %get-tuple-element.42), channel_id=1, source_target_pairs={{0,24},{1,97},{8,0},{9,105},{16,8},{17,113},{24,16},{25,121},{32,5... | collective-permute-start | bytes 221192 | tf_op jit(solution)/shard_map/ppermute | solution.py:76
  46.4 5.9 %collective-permute-start.10 = (bf16[72,512]{1,0:T(8,128)(2,1)S(1)}, bf16[72,512]{1,0:T(8,128)(2,1)S(1)}, u32[]{:S(2)}, u32[]{:S(2)}) collective-permute-start(bf16[72,512]{1,0:T(8,128)(2,1)S(1)} %get-tuple-element.43), channel_id=1, source_target_pairs={{0,16},{1,65},{8,24},{9,73},{16,0},{17,81},{24,8},{25,89},{32,48},... | collective-permute-start | bytes 221192 | tf_op jit(solution)/shard_map/ppermute | solution.py:76
  46.4 6.6 %collective-permute-start.11 = (bf16[72,512]{1,0:T(8,128)(2,1)S(1)}, bf16[72,512]{1,0:T(8,128)(2,1)S(1)}, u32[]{:S(2)}, u32[]{:S(2)}) collective-permute-start(bf16[72,512]{1,0:T(8,128)(2,1)S(1)} %get-tuple-element.44), channel_id=1, source_target_pairs={{0,8},{1,33},{8,16},{9,41},{16,24},{17,49},{24,0},{25,57},{32,40},... | collective-permute-start | bytes 221192 | tf_op jit(solution)/shard_map/ppermute | solution.py:76
  66.2 25.7 %copy-start.6 = (bf16[2,2048,352]{1,2,0:T(8,128)(2,1)S(1)}, bf16[2,2048,352]{1,2,0:T(8,128)(2,1)}, u32[]{:S(2)}) copy-start(bf16[2,2048,352]{1,2,0:T(8,128)(2,1)} %param.35) | copy-start | bytes 8650756
  88.3 3.7 %copy-start.5 = (bf16[2,2048,352]{1,2,0:T(8,128)(2,1)S(1)}, bf16[2,2048,352]{1,2,0:T(8,128)(2,1)}, u32[]{:S(2)}) copy-start(bf16[2,2048,352]{1,2,0:T(8,128)(2,1)} %param.34) | copy-start | bytes 8650756
  88.3 3.6 %collective-permute-start.12 = (bf16[512,1024]{1,0:T(8,128)(2,1)S(1)}, bf16[512,1024]{1,0:T(8,128)(2,1)S(1)}, u32[]{:S(2)}, u32[]{:S(2)}) collective-permute-start(bf16[512,1024]{1,0:T(8,128)(2,1)S(1)} %bitcast.26), channel_id=1, source_target_pairs={{0,1},{1,0},{2,3},{3,2},{4,5},{5,4},{6,7},{7,6},{8,9},{9,8},{10,11... | collective-permute-start | bytes 3145736 | tf_op jit(solution)/shard_map/ppermute | solution.py:573
  96.1 2.9 %collective-permute-start.13 = (bf16[512,1024]{1,0:T(8,128)(2,1)S(1)}, bf16[512,1024]{1,0:T(8,128)(2,1)S(1)}, u32[]{:S(2)}, u32[]{:S(2)}) collective-permute-start(bf16[512,1024]{1,0:T(8,128)(2,1)S(1)} %get-tuple-element.54), channel_id=1, source_target_pairs={{0,1},{1,0},{2,3},{3,2},{4,5},{5,4},{6,7},{7,6},{8,9},{9,8},{10,11... | collective-permute-start | bytes 3145736 | tf_op jit(solution)/shard_map/ppermute | solution.py:609

commit v5 on v4

--- a/solution.py
+++ b/solution.py
@@ -124,8 +124,8 @@
     rope = queries[:, 128:]
     cosine, sine = rope_parts(cos_ref, 64)
     rope = (rope.astype(f32) * cosine + turned(rope) * sine).astype(bf16)
-    result_ref[:, :512] = latent
-    result_ref[:, 512:] = rope
+    result_ref[:64, :] = latent
+    result_ref[64:, :] = jnp.concatenate([rope[8 * k : 8 * k + 8] for k in range(8)], axis=1)
     copies[6].wait()
 
 
@@ -168,8 +168,7 @@
     q_refs, out_refs = refs[:4], refs[8:12]
     cache_ref, entry_ref, parent_ref, table_ref = refs[4:8]
     sum_ref = refs[12]
-    near, rows_all, width = q_refs[0].shape
-    heads = 4 * near
+    near, heads, rows_all, width = 4, 16, 64, entry_ref.shape[1]
     groups, beams, _ = table_ref.shape
     rows = rows_all // groups
     pool, _, block_len = cache_ref.shape[1:]
@@ -206,7 +205,10 @@
         recent_bias = jnp.where((seen > 0.5) & (blk == 0), 0.0, NEG)
 
         part = slice(g * rows, (g + 1) * rows)
-        q = jnp.concatenate([ref[:, part, :] for ref in q_refs], axis=0).reshape(heads * rows, width)
+        lat_part = jnp.concatenate([ref[:, part, :] for ref in q_refs], axis=0)
+        rope_tile = jnp.concatenate([ref[:, rows_all:, :] for ref in q_refs], axis=0)
+        rope_part = [rope_tile[:, :, 64 * k : 64 * k + 64] for k in range(steps * g, steps * g + steps)]
+        q = jnp.concatenate([lat_part, jnp.concatenate(rope_part, axis=1)], axis=2).reshape(heads * rows, width)
         keys = jnp.concatenate([cache_ref[g, p] for p in range(pool)], axis=1)
         entry = entry_ref[part]
         scores = jnp.dot(q, keys, preferred_element_type=f32)
@@ -223,7 +225,7 @@
         recent = recent.astype(bf16).reshape(heads * rows, rows)
         lat = lax.dot_general(weights, keys[:latent], LAST, preferred_element_type=f32)
         lat = lat + jnp.dot(recent, entry[:, :latent], preferred_element_type=f32)
-        lat = (lat.reshape(heads, rows, latent) / total).astype(bf16)
+        lat = (lat.reshape(heads, rows, latent) * (1.0 / total)).astype(bf16)
         lse = jnp.where(top > 0.1 * NEG, top + jnp.log(total), NEG)
         lse = jnp.broadcast_to(lse, (heads, rows, 128))
         for s in range(near):
@@ -340,8 +342,7 @@
 
 def line_places(line, core, lines):
     row = line_row(line, core)
-    chip = 16 * ((row >> 1) & 3) + 4 * ((row >> 3) & 3) + (row >> 5)
-    return ((row & 1) ^ core) * (lines // 2) + chip * 4 + ((line >> 1) & 3)
+    return ((row & 1) ^ core) * (lines // 2) + (row >> 1) * 4 + ((line >> 1) & 3)
 
 
 def picked(source_ref, hit, line, place, weights):
@@ -488,7 +489,7 @@
     query, normed, cosines, latent_weights = kernel_call(
         query_kernel,
         "query",
-        [((rows_all, entry_width), bf16), ((rows_all, width), bf16), ((8, 128), f32), ((entry_width, width), bf16)],
+        [((rows_all + 8, latent), bf16), ((rows_all, width), bf16), ((8, 128), f32), ((entry_width, width), bf16)],
         [pltpu.VMEM(a.shape, a.dtype) for a in sources[:-2]]
         + [pltpu.SMEM(block_counts.shape, jnp.int32), pltpu.SemaphoreType.DMA((len(sources),))],
         (60_000_000, 20_000_000, 0),
@@ -612,7 +613,7 @@
     )
     own_out = own_out.astype(f32) + arrived.astype(f32)
     own_out = own_out.astype(bf16).reshape(chips, 2 * steps, half)
-    result = jnp.sum(lax.all_to_all(own_out, ("y", "z", "x"), 0, 0).astype(f32), axis=0)
+    result = jnp.sum(lax.all_to_all(own_out, ("x", "z", "y"), 0, 0).astype(f32), axis=0)
     return result.reshape(steps, 1, width)
 
 

time: 124 us -> 123 us (level)
  waiting for transfers between devices: 28.9 us -> 27.1 us
    ppermute x12, waiting for transfers between devices: 27.3 us -> 25.5 us  [shifted(): return lax.ppermute(value, ('x', 'z', 'core'), pairs)]
  transfers between devices with their start and end apart: 14 -> 14, of which waited for: 13 -> 13; matrix products, arithmetic and copies ran while one was open for 0% -> 1% of each run, Pallas kernels for 6% -> 6%
where the time goes in v5:
time: 123 us; the launch traced here: 122 us
  blocking collectives  56.9 us (46%)
  waiting for transfers between devices  27.1 us (22%)
  Pallas kernels  20.6 us (17%)
  starting transfers between devices  15.3 us (12%)
  other arithmetic  1.47 us (1%)
    ppermute x12, waiting for transfers between devices, shifted(): return lax.ppermute(value, ('x', 'z', 'core'), pairs)  25.5 us
    all_to_all x1, blocking collectives, per_device(): lax.all_to_all(own_out, ('x', 'z', 'y'), 0, 0).astype(f32)  23.4 us
    all_to_all x1, blocking collectives, per_device(): mine = lax.all_to_all(spread, ('y', 'z', 'x'), 0, 0).reshape(lines, half)  22 us
    pallas_call x10, Pallas kernels, kernel_call(): pl.pallas_call(body, out_shape=[jax.ShapeDtypeStruct(shape, dtype) for sh...  20.6 us
    ppermute x12, starting transfers between devices, shifted(): return lax.ppermute(value, ('x', 'z', 'core'), pairs)  14.8 us
    all_to_all x1, blocking collectives, per_device(): lax.all_to_all(attn_part.reshape(row_dev, 2 * steps, half), BLK, 0, 0)  11.5 us
  transfers between devices with their start and end apart: 14, of which 13 were waited for; matrix products, arithmetic and copies ran while one was open for 1% of the time, Pallas kernels for 6%

profile of v5, /device:TPU:0, one launch (start us, length us, event | category | flops | bytes accessed | tf_op | source)
XLA Modules:
  0.0 122.3 jit_solution(10824093544445010050)
XLA Ops:
  0.0 2.2 %query.1 = (bf16[72,512]{1,0:T(8,128)(2,1)S(1)}, bf16[64,2048]{1,0:T(8,128)(2,1)S(1)}, f32[8,128]{1,0:T(8,128)S(1)}, bf16[576,2048]{1,0:T(8,128)(2,1)S(1)}) custom-call(bf16[4,16,2048]{2,1,0:T(8,128)(2,1)} %embeds_ref.1, bf16[192,2048]{1,0:T(8,128)(2,1)} %bitcast.37, bf16[1,128,512]{2,1,0:T(8,128)(2,1)} %key_up_hbm.1, f32[1,2048]{1,0:T(1,128)} %bitcast.41, ...), custom_call_target="tpu_custom_call" | custom-call | flops 60000000 | bytes 20000000 | tf_op jit(solution)/shard_map/query/pallas_call | solution.py:41
  2.2 0.0 copy-start.11
  2.2 0.0 copy-start.12
  2.2 2.9 %collective-permute-start.2 = (bf16[72,512]{1,0:T(8,128)(2,1)S(1)}, bf16[72,512]{1,0:T(8,128)(2,1)S(1)}, u32[]{:S(2)}, u32[]{:S(2)}) collective-permute-start(bf16[72,512]{1,0:T(8,128)(2,1)S(1)} %get-tuple-element.30), channel_id=1, source_target_pairs={{0,96},{1,25},{8,104},{9,1},{16,112},{17,9},{24,120},{25,17},{32,0... | collective-permute-start | bytes 221192 | tf_op jit(solution)/shard_map/ppermute | solution.py:76
  5.1 0.8 collective-permute-start.1
  5.9 0.9 collective-permute-start
  6.8 0.3 collective-permute-done.2
  7.1 3.9 %collective-permute-done.1 = bf16[72,512]{1,0:T(8,128)(2,1)S(1)} collective-permute-done((bf16[72,512]{1,0:T(8,128)(2,1)S(1)}, bf16[72,512]{1,0:T(8,128)(2,1)S(1)}, u32[]{:S(2)}, u32[]{:S(2)}) %collective-permute-start.1) | collective-permute-done | bytes 73760 | tf_op jit(solution)/shard_map/ppermute | solution.py:76
  11.0 0.8 collective-permute-done
  11.8 4.1 %collective-permute-start.5 = (bf16[4,72,512]{2,1,0:T(8,128)(2,1)S(1)}, bf16[4,72,512]{2,1,0:T(8,128)(2,1)S(1)}, u32[]{:S(2)}, u32[]{:S(2)}) collective-permute-start(bf16[4,72,512]{2,1,0:T(8,128)(2,1)S(1)} %pad_maximum_fusion.refs_0_), channel_id=1, source_target_pairs={{0,24},{1,97},{8,0},{9,105},{16,8},{17,113},{24,16},{25,121},{32,5... | collective-permute-start | bytes 884744 | tf_op jit(solution)/shard_map/ppermute | solution.py:76
  15.9 1.3 %collective-permute-start.3 = (bf16[4,72,512]{2,1,0:T(8,128)(2,1)S(1)}, bf16[4,72,512]{2,1,0:T(8,128)(2,1)}, u32[]{:S(2)}, u32[]{:S(2)}) collective-permute-start(bf16[4,72,512]{2,1,0:T(8,128)(2,1)S(1)} %pad_maximum_fusion.refs_0_), channel_id=1, source_target_pairs={{0,8},{1,33},{8,16},{9,41},{16,24},{17,49},{24,0},{25,57},{32,40},... | collective-permute-start | bytes 884744 | tf_op jit(solution)/shard_map/ppermute | solution.py:76
  17.2 0.1 stack.38.info_ref
  17.3 0.9 pad_add_fusion.info_ref
  18.1 1.7 %route.1.route_ref = f32[8,1024]{1,0:T(8,128)S(1)} custom-call(s32[5]{0:T(128)S(1)} %stack.38.info_ref, s32[6,4,128]{2,1,0:T(4,128)S(1)} %bitcast.34, f32[6,4,128]{2,1,0:T(4,128)S(1)} %bitcast.35), custom_call_target="tpu_custom_call" | custom-call | flops 60000000 | bytes 60000 | tf_op jit(solution)/shard_map/route/pallas_call | solution.py:41
  19.8 1.0 entry.1.refs_5_
  20.8 2.5 %collective-permute-done.5.refs_3_ = bf16[4,72,512]{2,1,0:T(8,128)(2,1)S(1)} collective-permute-done((bf16[4,72,512]{2,1,0:T(8,128)(2,1)S(1)}, bf16[4,72,512]{2,1,0:T(8,128)(2,1)S(1)}, u32[]{:S(2)}, u32[]{:S(2)}) %collective-permute-start.5) | collective-permute-done | bytes 294944 | tf_op jit(solution)/shard_map/ppermute | solution.py:76
  23.3 0.9 collective-permute-done.4.refs_2_
  24.2 2.9 %collective-permute-done.3.refs_1_ = bf16[4,72,512]{2,1,0:T(8,128)(2,1)} collective-permute-done((bf16[4,72,512]{2,1,0:T(8,128)(2,1)S(1)}, bf16[4,72,512]{2,1,0:T(8,128)(2,1)}, u32[]{:S(2)}, u32[]{:S(2)}) %collective-permute-start.3) | collective-permute-done | bytes 294944 | tf_op jit(solution)/shard_map/ppermute | solution.py:76
  27.1 0.0 copy-start.1
  27.1 0.0 copy-start.2
  27.2 5.4 %attend.1 = (bf16[264,512]{1,0:T(8,128)(2,1)S(1)}, bf16[264,512]{1,0:T(8,128)(2,1)S(1)}, bf16[264,512]{1,0:T(8,128)(2,1)S(1)}, bf16[264,512]{1,0:T(8,128)(2,1)S(1)}) custom-call(s32[3]{0:T(128)S(1)} %pad_add_fusion.info_ref, bf16[4,72,512]{2,1,0:T(8,128)(2,1)S(1)} %pad_maximum_fusion.refs_0_, bf16[4,72,512]{2,1,0:T(8,128)(2,1)} %collective-permute-done.3.refs_1_, ...), custom_call_target="tpu_custom_call" | custom-call | flops 1800000000 | bytes 5000000 | tf_op jit(solution)/shard_map/attend/pallas_call | solution.py:41
  32.6 0.0 copy-start
  32.6 0.0 copy-start.3
  32.6 0.6 collective-permute-start.6
  33.2 0.9 collective-permute-start.7
  34.1 1.2 collective-permute-start.8
  35.3 3.8 %collective-permute-done.6.refs_1_ = bf16[264,512]{1,0:T(8,128)(2,1)S(1)} collective-permute-done((bf16[264,512]{1,0:T(8,128)(2,1)S(1)}, bf16[264,512]{1,0:T(8,128)(2,1)S(1)}, u32[]{:S(2)}, u32[]{:S(2)}) %collective-permute-start.6) | collective-permute-done | bytes 270368 | tf_op jit(solution)/shard_map/ppermute | solution.py:76
  39.1 2.2 %collective-permute-done.7.refs_2_ = bf16[264,512]{1,0:T(8,128)(2,1)S(1)} collective-permute-done((bf16[264,512]{1,0:T(8,128)(2,1)S(1)}, bf16[264,512]{1,0:T(8,128)(2,1)S(1)}, u32[]{:S(2)}, u32[]{:S(2)}) %collective-permute-start.7) | collective-permute-done | bytes 270368 | tf_op jit(solution)/shard_map/ppermute | solution.py:76
  41.3 2.8 %collective-permute-done.8.refs_3_ = bf16[264,512]{1,0:T(8,128)(2,1)S(1)} collective-permute-done((bf16[264,512]{1,0:T(8,128)(2,1)S(1)}, bf16[264,512]{1,0:T(8,128)(2,1)S(1)}, u32[]{:S(2)}, u32[]{:S(2)}) %collective-permute-start.8) | collective-permute-done | bytes 270368 | tf_op jit(solution)/shard_map/ppermute | solution.py:76
  44.1 0.3 merge.1
  44.4 1.0 collective-permute-start.9
  45.4 1.1 collective-permute-start.11
  46.5 2.3 %collective-permute-done.9.refs_1_ = bf16[72,512]{1,0:T(8,128)(2,1)S(1)} collective-permute-done((bf16[72,512]{1,0:T(8,128)(2,1)S(1)}, bf16[72,512]{1,0:T(8,128)(2,1)S(1)}, u32[]{:S(2)}, u32[]{:S(2)}) %collective-permute-start.9) | collective-permute-done | bytes 73760 | tf_op jit(solution)/shard_map/ppermute | solution.py:76
  48.8 2.5 %collective-permute-done.10.refs_2_ = bf16[72,512]{1,0:T(8,128)(2,1)S(1)} collective-permute-done((bf16[72,512]{1,0:T(8,128)(2,1)S(1)}, bf16[72,512]{1,0:T(8,128)(2,1)S(1)}, u32[]{:S(2)}, u32[]{:S(2)}) %collective-permute-start.10) | collective-permute-done | bytes 73760 | tf_op jit(solution)/shard_map/ppermute | solution.py:76
  51.3 0.7 collective-permute-done.11.refs_3_
  52.0 0.7 output.1
  52.7 11.5 %all_to_all.15.parts_ref = bf16[16,8,1024]{2,1,0:T(8,128)(2,1)S(1)} all-to-all(bf16[16,8,1024]{2,1,0:T(8,128)(2,1)S(1)} %bitcast.25), channel_id=1, replica_groups=mesh['x'=4,'z'=4,'y'=4,'core'=2] {'x','z'}, dimensions={0} | all-to-all | bytes 524288 | tf_op jit(solution)/shard_map/all_to_all | solution.py:559
  64.2 1.1 norm.1
  65.3 22.0 %all_to_all.16 = bf16[64,8,1024]{2,1,0:T(8,128)(2,1)S(1)} all-to-all(bf16[64,8,1024]{2,1,0:T(8,128)(2,1)S(1)} %get-tuple-element.45), channel_id=1, replica_groups=mesh['x'=4,'z'=4,'y'=4,'core'=2] {'y','z','x'}, dimensions={0} | all-to-all | bytes 2097152 | tf_op jit(solution)/shard_map/all_to_all | solution.py:573
  87.3 3.4 %pick.1 = (bf16[192,2048]{1,0:T(8,128)(2,1)S(1)}, bf16[64,2048]{1,0:T(8,128)(2,1)S(1)}, f32[192,128]{1,0:T(8,128)S(1)}, f32[8,256]{1,0:T(8,128)S(1)}) custom-call(s32[5]{0:T(128)S(1)} %stack.38.info_ref, bf16[176,2048]{1,0:T(8,128)(2,1)} %bitcast.42, bf16[176,2048]{1,0:T(8,128)(2,1)} %bitcast.43, bf16[176,2048]{1,0:T(8,128)(2,1)} %down_hbm.1, ...), custom_call_target="tpu_custom_call" | custom-call | flops 1000000000 | bytes 20000000 | tf_op jit(solution)/shard_map/pick/pallas_call | solution.py:41
  90.7 4.2 %experts.1 = (bf16[512,1024]{1,0:T(8,128)(2,1)S(1)}, bf16[256,2048]{1,0:T(8,128)(2,1)S(1)}, s32[8,256]{1,0:T(8,128)S(1)}) custom-call(s32[5]{0:T(128)S(1)} %stack.38.info_ref, bf16[192,2048]{1,0:T(8,128)(2,1)S(1)} %get-tuple-element.48.mine_x_ref, bf16[64,2048]{1,0:T(8,128)(2,1)S(1)} %get-tuple-element.49.own_ref, ...), custom_call_target="tpu_custom_call" | custom-call | flops 3000000000 | bytes 15000000 | tf_op jit(solution)/shard_map/experts/pallas_call | solution.py:41
  94.9 0.5 collective-permute-start.13
  95.4 0.7 put.1
  96.1 1.6 %collective-permute-done.13 = bf16[512,1024]{1,0:T(8,128)(2,1)S(1)} collective-permute-done((bf16[512,1024]{1,0:T(8,128)(2,1)S(1)}, bf16[512,1024]{1,0:T(8,128)(2,1)S(1)}, u32[]{:S(2)}, u32[]{:S(2)}) %collective-permute-start.13) | collective-permute-done | bytes 1048608 | tf_op jit(solution)/shard_map/ppermute | solution.py:610
  97.7 0.4 fusion
  98.1 23.4 %all_to_all.17 = bf16[64,8,1024]{2,1,0:T(8,128)(2,1)S(1)} all-to-all(bf16[64,8,1024]{2,1,0:T(8,128)(2,1)S(1)} %fusion), channel_id=1, replica_groups=mesh['x'=4,'z'=4,'y'=4,'core'=2] {'x','z','y'}, dimensions={0} | all-to-all | bytes 2097152 | tf_op jit(solution)/shard_map/all_to_all | solution.py:616
  121.5 0.2 convert_reduce_fusion
  121.6 0.7 reshape.27
  (25 shorter events, 0.1 us)
Async XLA Ops:
  0.0 18.1 %copy-start.9 = (s32[4,128,6]{1,0,2:T(4,128)S(1)}, s32[4,128,6]{1,0,2:T(4,128)}, u32[]{:S(2)}) copy-start(s32[4,128,6]{1,0,2:T(4,128)} %param.41) | copy-start | bytes 36868
  0.0 18.1 %copy-start.10 = (f32[4,128,6]{1,0,2:T(4,128)S(1)}, f32[4,128,6]{1,0,2:T(4,128)}, u32[]{:S(2)}) copy-start(f32[4,128,6]{1,0,2:T(4,128)} %param.42) | copy-start | bytes 36868
  0.0 19.8 %copy-start.4 = (f32[512]{0:T(512)S(1)}, f32[512]{0:T(512)}, u32[]{:S(2)}) copy-start(f32[512]{0:T(512)} %param.26) | copy-start | bytes 6148
  2.2 24.9 %copy-start.11 = (s32[2,8,64]{2,1,0:T(8,128)S(1)}, s32[2,8,64]{2,1,0:T(8,128)}, u32[]{:S(2)}) copy-start(s32[2,8,64]{2,1,0:T(8,128)} %refs_7_.1) | copy-start | bytes 12292
  2.2 24.9 %copy-start.12 = (s32[4,2,8]{2,1,0:T(2,128)S(1)}, s32[4,2,8]{2,1,0:T(2,128)}, u32[]{:S(2)}) copy-start(s32[4,2,8]{2,1,0:T(2,128)} %refs_6_.1) | copy-start | bytes 772
  2.2 4.9 %collective-permute-start.2 = (bf16[72,512]{1,0:T(8,128)(2,1)S(1)}, bf16[72,512]{1,0:T(8,128)(2,1)S(1)}, u32[]{:S(2)}, u32[]{:S(2)}) collective-permute-start(bf16[72,512]{1,0:T(8,128)(2,1)S(1)} %get-tuple-element.30), channel_id=1, source_target_pairs={{0,96},{1,25},{8,104},{9,1},{16,112},{17,9},{24,120},{25,17},{32,0... | collective-permute-start | bytes 221192 | tf_op jit(solution)/shard_map/ppermute | solution.py:76
  5.1 5.9 %collective-permute-start.1 = (bf16[72,512]{1,0:T(8,128)(2,1)S(1)}, bf16[72,512]{1,0:T(8,128)(2,1)S(1)}, u32[]{:S(2)}, u32[]{:S(2)}) collective-permute-start(bf16[72,512]{1,0:T(8,128)(2,1)S(1)} %get-tuple-element.30), channel_id=1, source_target_pairs={{0,64},{1,17},{8,72},{9,25},{16,80},{17,1},{24,88},{25,9},{32,96},... | collective-permute-start | bytes 221192 | tf_op jit(solution)/shard_map/ppermute | solution.py:76
  5.9 5.8 %collective-permute-start = (bf16[72,512]{1,0:T(8,128)(2,1)S(1)}, bf16[72,512]{1,0:T(8,128)(2,1)S(1)}, u32[]{:S(2)}, u32[]{:S(2)}) collective-permute-start(bf16[72,512]{1,0:T(8,128)(2,1)S(1)} %get-tuple-element.30), channel_id=1, source_target_pairs={{0,32},{1,9},{8,40},{9,17},{16,48},{17,25},{24,56},{25,1},{32,64},... | collective-permute-start | bytes 221192 | tf_op jit(solution)/shard_map/ppermute | solution.py:76
  11.8 11.5 %collective-permute-start.5 = (bf16[4,72,512]{2,1,0:T(8,128)(2,1)S(1)}, bf16[4,72,512]{2,1,0:T(8,128)(2,1)S(1)}, u32[]{:S(2)}, u32[]{:S(2)}) collective-permute-start(bf16[4,72,512]{2,1,0:T(8,128)(2,1)S(1)} %pad_maximum_fusion.refs_0_), channel_id=1, source_target_pairs={{0,24},{1,97},{8,0},{9,105},{16,8},{17,113},{24,16},{25,121},{32,5... | collective-permute-start | bytes 884744 | tf_op jit(solution)/shard_map/ppermute | solution.py:76
  15.9 8.3 %collective-permute-start.4 = (bf16[4,72,512]{2,1,0:T(8,128)(2,1)S(1)}, bf16[4,72,512]{2,1,0:T(8,128)(2,1)S(1)}, u32[]{:S(2)}, u32[]{:S(2)}) collective-permute-start(bf16[4,72,512]{2,1,0:T(8,128)(2,1)S(1)} %pad_maximum_fusion.refs_0_), channel_id=1, source_target_pairs={{0,16},{1,65},{8,24},{9,73},{16,0},{17,81},{24,8},{25,89},{32,48},... | collective-permute-start | bytes 884744 | tf_op jit(solution)/shard_map/ppermute | solution.py:76
  15.9 11.2 %collective-permute-start.3 = (bf16[4,72,512]{2,1,0:T(8,128)(2,1)S(1)}, bf16[4,72,512]{2,1,0:T(8,128)(2,1)}, u32[]{:S(2)}, u32[]{:S(2)}) collective-permute-start(bf16[4,72,512]{2,1,0:T(8,128)(2,1)S(1)} %pad_maximum_fusion.refs_0_), channel_id=1, source_target_pairs={{0,8},{1,33},{8,16},{9,41},{16,24},{17,49},{24,0},{25,57},{32,40},... | collective-permute-start | bytes 884744 | tf_op jit(solution)/shard_map/ppermute | solution.py:76
  17.3 9.9 %copy-start.8 = (bf16[2,6,128,576]{2,3,1,0:T(8,128)(2,1)S(1)}, bf16[2,6,128,576]{2,3,1,0:T(8,128)(2,1)}, u32[]{:S(2)}) copy-start(bf16[2,6,128,576]{2,3,1,0:T(8,128)(2,1)} %param.37) | copy-start | bytes 5308420
  27.1 24.9 %copy-start.1 = (bf16[128,2048]{1,0:T(8,128)(2,1)S(1)}, bf16[128,2048]{1,0:T(8,128)(2,1)}, u32[]{:S(2)}) copy-start(bf16[128,2048]{1,0:T(8,128)(2,1)} %refs_5_.1) | copy-start | bytes 1572868
  27.1 24.9 %copy-start.2 = (bf16[1,512,128]{2,1,0:T(8,128)(2,1)S(1)}, bf16[1,512,128]{2,1,0:T(8,128)(2,1)}, u32[]{:S(2)}) copy-start(bf16[1,512,128]{2,1,0:T(8,128)(2,1)} %refs_4_.1) | copy-start | bytes 393220
  32.6 31.6 %copy-start = (bf16[4,16,2048]{2,1,0:T(8,128)(2,1)S(1)}, bf16[4,16,2048]{2,1,0:T(8,128)(2,1)}, u32[]{:S(2)}) copy-start(bf16[4,16,2048]{2,1,0:T(8,128)(2,1)} %embeds_ref.1) | copy-start | bytes 786436
  32.6 31.6 %copy-start.3 = (f32[2048]{0:T(1024)S(1)}, f32[2048]{0:T(1024)}, u32[]{:S(2)}) copy-start(f32[2048]{0:T(1024)} %param.30) | copy-start | bytes 24580
  32.6 6.5 %collective-permute-start.6 = (bf16[264,512]{1,0:T(8,128)(2,1)S(1)}, bf16[264,512]{1,0:T(8,128)(2,1)S(1)}, u32[]{:S(2)}, u32[]{:S(2)}) collective-permute-start(bf16[264,512]{1,0:T(8,128)(2,1)S(1)} %get-tuple-element.38), channel_id=1, source_target_pairs={{0,96},{1,25},{8,104},{9,1},{16,112},{17,9},{24,120},{25,17},{32,0... | collective-permute-start | bytes 811016 | tf_op jit(solution)/shard_map/ppermute | solution.py:76
  33.2 8.1 %collective-permute-start.7 = (bf16[264,512]{1,0:T(8,128)(2,1)S(1)}, bf16[264,512]{1,0:T(8,128)(2,1)S(1)}, u32[]{:S(2)}, u32[]{:S(2)}) collective-permute-start(bf16[264,512]{1,0:T(8,128)(2,1)S(1)} %get-tuple-element.39), channel_id=1, source_target_pairs={{0,64},{1,17},{8,72},{9,25},{16,80},{17,1},{24,88},{25,9},{32,96},... | collective-permute-start | bytes 811016 | tf_op jit(solution)/shard_map/ppermute | solution.py:76
  34.1 10.0 %collective-permute-start.8 = (bf16[264,512]{1,0:T(8,128)(2,1)S(1)}, bf16[264,512]{1,0:T(8,128)(2,1)S(1)}, u32[]{:S(2)}, u32[]{:S(2)}) collective-permute-start(bf16[264,512]{1,0:T(8,128)(2,1)S(1)} %get-tuple-element.40), channel_id=1, source_target_pairs={{0,32},{1,9},{8,40},{9,17},{16,48},{17,25},{24,56},{25,1},{32,64},... | collective-permute-start | bytes 811016 | tf_op jit(solution)/shard_map/ppermute | solution.py:76
  44.1 46.6 %copy-start.7 = (bf16[2,352,2048]{2,1,0:T(8,128)(2,1)S(1)}, bf16[2,352,2048]{2,1,0:T(8,128)(2,1)}, u32[]{:S(2)}) copy-start(bf16[2,352,2048]{2,1,0:T(8,128)(2,1)} %down_ref.1) | copy-start | bytes 8650756
  44.4 4.4 %collective-permute-start.9 = (bf16[72,512]{1,0:T(8,128)(2,1)S(1)}, bf16[72,512]{1,0:T(8,128)(2,1)S(1)}, u32[]{:S(2)}, u32[]{:S(2)}) collective-permute-start(bf16[72,512]{1,0:T(8,128)(2,1)S(1)} %get-tuple-element.42), channel_id=1, source_target_pairs={{0,24},{1,97},{8,0},{9,105},{16,8},{17,113},{24,16},{25,121},{32,5... | collective-permute-start | bytes 221192 | tf_op jit(solution)/shard_map/ppermute | solution.py:76
  45.4 5.9 %collective-permute-start.10 = (bf16[72,512]{1,0:T(8,128)(2,1)S(1)}, bf16[72,512]{1,0:T(8,128)(2,1)S(1)}, u32[]{:S(2)}, u32[]{:S(2)}) collective-permute-start(bf16[72,512]{1,0:T(8,128)(2,1)S(1)} %get-tuple-element.43), channel_id=1, source_target_pairs={{0,16},{1,65},{8,24},{9,73},{16,0},{17,81},{24,8},{25,89},{32,48},... | collective-permute-start | bytes 221192 | tf_op jit(solution)/shard_map/ppermute | solution.py:76
  45.4 6.6 %collective-permute-start.11 = (bf16[72,512]{1,0:T(8,128)(2,1)S(1)}, bf16[72,512]{1,0:T(8,128)(2,1)S(1)}, u32[]{:S(2)}, u32[]{:S(2)}) collective-permute-start(bf16[72,512]{1,0:T(8,128)(2,1)S(1)} %get-tuple-element.44), channel_id=1, source_target_pairs={{0,8},{1,33},{8,16},{9,41},{16,24},{17,49},{24,0},{25,57},{32,40},... | collective-permute-start | bytes 221192 | tf_op jit(solution)/shard_map/ppermute | solution.py:76
  65.3 25.4 %copy-start.6 = (bf16[2,2048,352]{1,2,0:T(8,128)(2,1)S(1)}, bf16[2,2048,352]{1,2,0:T(8,128)(2,1)}, u32[]{:S(2)}) copy-start(bf16[2,2048,352]{1,2,0:T(8,128)(2,1)} %param.35) | copy-start | bytes 8650756
  87.3 3.4 %copy-start.5 = (bf16[2,2048,352]{1,2,0:T(8,128)(2,1)S(1)}, bf16[2,2048,352]{1,2,0:T(8,128)(2,1)}, u32[]{:S(2)}) copy-start(bf16[2,2048,352]{1,2,0:T(8,128)(2,1)} %param.34) | copy-start | bytes 8650756
  87.3 3.4 %collective-permute-start.12 = (bf16[512,1024]{1,0:T(8,128)(2,1)S(1)}, bf16[512,1024]{1,0:T(8,128)(2,1)S(1)}, u32[]{:S(2)}, u32[]{:S(2)}) collective-permute-start(bf16[512,1024]{1,0:T(8,128)(2,1)S(1)} %bitcast.26), channel_id=1, source_target_pairs={{0,1},{1,0},{2,3},{3,2},{4,5},{5,4},{6,7},{7,6},{8,9},{9,8},{10,11... | collective-permute-start | bytes 3145736 | tf_op jit(solution)/shard_map/ppermute | solution.py:574
  94.9 2.8 %collective-permute-start.13 = (bf16[512,1024]{1,0:T(8,128)(2,1)S(1)}, bf16[512,1024]{1,0:T(8,128)(2,1)S(1)}, u32[]{:S(2)}, u32[]{:S(2)}) collective-permute-start(bf16[512,1024]{1,0:T(8,128)(2,1)S(1)} %get-tuple-element.54), channel_id=1, source_target_pairs={{0,1},{1,0},{2,3},{3,2},{4,5},{5,4},{6,7},{7,6},{8,9},{9,8},{10,11... | collective-permute-start | bytes 3145736 | tf_op jit(solution)/shard_map/ppermute | solution.py:610

commit v6 on v5

--- a/solution.py
+++ b/solution.py
@@ -309,8 +309,11 @@
     return 32 * (chip >> 4) + 16 * ((line >> 9) ^ core) + 4 * (chip & 3) + ((chip >> 2) & 3)
 
 
-def route_kernel(info_ref, ids_ref, weights_ref, out_ref):
+def route_kernel(
+    info_ref, gate_hbm, up_hbm, down_hbm, ids_ref, weights_ref, out_ref, gate_ref, up_ref, down_ref, sems
+):
     core = info_ref[0]
+    copies = fetch((gate_hbm, up_hbm, down_hbm), (gate_ref, up_ref, down_ref), sems)
     top, steps, rows = ids_ref.shape
     line = lanes((rows, out_ref.shape[1]))
     row = line_row(line, core)
@@ -338,6 +341,8 @@
         take = jnp.where((sublanes(line.shape) == row) & (((line >> 1) & 3) == t), 1.0, 0.0)
         total = total + jnp.dot(values, take, precision=lax.Precision.HIGHEST, preferred_element_type=f32)
     out_ref[...] = total
+    for copy in copies:
+        copy.wait()
 
 
 def line_places(line, core, lines):
@@ -367,15 +372,13 @@
 
 
 def pick_kernel(
-    info_ref, gate_hbm, up_hbm, down_hbm, mine_ref, route_ref, resid_ref,
+    info_ref, mine_ref, route_ref, resid_ref, gate_ref, up_ref, down_ref,
     x_ref, own_ref, scale_ref, spot_ref,
-    gate_ref, up_ref, down_ref, sems,
 ):
     core, blk, y = info_ref[0], info_ref[1], info_ref[2]
     own_chip = 4 * (blk & 3) + (blk >> 2)
     lines, half = mine_ref.shape
     routed = 2 * SLOTS
-    copies = fetch((gate_hbm, up_hbm, down_hbm), (gate_ref, up_ref, down_ref), sems)
     line = lanes((1, lines))
     hits = [sublanes((SLOTS, lines)) + 1 == route_ref[e : e + 1, :lines].astype(jnp.int32) for e in range(2)]
     hits.append(sublanes((OWN_ROWS, lines)) == (line >> 1) - y * OWN_ROWS)
@@ -387,8 +390,6 @@
     scale_ref[...] = jnp.broadcast_to(scale, scale_ref.shape)
     spot_ref[...] = spot
     own_rows = jnp.concatenate([v[routed:].astype(bf16) for v in halves], axis=1)
-    for copy in copies:
-        copy.wait()
     act = gated(own_rows, gate_ref[...], up_ref[...])
     own = jnp.dot(act, down_ref[...], preferred_element_type=f32)
     for t in range(4):
@@ -512,14 +513,16 @@
         cosines,
     )
     cache = cache_pool.transpose(0, 1, 3, 2)
-    (route,) = kernel_call(
+    fetched = (w_shared_gate.T, w_shared_up.T, w_shared_down)
+    route, *shared = kernel_call(
         route_kernel,
         "route",
-        [((8, 2 * lines), f32)],
-        [],
+        [((8, 2 * lines), f32)] + [(a.shape, bf16) for a in fetched],
+        room_for(fetched)[-1:],
         (60_000_000, 60_000, 0),
-        SCALARS,
+        SCALARS + (pltpu.HBM,) * len(fetched),
         place,
+        *in_hbm(*fetched),
         expert_ids.transpose(2, 0, 1),
         expert_weights.transpose(2, 0, 1),
     )
@@ -575,19 +578,18 @@
     routed = pair_dev * SLOTS
     total = routed + OWN_ROWS
     slots = [((routed, width), bf16), ((OWN_ROWS, width), bf16), ((routed, 128), f32), ((8, total), f32)]
-    fetched = (w_shared_gate.T, w_shared_up.T, w_shared_down)
     x_mine, own, scale, spot = kernel_call(
         pick_kernel,
         "pick",
         slots,
-        room_for(fetched),
+        [],
         (1_000_000_000, 20_000_000, 0),
-        SCALARS + (pltpu.HBM,) * len(fetched),
+        SCALARS,
         place,
-        *in_hbm(*fetched),
         mine,
         route,
         resid,
+        *shared,
     )
     other_out, outs, spot = kernel_call(
         expert_kernel,

time: 123 us -> 122 us (level)
  transfers between devices with their start and end apart: 14 -> 14, of which waited for: 13 -> 14; matrix products, arithmetic and copies ran while one was open for 1% -> 0% of each run, Pallas kernels for 6% -> 5%
where the time goes in v6:
time: 122 us; the launch traced here: 121 us
  blocking collectives  56.7 us (46%)
  waiting for transfers between devices  28.3 us (23%)
  Pallas kernels  19.7 us (16%)
  starting transfers between devices  15 us (12%)
    ppermute x12, waiting for transfers between devices, shifted(): return lax.ppermute(value, ('x', 'z', 'core'), pairs)  25.9 us
    all_to_all x1, blocking collectives, per_device(): lax.all_to_all(own_out, ('x', 'z', 'y'), 0, 0).astype(f32)  23.2 us
    all_to_all x1, blocking collectives, per_device(): mine = lax.all_to_all(spread, ('y', 'z', 'x'), 0, 0).reshape(lines, half)  22 us
    pallas_call x10, Pallas kernels, kernel_call(): pl.pallas_call(body, out_shape=[jax.ShapeDtypeStruct(shape, dtype) for sh...  19.7 us
    ppermute x12, starting transfers between devices, shifted(): return lax.ppermute(value, ('x', 'z', 'core'), pairs)  14.8 us
    all_to_all x1, blocking collectives, per_device(): lax.all_to_all(attn_part.reshape(row_dev, 2 * steps, half), BLK, 0, 0)  11.5 us
  transfers between devices with their start and end apart: 14, of which 14 were waited for; matrix products, arithmetic and copies ran while one was open for 0% of the time, Pallas kernels for 5%

profile of v6, /device:TPU:0, one launch (start us, length us, event | category | flops | bytes accessed | tf_op | source)
XLA Modules:
  0.0 121.4 jit_solution(1206411604701516355)
XLA Ops:
  0.0 2.2 %query.1 = (bf16[72,512]{1,0:T(8,128)(2,1)S(1)}, bf16[64,2048]{1,0:T(8,128)(2,1)S(1)}, f32[8,128]{1,0:T(8,128)S(1)}, bf16[576,2048]{1,0:T(8,128)(2,1)S(1)}) custom-call(bf16[4,16,2048]{2,1,0:T(8,128)(2,1)} %embeds_ref.1, bf16[192,2048]{1,0:T(8,128)(2,1)} %bitcast.37, bf16[1,128,512]{2,1,0:T(8,128)(2,1)} %key_up_hbm.1, f32[1,2048]{1,0:T(1,128)} %bitcast.43, ...), custom_call_target="tpu_custom_call" | custom-call | flops 60000000 | bytes 20000000 | tf_op jit(solution)/shard_map/query/pallas_call | solution.py:41
  2.2 2.9 %collective-permute-start.2 = (bf16[72,512]{1,0:T(8,128)(2,1)S(1)}, bf16[72,512]{1,0:T(8,128)(2,1)S(1)}, u32[]{:S(2)}, u32[]{:S(2)}) collective-permute-start(bf16[72,512]{1,0:T(8,128)(2,1)S(1)} %get-tuple-element.34), channel_id=1, source_target_pairs={{0,96},{1,25},{8,104},{9,1},{16,112},{17,9},{24,120},{25,17},{32,0... | collective-permute-start | bytes 221192 | tf_op jit(solution)/shard_map/ppermute | solution.py:76
  5.1 0.8 collective-permute-start.1
  5.9 0.9 collective-permute-start
  6.8 0.3 collective-permute-done.2
  7.1 3.9 %collective-permute-done.1 = bf16[72,512]{1,0:T(8,128)(2,1)S(1)} collective-permute-done((bf16[72,512]{1,0:T(8,128)(2,1)S(1)}, bf16[72,512]{1,0:T(8,128)(2,1)S(1)}, u32[]{:S(2)}, u32[]{:S(2)}) %collective-permute-start.1) | collective-permute-done | bytes 73760 | tf_op jit(solution)/shard_map/ppermute | solution.py:76
  11.0 0.8 collective-permute-done
  11.8 4.1 %collective-permute-start.5 = (bf16[4,72,512]{2,1,0:T(8,128)(2,1)S(1)}, bf16[4,72,512]{2,1,0:T(8,128)(2,1)S(1)}, u32[]{:S(2)}, u32[]{:S(2)}) collective-permute-start(bf16[4,72,512]{2,1,0:T(8,128)(2,1)S(1)} %pad_maximum_fusion.refs_0_), channel_id=1, source_target_pairs={{0,24},{1,97},{8,0},{9,105},{16,8},{17,113},{24,16},{25,121},{32,5... | collective-permute-start | bytes 884744 | tf_op jit(solution)/shard_map/ppermute | solution.py:76
  15.9 1.3 %collective-permute-start.3 = (bf16[4,72,512]{2,1,0:T(8,128)(2,1)S(1)}, bf16[4,72,512]{2,1,0:T(8,128)(2,1)}, u32[]{:S(2)}, u32[]{:S(2)}) collective-permute-start(bf16[4,72,512]{2,1,0:T(8,128)(2,1)S(1)} %pad_maximum_fusion.refs_0_), channel_id=1, source_target_pairs={{0,8},{1,33},{8,16},{9,41},{16,24},{17,49},{24,0},{25,57},{32,40},... | collective-permute-start | bytes 884744 | tf_op jit(solution)/shard_map/ppermute | solution.py:76
  17.2 0.1 stack.38.info_ref
  17.3 0.1 pad_add_fusion.info_ref
  17.3 0.0 copy-start.12
  17.4 2.1 %route.1 = (f32[8,1024]{1,0:T(8,128)S(1)}, bf16[176,2048]{1,0:T(8,128)(2,1)S(1)}, bf16[176,2048]{1,0:T(8,128)(2,1)S(1)}, bf16[176,2048]{1,0:T(8,128)(2,1)S(1)}) custom-call(s32[5]{0:T(128)S(1)} %stack.38.info_ref, bf16[176,2048]{1,0:T(8,128)(2,1)} %bitcast.38, bf16[176,2048]{1,0:T(8,128)(2,1)} %bitcast.39, bf16[176,2048]{1,0:T(8,128)(2,1)} %down_hbm.1, ...), custom_call_target="tpu_custom_call" | custom-call | flops 60000000 | bytes 60000 | tf_op jit(solution)/shard_map/route/pallas_call | solution.py:41
  19.5 1.0 entry.1.refs_5_
  20.5 2.8 %collective-permute-done.5.refs_3_ = bf16[4,72,512]{2,1,0:T(8,128)(2,1)S(1)} collective-permute-done((bf16[4,72,512]{2,1,0:T(8,128)(2,1)S(1)}, bf16[4,72,512]{2,1,0:T(8,128)(2,1)S(1)}, u32[]{:S(2)}, u32[]{:S(2)}) %collective-permute-start.5) | collective-permute-done | bytes 294944 | tf_op jit(solution)/shard_map/ppermute | solution.py:76
  23.3 0.9 collective-permute-done.4.refs_2_
  24.2 2.9 %collective-permute-done.3.refs_1_ = bf16[4,72,512]{2,1,0:T(8,128)(2,1)} collective-permute-done((bf16[4,72,512]{2,1,0:T(8,128)(2,1)S(1)}, bf16[4,72,512]{2,1,0:T(8,128)(2,1)}, u32[]{:S(2)}, u32[]{:S(2)}) %collective-permute-start.3) | collective-permute-done | bytes 294944 | tf_op jit(solution)/shard_map/ppermute | solution.py:76
  27.1 0.0 copy-start.1
  27.1 0.0 copy-start.2
  27.1 5.5 %attend.1 = (bf16[264,512]{1,0:T(8,128)(2,1)S(1)}, bf16[264,512]{1,0:T(8,128)(2,1)S(1)}, bf16[264,512]{1,0:T(8,128)(2,1)S(1)}, bf16[264,512]{1,0:T(8,128)(2,1)S(1)}) custom-call(s32[3]{0:T(128)S(1)} %pad_add_fusion.info_ref, bf16[4,72,512]{2,1,0:T(8,128)(2,1)S(1)} %pad_maximum_fusion.refs_0_, bf16[4,72,512]{2,1,0:T(8,128)(2,1)} %collective-permute-done.3.refs_1_, ...), custom_call_target="tpu_custom_call" | custom-call | flops 1800000000 | bytes 5000000 | tf_op jit(solution)/shard_map/attend/pallas_call | solution.py:41
  32.6 0.0 copy-start
  32.7 0.6 collective-permute-start.6
  33.3 0.9 collective-permute-start.7
  34.2 1.2 collective-permute-start.8
  35.4 3.8 %collective-permute-done.6.refs_1_ = bf16[264,512]{1,0:T(8,128)(2,1)S(1)} collective-permute-done((bf16[264,512]{1,0:T(8,128)(2,1)S(1)}, bf16[264,512]{1,0:T(8,128)(2,1)S(1)}, u32[]{:S(2)}, u32[]{:S(2)}) %collective-permute-start.6) | collective-permute-done | bytes 270368 | tf_op jit(solution)/shard_map/ppermute | solution.py:76
  39.2 2.2 %collective-permute-done.7.refs_2_ = bf16[264,512]{1,0:T(8,128)(2,1)S(1)} collective-permute-done((bf16[264,512]{1,0:T(8,128)(2,1)S(1)}, bf16[264,512]{1,0:T(8,128)(2,1)S(1)}, u32[]{:S(2)}, u32[]{:S(2)}) %collective-permute-start.7) | collective-permute-done | bytes 270368 | tf_op jit(solution)/shard_map/ppermute | solution.py:76
  41.4 2.8 %collective-permute-done.8.refs_3_ = bf16[264,512]{1,0:T(8,128)(2,1)S(1)} collective-permute-done((bf16[264,512]{1,0:T(8,128)(2,1)S(1)}, bf16[264,512]{1,0:T(8,128)(2,1)S(1)}, u32[]{:S(2)}, u32[]{:S(2)}) %collective-permute-start.8) | collective-permute-done | bytes 270368 | tf_op jit(solution)/shard_map/ppermute | solution.py:76
  44.2 0.3 merge.1
  44.5 1.0 collective-permute-start.9
  45.4 1.1 collective-permute-start.11
  46.6 2.3 %collective-permute-done.9.refs_1_ = bf16[72,512]{1,0:T(8,128)(2,1)S(1)} collective-permute-done((bf16[72,512]{1,0:T(8,128)(2,1)S(1)}, bf16[72,512]{1,0:T(8,128)(2,1)S(1)}, u32[]{:S(2)}, u32[]{:S(2)}) %collective-permute-start.9) | collective-permute-done | bytes 73760 | tf_op jit(solution)/shard_map/ppermute | solution.py:76
  48.9 2.4 %collective-permute-done.10.refs_2_ = bf16[72,512]{1,0:T(8,128)(2,1)S(1)} collective-permute-done((bf16[72,512]{1,0:T(8,128)(2,1)S(1)}, bf16[72,512]{1,0:T(8,128)(2,1)S(1)}, u32[]{:S(2)}, u32[]{:S(2)}) %collective-permute-start.10) | collective-permute-done | bytes 73760 | tf_op jit(solution)/shard_map/ppermute | solution.py:76
  51.3 0.7 collective-permute-done.11.refs_3_
  52.1 0.7 output.1
  52.8 11.5 %all_to_all.15.parts_ref = bf16[16,8,1024]{2,1,0:T(8,128)(2,1)S(1)} all-to-all(bf16[16,8,1024]{2,1,0:T(8,128)(2,1)S(1)} %bitcast.25), channel_id=1, replica_groups=mesh['x'=4,'z'=4,'y'=4,'core'=2] {'x','z'}, dimensions={0} | all-to-all | bytes 524288 | tf_op jit(solution)/shard_map/all_to_all | solution.py:562
  64.3 1.1 norm.1
  65.3 0.0 copy-start.8
  65.3 22.0 %all_to_all.16 = bf16[64,8,1024]{2,1,0:T(8,128)(2,1)S(1)} all-to-all(bf16[64,8,1024]{2,1,0:T(8,128)(2,1)S(1)} %get-tuple-element.50), channel_id=1, replica_groups=mesh['x'=4,'z'=4,'y'=4,'core'=2] {'y','z','x'}, dimensions={0} | all-to-all | bytes 2097152 | tf_op jit(solution)/shard_map/all_to_all | solution.py:576
  87.4 2.0 %pick.1 = (bf16[192,2048]{1,0:T(8,128)(2,1)S(1)}, bf16[64,2048]{1,0:T(8,128)(2,1)S(1)}, f32[192,128]{1,0:T(8,128)S(1)}, f32[8,256]{1,0:T(8,128)S(1)}) custom-call(s32[5]{0:T(128)S(1)} %stack.38.info_ref, bf16[512,1024]{1,0:T(8,128)(2,1)S(1)} %bitcast.27, f32[8,1024]{1,0:T(8,128)S(1)} %get-tuple-element.51.route_ref, ...), custom_call_target="tpu_custom_call" | custom-call | flops 1000000000 | bytes 20000000 | tf_op jit(solution)/shard_map/pick/pallas_call | solution.py:41
  89.4 0.6 collective-permute-done.12.other_ref
  90.0 4.2 %experts.1 = (bf16[512,1024]{1,0:T(8,128)(2,1)S(1)}, bf16[256,2048]{1,0:T(8,128)(2,1)S(1)}, s32[8,256]{1,0:T(8,128)S(1)}) custom-call(s32[5]{0:T(128)S(1)} %stack.38.info_ref, bf16[192,2048]{1,0:T(8,128)(2,1)S(1)} %get-tuple-element.56.mine_x_ref, bf16[64,2048]{1,0:T(8,128)(2,1)S(1)} %get-tuple-element.57.own_ref, ...), custom_call_target="tpu_custom_call" | custom-call | flops 3000000000 | bytes 15000000 | tf_op jit(solution)/shard_map/experts/pallas_call | solution.py:41
  94.2 0.2 collective-permute-start.13
  94.4 0.7 put.1
  95.2 1.8 %collective-permute-done.13 = bf16[512,1024]{1,0:T(8,128)(2,1)S(1)} collective-permute-done((bf16[512,1024]{1,0:T(8,128)(2,1)S(1)}, bf16[512,1024]{1,0:T(8,128)(2,1)S(1)}, u32[]{:S(2)}, u32[]{:S(2)}) %collective-permute-start.13) | collective-permute-done | bytes 1048608 | tf_op jit(solution)/shard_map/ppermute | solution.py:612
  97.0 0.4 fusion
  97.4 23.2 %all_to_all.17 = bf16[64,8,1024]{2,1,0:T(8,128)(2,1)S(1)} all-to-all(bf16[64,8,1024]{2,1,0:T(8,128)(2,1)S(1)} %fusion), channel_id=1, replica_groups=mesh['x'=4,'z'=4,'y'=4,'core'=2] {'x','z','y'}, dimensions={0} | all-to-all | bytes 2097152 | tf_op jit(solution)/shard_map/all_to_all | solution.py:618
  120.6 0.2 convert_reduce_fusion
  120.7 0.7 reshape.27
  (27 shorter events, 0.1 us)
Async XLA Ops:
  0.0 17.3 %copy-start.13 = (s32[2]{0:T(128)S(1)}, s32[2]{0:T(128)}, u32[]{:S(2)}) copy-start(s32[2]{0:T(128)} %counts_hbm.1) | copy-start | bytes 28
  0.0 17.3 %copy-start.3 = (s32[4,128,6]{1,0,2:T(4,128)S(1)}, s32[4,128,6]{1,0,2:T(4,128)}, u32[]{:S(2)}) copy-start(s32[4,128,6]{1,0,2:T(4,128)} %param.41) | copy-start | bytes 36868
  0.0 17.3 %copy-start.4 = (f32[4,128,6]{1,0,2:T(4,128)S(1)}, f32[4,128,6]{1,0,2:T(4,128)}, u32[]{:S(2)}) copy-start(f32[4,128,6]{1,0,2:T(4,128)} %param.42) | copy-start | bytes 36868
  0.0 19.5 %copy-start.6 = (f32[512]{0:T(512)S(1)}, f32[512]{0:T(512)}, u32[]{:S(2)}) copy-start(f32[512]{0:T(512)} %param.26) | copy-start | bytes 6148
  2.2 4.9 %collective-permute-start.2 = (bf16[72,512]{1,0:T(8,128)(2,1)S(1)}, bf16[72,512]{1,0:T(8,128)(2,1)S(1)}, u32[]{:S(2)}, u32[]{:S(2)}) collective-permute-start(bf16[72,512]{1,0:T(8,128)(2,1)S(1)} %get-tuple-element.34), channel_id=1, source_target_pairs={{0,96},{1,25},{8,104},{9,1},{16,112},{17,9},{24,120},{25,17},{32,0... | collective-permute-start | bytes 221192 | tf_op jit(solution)/shard_map/ppermute | solution.py:76
  5.1 5.9 %collective-permute-start.1 = (bf16[72,512]{1,0:T(8,128)(2,1)S(1)}, bf16[72,512]{1,0:T(8,128)(2,1)S(1)}, u32[]{:S(2)}, u32[]{:S(2)}) collective-permute-start(bf16[72,512]{1,0:T(8,128)(2,1)S(1)} %get-tuple-element.34), channel_id=1, source_target_pairs={{0,64},{1,17},{8,72},{9,25},{16,80},{17,1},{24,88},{25,9},{32,96},... | collective-permute-start | bytes 221192 | tf_op jit(solution)/shard_map/ppermute | solution.py:76
  5.9 5.8 %collective-permute-start = (bf16[72,512]{1,0:T(8,128)(2,1)S(1)}, bf16[72,512]{1,0:T(8,128)(2,1)S(1)}, u32[]{:S(2)}, u32[]{:S(2)}) collective-permute-start(bf16[72,512]{1,0:T(8,128)(2,1)S(1)} %get-tuple-element.34), channel_id=1, source_target_pairs={{0,32},{1,9},{8,40},{9,17},{16,48},{17,25},{24,56},{25,1},{32,64},... | collective-permute-start | bytes 221192 | tf_op jit(solution)/shard_map/ppermute | solution.py:76
  11.8 11.5 %collective-permute-start.5 = (bf16[4,72,512]{2,1,0:T(8,128)(2,1)S(1)}, bf16[4,72,512]{2,1,0:T(8,128)(2,1)S(1)}, u32[]{:S(2)}, u32[]{:S(2)}) collective-permute-start(bf16[4,72,512]{2,1,0:T(8,128)(2,1)S(1)} %pad_maximum_fusion.refs_0_), channel_id=1, source_target_pairs={{0,24},{1,97},{8,0},{9,105},{16,8},{17,113},{24,16},{25,121},{32,5... | collective-permute-start | bytes 884744 | tf_op jit(solution)/shard_map/ppermute | solution.py:76
  15.9 8.3 %collective-permute-start.4 = (bf16[4,72,512]{2,1,0:T(8,128)(2,1)S(1)}, bf16[4,72,512]{2,1,0:T(8,128)(2,1)S(1)}, u32[]{:S(2)}, u32[]{:S(2)}) collective-permute-start(bf16[4,72,512]{2,1,0:T(8,128)(2,1)S(1)} %pad_maximum_fusion.refs_0_), channel_id=1, source_target_pairs={{0,16},{1,65},{8,24},{9,73},{16,0},{17,81},{24,8},{25,89},{32,48},... | collective-permute-start | bytes 884744 | tf_op jit(solution)/shard_map/ppermute | solution.py:76
  15.9 11.2 %collective-permute-start.3 = (bf16[4,72,512]{2,1,0:T(8,128)(2,1)S(1)}, bf16[4,72,512]{2,1,0:T(8,128)(2,1)}, u32[]{:S(2)}, u32[]{:S(2)}) collective-permute-start(bf16[4,72,512]{2,1,0:T(8,128)(2,1)S(1)} %pad_maximum_fusion.refs_0_), channel_id=1, source_target_pairs={{0,8},{1,33},{8,16},{9,41},{16,24},{17,49},{24,0},{25,57},{32,40},... | collective-permute-start | bytes 884744 | tf_op jit(solution)/shard_map/ppermute | solution.py:76
  17.3 9.8 %copy-start.10 = (bf16[2,6,128,576]{2,3,1,0:T(8,128)(2,1)S(1)}, bf16[2,6,128,576]{2,3,1,0:T(8,128)(2,1)}, u32[]{:S(2)}) copy-start(bf16[2,6,128,576]{2,3,1,0:T(8,128)(2,1)} %param.37) | copy-start | bytes 5308420
  17.3 9.8 %copy-start.11 = (s32[2,8,64]{2,1,0:T(8,128)S(1)}, s32[2,8,64]{2,1,0:T(8,128)}, u32[]{:S(2)}) copy-start(s32[2,8,64]{2,1,0:T(8,128)} %refs_7_.1) | copy-start | bytes 12292
  17.3 9.8 %copy-start.12 = (s32[4,2,8]{2,1,0:T(2,128)S(1)}, s32[4,2,8]{2,1,0:T(2,128)}, u32[]{:S(2)}) copy-start(s32[4,2,8]{2,1,0:T(2,128)} %refs_6_.1) | copy-start | bytes 772
  27.1 25.0 %copy-start.1 = (bf16[128,2048]{1,0:T(8,128)(2,1)S(1)}, bf16[128,2048]{1,0:T(8,128)(2,1)}, u32[]{:S(2)}) copy-start(bf16[128,2048]{1,0:T(8,128)(2,1)} %refs_5_.1) | copy-start | bytes 1572868
  27.1 25.0 %copy-start.2 = (bf16[1,512,128]{2,1,0:T(8,128)(2,1)S(1)}, bf16[1,512,128]{2,1,0:T(8,128)(2,1)}, u32[]{:S(2)}) copy-start(bf16[1,512,128]{2,1,0:T(8,128)(2,1)} %refs_4_.1) | copy-start | bytes 393220
  32.6 31.6 %copy-start = (bf16[4,16,2048]{2,1,0:T(8,128)(2,1)S(1)}, bf16[4,16,2048]{2,1,0:T(8,128)(2,1)}, u32[]{:S(2)}) copy-start(bf16[4,16,2048]{2,1,0:T(8,128)(2,1)} %embeds_ref.1) | copy-start | bytes 786436
  32.6 31.6 %copy-start.5 = (f32[2048]{0:T(1024)S(1)}, f32[2048]{0:T(1024)}, u32[]{:S(2)}) copy-start(f32[2048]{0:T(1024)} %param.30) | copy-start | bytes 24580
  32.7 6.5 %collective-permute-start.6 = (bf16[264,512]{1,0:T(8,128)(2,1)S(1)}, bf16[264,512]{1,0:T(8,128)(2,1)S(1)}, u32[]{:S(2)}, u32[]{:S(2)}) collective-permute-start(bf16[264,512]{1,0:T(8,128)(2,1)S(1)} %get-tuple-element.43), channel_id=1, source_target_pairs={{0,96},{1,25},{8,104},{9,1},{16,112},{17,9},{24,120},{25,17},{32,0... | collective-permute-start | bytes 811016 | tf_op jit(solution)/shard_map/ppermute | solution.py:76
  33.3 8.1 %collective-permute-start.7 = (bf16[264,512]{1,0:T(8,128)(2,1)S(1)}, bf16[264,512]{1,0:T(8,128)(2,1)S(1)}, u32[]{:S(2)}, u32[]{:S(2)}) collective-permute-start(bf16[264,512]{1,0:T(8,128)(2,1)S(1)} %get-tuple-element.44), channel_id=1, source_target_pairs={{0,64},{1,17},{8,72},{9,25},{16,80},{17,1},{24,88},{25,9},{32,96},... | collective-permute-start | bytes 811016 | tf_op jit(solution)/shard_map/ppermute | solution.py:76
  34.2 10.0 %collective-permute-start.8 = (bf16[264,512]{1,0:T(8,128)(2,1)S(1)}, bf16[264,512]{1,0:T(8,128)(2,1)S(1)}, u32[]{:S(2)}, u32[]{:S(2)}) collective-permute-start(bf16[264,512]{1,0:T(8,128)(2,1)S(1)} %get-tuple-element.45), channel_id=1, source_target_pairs={{0,32},{1,9},{8,40},{9,17},{16,48},{17,25},{24,56},{25,1},{32,64},... | collective-permute-start | bytes 811016 | tf_op jit(solution)/shard_map/ppermute | solution.py:76
  44.2 45.9 %copy-start.9 = (bf16[2,352,2048]{2,1,0:T(8,128)(2,1)S(1)}, bf16[2,352,2048]{2,1,0:T(8,128)(2,1)}, u32[]{:S(2)}) copy-start(bf16[2,352,2048]{2,1,0:T(8,128)(2,1)} %down_ref.1) | copy-start | bytes 8650756
  44.5 4.4 %collective-permute-start.9 = (bf16[72,512]{1,0:T(8,128)(2,1)S(1)}, bf16[72,512]{1,0:T(8,128)(2,1)S(1)}, u32[]{:S(2)}, u32[]{:S(2)}) collective-permute-start(bf16[72,512]{1,0:T(8,128)(2,1)S(1)} %get-tuple-element.47), channel_id=1, source_target_pairs={{0,24},{1,97},{8,0},{9,105},{16,8},{17,113},{24,16},{25,121},{32,5... | collective-permute-start | bytes 221192 | tf_op jit(solution)/shard_map/ppermute | solution.py:76
  45.4 5.9 %collective-permute-start.10 = (bf16[72,512]{1,0:T(8,128)(2,1)S(1)}, bf16[72,512]{1,0:T(8,128)(2,1)S(1)}, u32[]{:S(2)}, u32[]{:S(2)}) collective-permute-start(bf16[72,512]{1,0:T(8,128)(2,1)S(1)} %get-tuple-element.48), channel_id=1, source_target_pairs={{0,16},{1,65},{8,24},{9,73},{16,0},{17,81},{24,8},{25,89},{32,48},... | collective-permute-start | bytes 221192 | tf_op jit(solution)/shard_map/ppermute | solution.py:76
  45.4 6.6 %collective-permute-start.11 = (bf16[72,512]{1,0:T(8,128)(2,1)S(1)}, bf16[72,512]{1,0:T(8,128)(2,1)S(1)}, u32[]{:S(2)}, u32[]{:S(2)}) collective-permute-start(bf16[72,512]{1,0:T(8,128)(2,1)S(1)} %get-tuple-element.49), channel_id=1, source_target_pairs={{0,8},{1,33},{8,16},{9,41},{16,24},{17,49},{24,0},{25,57},{32,40},... | collective-permute-start | bytes 221192 | tf_op jit(solution)/shard_map/ppermute | solution.py:76
  65.3 24.7 %copy-start.8 = (bf16[2,2048,352]{1,2,0:T(8,128)(2,1)S(1)}, bf16[2,2048,352]{1,2,0:T(8,128)(2,1)}, u32[]{:S(2)}) copy-start(bf16[2,2048,352]{1,2,0:T(8,128)(2,1)} %param.35) | copy-start | bytes 8650756
  87.3 2.7 %copy-start.7 = (bf16[2,2048,352]{1,2,0:T(8,128)(2,1)S(1)}, bf16[2,2048,352]{1,2,0:T(8,128)(2,1)}, u32[]{:S(2)}) copy-start(bf16[2,2048,352]{1,2,0:T(8,128)(2,1)} %param.34) | copy-start | bytes 8650756
  87.4 2.7 %collective-permute-start.12 = (bf16[512,1024]{1,0:T(8,128)(2,1)S(1)}, bf16[512,1024]{1,0:T(8,128)(2,1)S(1)}, u32[]{:S(2)}, u32[]{:S(2)}) collective-permute-start(bf16[512,1024]{1,0:T(8,128)(2,1)S(1)} %bitcast.26), channel_id=1, source_target_pairs={{0,1},{1,0},{2,3},{3,2},{4,5},{5,4},{6,7},{7,6},{8,9},{9,8},{10,11... | collective-permute-start | bytes 3145736 | tf_op jit(solution)/shard_map/ppermute | solution.py:577
  94.2 2.7 %collective-permute-start.13 = (bf16[512,1024]{1,0:T(8,128)(2,1)S(1)}, bf16[512,1024]{1,0:T(8,128)(2,1)S(1)}, u32[]{:S(2)}, u32[]{:S(2)}) collective-permute-start(bf16[512,1024]{1,0:T(8,128)(2,1)S(1)} %get-tuple-element.62), channel_id=1, source_target_pairs={{0,1},{1,0},{2,3},{3,2},{4,5},{5,4},{6,7},{7,6},{8,9},{9,8},{10,11... | collective-permute-start | bytes 3145736 | tf_op jit(solution)/shard_map/ppermute | solution.py:612

commit v7 on v6

--- a/solution.py
+++ b/solution.py
@@ -306,7 +306,7 @@
 
 def line_row(line, core):
     chip = (line >> 3) & 63
-    return 32 * (chip >> 4) + 16 * ((line >> 9) ^ core) + 4 * (chip & 3) + ((chip >> 2) & 3)
+    return 32 * (chip >> 4) + 16 * ((line >> 9) ^ core) + (chip & 15)
 
 
 def route_kernel(
@@ -376,7 +376,7 @@
     x_ref, own_ref, scale_ref, spot_ref,
 ):
     core, blk, y = info_ref[0], info_ref[1], info_ref[2]
-    own_chip = 4 * (blk & 3) + (blk >> 2)
+    own_chip = blk
     lines, half = mine_ref.shape
     routed = 2 * SLOTS
     line = lanes((1, lines))
@@ -573,7 +573,7 @@
         ffn_gain.reshape(1, width),
     )
 
-    mine = lax.all_to_all(spread, ("y", "z", "x"), 0, 0).reshape(lines, half)
+    mine = lax.all_to_all(spread, ("y", "x", "z"), 0, 0).reshape(lines, half)
     other = lax.ppermute(mine, "core", CORES)
     routed = pair_dev * SLOTS
     total = routed + OWN_ROWS

time: 122 us -> 122 us (level)
  no operation moved by 1% of the time
where the time goes in v7:
time: 122 us; the launch traced here: 121 us
  blocking collectives  56.6 us (46%)
  waiting for transfers between devices  28.3 us (23%)
  Pallas kernels  19.7 us (16%)
  starting transfers between devices  15 us (12%)
    ppermute x12, waiting for transfers between devices, shifted(): return lax.ppermute(value, ('x', 'z', 'core'), pairs)  25.9 us
    all_to_all x1, blocking collectives, per_device(): lax.all_to_all(own_out, ('x', 'z', 'y'), 0, 0).astype(f32)  23.3 us
    all_to_all x1, blocking collectives, per_device(): mine = lax.all_to_all(spread, ('y', 'x', 'z'), 0, 0).reshape(lines, half)  21.8 us
    pallas_call x10, Pallas kernels, kernel_call(): pl.pallas_call(body, out_shape=[jax.ShapeDtypeStruct(shape, dtype) for sh...  19.7 us
    ppermute x12, starting transfers between devices, shifted(): return lax.ppermute(value, ('x', 'z', 'core'), pairs)  14.8 us
    all_to_all x1, blocking collectives, per_device(): lax.all_to_all(attn_part.reshape(row_dev, 2 * steps, half), BLK, 0, 0)  11.5 us
  transfers between devices with their start and end apart: 14, of which 14 were waited for; matrix products, arithmetic and copies ran while one was open for 0% of the time, Pallas kernels for 5%

profile of v7, /device:TPU:0, one launch (start us, length us, event | category | flops | bytes accessed | tf_op | source)
XLA Modules:
  0.0 121.3 jit_solution(7415364134650942457)
XLA Ops:
  0.0 2.2 %query.1 = (bf16[72,512]{1,0:T(8,128)(2,1)S(1)}, bf16[64,2048]{1,0:T(8,128)(2,1)S(1)}, f32[8,128]{1,0:T(8,128)S(1)}, bf16[576,2048]{1,0:T(8,128)(2,1)S(1)}) custom-call(bf16[4,16,2048]{2,1,0:T(8,128)(2,1)} %embeds_ref.1, bf16[192,2048]{1,0:T(8,128)(2,1)} %bitcast.37, bf16[1,128,512]{2,1,0:T(8,128)(2,1)} %key_up_hbm.1, f32[1,2048]{1,0:T(1,128)} %bitcast.43, ...), custom_call_target="tpu_custom_call" | custom-call | flops 60000000 | bytes 20000000 | tf_op jit(solution)/shard_map/query/pallas_call | solution.py:41
  2.2 2.9 %collective-permute-start.2 = (bf16[72,512]{1,0:T(8,128)(2,1)S(1)}, bf16[72,512]{1,0:T(8,128)(2,1)S(1)}, u32[]{:S(2)}, u32[]{:S(2)}) collective-permute-start(bf16[72,512]{1,0:T(8,128)(2,1)S(1)} %get-tuple-element.34), channel_id=1, source_target_pairs={{0,96},{1,25},{8,104},{9,1},{16,112},{17,9},{24,120},{25,17},{32,0... | collective-permute-start | bytes 221192 | tf_op jit(solution)/shard_map/ppermute | solution.py:76
  5.1 0.8 collective-permute-start.1
  5.9 0.9 collective-permute-start
  6.8 0.3 collective-permute-done.2
  7.1 3.9 %collective-permute-done.1 = bf16[72,512]{1,0:T(8,128)(2,1)S(1)} collective-permute-done((bf16[72,512]{1,0:T(8,128)(2,1)S(1)}, bf16[72,512]{1,0:T(8,128)(2,1)S(1)}, u32[]{:S(2)}, u32[]{:S(2)}) %collective-permute-start.1) | collective-permute-done | bytes 73760 | tf_op jit(solution)/shard_map/ppermute | solution.py:76
  11.0 0.8 collective-permute-done
  11.8 4.1 %collective-permute-start.5 = (bf16[4,72,512]{2,1,0:T(8,128)(2,1)S(1)}, bf16[4,72,512]{2,1,0:T(8,128)(2,1)S(1)}, u32[]{:S(2)}, u32[]{:S(2)}) collective-permute-start(bf16[4,72,512]{2,1,0:T(8,128)(2,1)S(1)} %pad_maximum_fusion.refs_0_), channel_id=1, source_target_pairs={{0,24},{1,97},{8,0},{9,105},{16,8},{17,113},{24,16},{25,121},{32,5... | collective-permute-start | bytes 884744 | tf_op jit(solution)/shard_map/ppermute | solution.py:76
  15.9 1.3 %collective-permute-start.3 = (bf16[4,72,512]{2,1,0:T(8,128)(2,1)S(1)}, bf16[4,72,512]{2,1,0:T(8,128)(2,1)}, u32[]{:S(2)}, u32[]{:S(2)}) collective-permute-start(bf16[4,72,512]{2,1,0:T(8,128)(2,1)S(1)} %pad_maximum_fusion.refs_0_), channel_id=1, source_target_pairs={{0,8},{1,33},{8,16},{9,41},{16,24},{17,49},{24,0},{25,57},{32,40},... | collective-permute-start | bytes 884744 | tf_op jit(solution)/shard_map/ppermute | solution.py:76
  17.2 0.1 stack.38.info_ref
  17.3 0.1 pad_add_fusion.info_ref
  17.3 0.0 copy-start.12
  17.4 2.1 %route.1 = (f32[8,1024]{1,0:T(8,128)S(1)}, bf16[176,2048]{1,0:T(8,128)(2,1)S(1)}, bf16[176,2048]{1,0:T(8,128)(2,1)S(1)}, bf16[176,2048]{1,0:T(8,128)(2,1)S(1)}) custom-call(s32[5]{0:T(128)S(1)} %stack.38.info_ref, bf16[176,2048]{1,0:T(8,128)(2,1)} %bitcast.38, bf16[176,2048]{1,0:T(8,128)(2,1)} %bitcast.39, bf16[176,2048]{1,0:T(8,128)(2,1)} %down_hbm.1, ...), custom_call_target="tpu_custom_call" | custom-call | flops 60000000 | bytes 60000 | tf_op jit(solution)/shard_map/route/pallas_call | solution.py:41
  19.5 1.0 entry.1.refs_5_
  20.5 2.8 %collective-permute-done.5.refs_3_ = bf16[4,72,512]{2,1,0:T(8,128)(2,1)S(1)} collective-permute-done((bf16[4,72,512]{2,1,0:T(8,128)(2,1)S(1)}, bf16[4,72,512]{2,1,0:T(8,128)(2,1)S(1)}, u32[]{:S(2)}, u32[]{:S(2)}) %collective-permute-start.5) | collective-permute-done | bytes 294944 | tf_op jit(solution)/shard_map/ppermute | solution.py:76
  23.3 0.9 collective-permute-done.4.refs_2_
  24.2 2.9 %collective-permute-done.3.refs_1_ = bf16[4,72,512]{2,1,0:T(8,128)(2,1)} collective-permute-done((bf16[4,72,512]{2,1,0:T(8,128)(2,1)S(1)}, bf16[4,72,512]{2,1,0:T(8,128)(2,1)}, u32[]{:S(2)}, u32[]{:S(2)}) %collective-permute-start.3) | collective-permute-done | bytes 294944 | tf_op jit(solution)/shard_map/ppermute | solution.py:76
  27.1 0.0 copy-start.1
  27.1 0.0 copy-start.2
  27.1 5.5 %attend.1 = (bf16[264,512]{1,0:T(8,128)(2,1)S(1)}, bf16[264,512]{1,0:T(8,128)(2,1)S(1)}, bf16[264,512]{1,0:T(8,128)(2,1)S(1)}, bf16[264,512]{1,0:T(8,128)(2,1)S(1)}) custom-call(s32[3]{0:T(128)S(1)} %pad_add_fusion.info_ref, bf16[4,72,512]{2,1,0:T(8,128)(2,1)S(1)} %pad_maximum_fusion.refs_0_, bf16[4,72,512]{2,1,0:T(8,128)(2,1)} %collective-permute-done.3.refs_1_, ...), custom_call_target="tpu_custom_call" | custom-call | flops 1800000000 | bytes 5000000 | tf_op jit(solution)/shard_map/attend/pallas_call | solution.py:41
  32.6 0.0 copy-start
  32.7 0.6 collective-permute-start.6
  33.3 0.9 collective-permute-start.7
  34.2 1.2 collective-permute-start.8
  35.4 3.8 %collective-permute-done.6.refs_1_ = bf16[264,512]{1,0:T(8,128)(2,1)S(1)} collective-permute-done((bf16[264,512]{1,0:T(8,128)(2,1)S(1)}, bf16[264,512]{1,0:T(8,128)(2,1)S(1)}, u32[]{:S(2)}, u32[]{:S(2)}) %collective-permute-start.6) | collective-permute-done | bytes 270368 | tf_op jit(solution)/shard_map/ppermute | solution.py:76
  39.2 2.2 %collective-permute-done.7.refs_2_ = bf16[264,512]{1,0:T(8,128)(2,1)S(1)} collective-permute-done((bf16[264,512]{1,0:T(8,128)(2,1)S(1)}, bf16[264,512]{1,0:T(8,128)(2,1)S(1)}, u32[]{:S(2)}, u32[]{:S(2)}) %collective-permute-start.7) | collective-permute-done | bytes 270368 | tf_op jit(solution)/shard_map/ppermute | solution.py:76
  41.4 2.8 %collective-permute-done.8.refs_3_ = bf16[264,512]{1,0:T(8,128)(2,1)S(1)} collective-permute-done((bf16[264,512]{1,0:T(8,128)(2,1)S(1)}, bf16[264,512]{1,0:T(8,128)(2,1)S(1)}, u32[]{:S(2)}, u32[]{:S(2)}) %collective-permute-start.8) | collective-permute-done | bytes 270368 | tf_op jit(solution)/shard_map/ppermute | solution.py:76
  44.2 0.3 merge.1
  44.5 1.0 collective-permute-start.9
  45.4 1.1 collective-permute-start.11
  46.6 2.3 %collective-permute-done.9.refs_1_ = bf16[72,512]{1,0:T(8,128)(2,1)S(1)} collective-permute-done((bf16[72,512]{1,0:T(8,128)(2,1)S(1)}, bf16[72,512]{1,0:T(8,128)(2,1)S(1)}, u32[]{:S(2)}, u32[]{:S(2)}) %collective-permute-start.9) | collective-permute-done | bytes 73760 | tf_op jit(solution)/shard_map/ppermute | solution.py:76
  48.9 2.4 %collective-permute-done.10.refs_2_ = bf16[72,512]{1,0:T(8,128)(2,1)S(1)} collective-permute-done((bf16[72,512]{1,0:T(8,128)(2,1)S(1)}, bf16[72,512]{1,0:T(8,128)(2,1)S(1)}, u32[]{:S(2)}, u32[]{:S(2)}) %collective-permute-start.10) | collective-permute-done | bytes 73760 | tf_op jit(solution)/shard_map/ppermute | solution.py:76
  51.3 0.7 collective-permute-done.11.refs_3_
  52.1 0.7 output.1
  52.8 11.5 %all_to_all.15.parts_ref = bf16[16,8,1024]{2,1,0:T(8,128)(2,1)S(1)} all-to-all(bf16[16,8,1024]{2,1,0:T(8,128)(2,1)S(1)} %bitcast.25), channel_id=1, replica_groups=mesh['x'=4,'z'=4,'y'=4,'core'=2] {'x','z'}, dimensions={0} | all-to-all | bytes 524288 | tf_op jit(solution)/shard_map/all_to_all | solution.py:562
  64.3 1.1 norm.1
  65.3 0.0 copy-start.8
  65.3 21.8 %all_to_all.16 = bf16[64,8,1024]{2,1,0:T(8,128)(2,1)S(1)} all-to-all(bf16[64,8,1024]{2,1,0:T(8,128)(2,1)S(1)} %get-tuple-element.50), channel_id=1, replica_groups=mesh['x'=4,'z'=4,'y'=4,'core'=2] {'y','x','z'}, dimensions={0} | all-to-all | bytes 2097152 | tf_op jit(solution)/shard_map/all_to_all | solution.py:576
  87.1 2.0 %pick.1 = (bf16[192,2048]{1,0:T(8,128)(2,1)S(1)}, bf16[64,2048]{1,0:T(8,128)(2,1)S(1)}, f32[192,128]{1,0:T(8,128)S(1)}, f32[8,256]{1,0:T(8,128)S(1)}) custom-call(s32[5]{0:T(128)S(1)} %stack.38.info_ref, bf16[512,1024]{1,0:T(8,128)(2,1)S(1)} %bitcast.27, f32[8,1024]{1,0:T(8,128)S(1)} %get-tuple-element.51.route_ref, ...), custom_call_target="tpu_custom_call" | custom-call | flops 1000000000 | bytes 20000000 | tf_op jit(solution)/shard_map/pick/pallas_call | solution.py:41
  89.2 0.6 collective-permute-done.12.other_ref
  89.8 4.2 %experts.1 = (bf16[512,1024]{1,0:T(8,128)(2,1)S(1)}, bf16[256,2048]{1,0:T(8,128)(2,1)S(1)}, s32[8,256]{1,0:T(8,128)S(1)}) custom-call(s32[5]{0:T(128)S(1)} %stack.38.info_ref, bf16[192,2048]{1,0:T(8,128)(2,1)S(1)} %get-tuple-element.56.mine_x_ref, bf16[64,2048]{1,0:T(8,128)(2,1)S(1)} %get-tuple-element.57.own_ref, ...), custom_call_target="tpu_custom_call" | custom-call | flops 3000000000 | bytes 15000000 | tf_op jit(solution)/shard_map/experts/pallas_call | solution.py:41
  94.0 0.2 collective-permute-start.13
  94.2 0.7 put.1
  94.9 1.8 %collective-permute-done.13 = bf16[512,1024]{1,0:T(8,128)(2,1)S(1)} collective-permute-done((bf16[512,1024]{1,0:T(8,128)(2,1)S(1)}, bf16[512,1024]{1,0:T(8,128)(2,1)S(1)}, u32[]{:S(2)}, u32[]{:S(2)}) %collective-permute-start.13) | collective-permute-done | bytes 1048608 | tf_op jit(solution)/shard_map/ppermute | solution.py:612
  96.7 0.4 fusion
  97.1 23.3 %all_to_all.17 = bf16[64,8,1024]{2,1,0:T(8,128)(2,1)S(1)} all-to-all(bf16[64,8,1024]{2,1,0:T(8,128)(2,1)S(1)} %fusion), channel_id=1, replica_groups=mesh['x'=4,'z'=4,'y'=4,'core'=2] {'x','z','y'}, dimensions={0} | all-to-all | bytes 2097152 | tf_op jit(solution)/shard_map/all_to_all | solution.py:618
  120.5 0.2 convert_reduce_fusion
  120.7 0.7 reshape.27
  (27 shorter events, 0.1 us)
Async XLA Ops:
  0.0 17.3 %copy-start.13 = (s32[2]{0:T(128)S(1)}, s32[2]{0:T(128)}, u32[]{:S(2)}) copy-start(s32[2]{0:T(128)} %counts_hbm.1) | copy-start | bytes 28
  0.0 17.3 %copy-start.3 = (s32[4,128,6]{1,0,2:T(4,128)S(1)}, s32[4,128,6]{1,0,2:T(4,128)}, u32[]{:S(2)}) copy-start(s32[4,128,6]{1,0,2:T(4,128)} %param.41) | copy-start | bytes 36868
  0.0 17.3 %copy-start.4 = (f32[4,128,6]{1,0,2:T(4,128)S(1)}, f32[4,128,6]{1,0,2:T(4,128)}, u32[]{:S(2)}) copy-start(f32[4,128,6]{1,0,2:T(4,128)} %param.42) | copy-start | bytes 36868
  0.0 19.5 %copy-start.6 = (f32[512]{0:T(512)S(1)}, f32[512]{0:T(512)}, u32[]{:S(2)}) copy-start(f32[512]{0:T(512)} %param.26) | copy-start | bytes 6148
  2.2 4.9 %collective-permute-start.2 = (bf16[72,512]{1,0:T(8,128)(2,1)S(1)}, bf16[72,512]{1,0:T(8,128)(2,1)S(1)}, u32[]{:S(2)}, u32[]{:S(2)}) collective-permute-start(bf16[72,512]{1,0:T(8,128)(2,1)S(1)} %get-tuple-element.34), channel_id=1, source_target_pairs={{0,96},{1,25},{8,104},{9,1},{16,112},{17,9},{24,120},{25,17},{32,0... | collective-permute-start | bytes 221192 | tf_op jit(solution)/shard_map/ppermute | solution.py:76
  5.1 5.9 %collective-permute-start.1 = (bf16[72,512]{1,0:T(8,128)(2,1)S(1)}, bf16[72,512]{1,0:T(8,128)(2,1)S(1)}, u32[]{:S(2)}, u32[]{:S(2)}) collective-permute-start(bf16[72,512]{1,0:T(8,128)(2,1)S(1)} %get-tuple-element.34), channel_id=1, source_target_pairs={{0,64},{1,17},{8,72},{9,25},{16,80},{17,1},{24,88},{25,9},{32,96},... | collective-permute-start | bytes 221192 | tf_op jit(solution)/shard_map/ppermute | solution.py:76
  5.9 5.8 %collective-permute-start = (bf16[72,512]{1,0:T(8,128)(2,1)S(1)}, bf16[72,512]{1,0:T(8,128)(2,1)S(1)}, u32[]{:S(2)}, u32[]{:S(2)}) collective-permute-start(bf16[72,512]{1,0:T(8,128)(2,1)S(1)} %get-tuple-element.34), channel_id=1, source_target_pairs={{0,32},{1,9},{8,40},{9,17},{16,48},{17,25},{24,56},{25,1},{32,64},... | collective-permute-start | bytes 221192 | tf_op jit(solution)/shard_map/ppermute | solution.py:76
  11.8 11.5 %collective-permute-start.5 = (bf16[4,72,512]{2,1,0:T(8,128)(2,1)S(1)}, bf16[4,72,512]{2,1,0:T(8,128)(2,1)S(1)}, u32[]{:S(2)}, u32[]{:S(2)}) collective-permute-start(bf16[4,72,512]{2,1,0:T(8,128)(2,1)S(1)} %pad_maximum_fusion.refs_0_), channel_id=1, source_target_pairs={{0,24},{1,97},{8,0},{9,105},{16,8},{17,113},{24,16},{25,121},{32,5... | collective-permute-start | bytes 884744 | tf_op jit(solution)/shard_map/ppermute | solution.py:76
  15.9 8.3 %collective-permute-start.4 = (bf16[4,72,512]{2,1,0:T(8,128)(2,1)S(1)}, bf16[4,72,512]{2,1,0:T(8,128)(2,1)S(1)}, u32[]{:S(2)}, u32[]{:S(2)}) collective-permute-start(bf16[4,72,512]{2,1,0:T(8,128)(2,1)S(1)} %pad_maximum_fusion.refs_0_), channel_id=1, source_target_pairs={{0,16},{1,65},{8,24},{9,73},{16,0},{17,81},{24,8},{25,89},{32,48},... | collective-permute-start | bytes 884744 | tf_op jit(solution)/shard_map/ppermute | solution.py:76
  15.9 11.2 %collective-permute-start.3 = (bf16[4,72,512]{2,1,0:T(8,128)(2,1)S(1)}, bf16[4,72,512]{2,1,0:T(8,128)(2,1)}, u32[]{:S(2)}, u32[]{:S(2)}) collective-permute-start(bf16[4,72,512]{2,1,0:T(8,128)(2,1)S(1)} %pad_maximum_fusion.refs_0_), channel_id=1, source_target_pairs={{0,8},{1,33},{8,16},{9,41},{16,24},{17,49},{24,0},{25,57},{32,40},... | collective-permute-start | bytes 884744 | tf_op jit(solution)/shard_map/ppermute | solution.py:76
  17.3 9.8 %copy-start.10 = (bf16[2,6,128,576]{2,3,1,0:T(8,128)(2,1)S(1)}, bf16[2,6,128,576]{2,3,1,0:T(8,128)(2,1)}, u32[]{:S(2)}) copy-start(bf16[2,6,128,576]{2,3,1,0:T(8,128)(2,1)} %param.37) | copy-start | bytes 5308420
  17.3 9.8 %copy-start.11 = (s32[2,8,64]{2,1,0:T(8,128)S(1)}, s32[2,8,64]{2,1,0:T(8,128)}, u32[]{:S(2)}) copy-start(s32[2,8,64]{2,1,0:T(8,128)} %refs_7_.1) | copy-start | bytes 12292
  17.3 9.8 %copy-start.12 = (s32[4,2,8]{2,1,0:T(2,128)S(1)}, s32[4,2,8]{2,1,0:T(2,128)}, u32[]{:S(2)}) copy-start(s32[4,2,8]{2,1,0:T(2,128)} %refs_6_.1) | copy-start | bytes 772
  27.1 25.0 %copy-start.1 = (bf16[128,2048]{1,0:T(8,128)(2,1)S(1)}, bf16[128,2048]{1,0:T(8,128)(2,1)}, u32[]{:S(2)}) copy-start(bf16[128,2048]{1,0:T(8,128)(2,1)} %refs_5_.1) | copy-start | bytes 1572868
  27.1 25.0 %copy-start.2 = (bf16[1,512,128]{2,1,0:T(8,128)(2,1)S(1)}, bf16[1,512,128]{2,1,0:T(8,128)(2,1)}, u32[]{:S(2)}) copy-start(bf16[1,512,128]{2,1,0:T(8,128)(2,1)} %refs_4_.1) | copy-start | bytes 393220
  32.6 31.6 %copy-start = (bf16[4,16,2048]{2,1,0:T(8,128)(2,1)S(1)}, bf16[4,16,2048]{2,1,0:T(8,128)(2,1)}, u32[]{:S(2)}) copy-start(bf16[4,16,2048]{2,1,0:T(8,128)(2,1)} %embeds_ref.1) | copy-start | bytes 786436
  32.6 31.6 %copy-start.5 = (f32[2048]{0:T(1024)S(1)}, f32[2048]{0:T(1024)}, u32[]{:S(2)}) copy-start(f32[2048]{0:T(1024)} %param.30) | copy-start | bytes 24580
  32.7 6.5 %collective-permute-start.6 = (bf16[264,512]{1,0:T(8,128)(2,1)S(1)}, bf16[264,512]{1,0:T(8,128)(2,1)S(1)}, u32[]{:S(2)}, u32[]{:S(2)}) collective-permute-start(bf16[264,512]{1,0:T(8,128)(2,1)S(1)} %get-tuple-element.43), channel_id=1, source_target_pairs={{0,96},{1,25},{8,104},{9,1},{16,112},{17,9},{24,120},{25,17},{32,0... | collective-permute-start | bytes 811016 | tf_op jit(solution)/shard_map/ppermute | solution.py:76
  33.3 8.1 %collective-permute-start.7 = (bf16[264,512]{1,0:T(8,128)(2,1)S(1)}, bf16[264,512]{1,0:T(8,128)(2,1)S(1)}, u32[]{:S(2)}, u32[]{:S(2)}) collective-permute-start(bf16[264,512]{1,0:T(8,128)(2,1)S(1)} %get-tuple-element.44), channel_id=1, source_target_pairs={{0,64},{1,17},{8,72},{9,25},{16,80},{17,1},{24,88},{25,9},{32,96},... | collective-permute-start | bytes 811016 | tf_op jit(solution)/shard_map/ppermute | solution.py:76
  34.2 10.0 %collective-permute-start.8 = (bf16[264,512]{1,0:T(8,128)(2,1)S(1)}, bf16[264,512]{1,0:T(8,128)(2,1)S(1)}, u32[]{:S(2)}, u32[]{:S(2)}) collective-permute-start(bf16[264,512]{1,0:T(8,128)(2,1)S(1)} %get-tuple-element.45), channel_id=1, source_target_pairs={{0,32},{1,9},{8,40},{9,17},{16,48},{17,25},{24,56},{25,1},{32,64},... | collective-permute-start | bytes 811016 | tf_op jit(solution)/shard_map/ppermute | solution.py:76
  44.2 45.6 %copy-start.9 = (bf16[2,352,2048]{2,1,0:T(8,128)(2,1)S(1)}, bf16[2,352,2048]{2,1,0:T(8,128)(2,1)}, u32[]{:S(2)}) copy-start(bf16[2,352,2048]{2,1,0:T(8,128)(2,1)} %down_ref.1) | copy-start | bytes 8650756
  44.5 4.4 %collective-permute-start.9 = (bf16[72,512]{1,0:T(8,128)(2,1)S(1)}, bf16[72,512]{1,0:T(8,128)(2,1)S(1)}, u32[]{:S(2)}, u32[]{:S(2)}) collective-permute-start(bf16[72,512]{1,0:T(8,128)(2,1)S(1)} %get-tuple-element.47), channel_id=1, source_target_pairs={{0,24},{1,97},{8,0},{9,105},{16,8},{17,113},{24,16},{25,121},{32,5... | collective-permute-start | bytes 221192 | tf_op jit(solution)/shard_map/ppermute | solution.py:76
  45.4 5.9 %collective-permute-start.10 = (bf16[72,512]{1,0:T(8,128)(2,1)S(1)}, bf16[72,512]{1,0:T(8,128)(2,1)S(1)}, u32[]{:S(2)}, u32[]{:S(2)}) collective-permute-start(bf16[72,512]{1,0:T(8,128)(2,1)S(1)} %get-tuple-element.48), channel_id=1, source_target_pairs={{0,16},{1,65},{8,24},{9,73},{16,0},{17,81},{24,8},{25,89},{32,48},... | collective-permute-start | bytes 221192 | tf_op jit(solution)/shard_map/ppermute | solution.py:76
  45.4 6.6 %collective-permute-start.11 = (bf16[72,512]{1,0:T(8,128)(2,1)S(1)}, bf16[72,512]{1,0:T(8,128)(2,1)S(1)}, u32[]{:S(2)}, u32[]{:S(2)}) collective-permute-start(bf16[72,512]{1,0:T(8,128)(2,1)S(1)} %get-tuple-element.49), channel_id=1, source_target_pairs={{0,8},{1,33},{8,16},{9,41},{16,24},{17,49},{24,0},{25,57},{32,40},... | collective-permute-start | bytes 221192 | tf_op jit(solution)/shard_map/ppermute | solution.py:76
  65.3 24.5 %copy-start.8 = (bf16[2,2048,352]{1,2,0:T(8,128)(2,1)S(1)}, bf16[2,2048,352]{1,2,0:T(8,128)(2,1)}, u32[]{:S(2)}) copy-start(bf16[2,2048,352]{1,2,0:T(8,128)(2,1)} %param.35) | copy-start | bytes 8650756
  87.1 2.7 %copy-start.7 = (bf16[2,2048,352]{1,2,0:T(8,128)(2,1)S(1)}, bf16[2,2048,352]{1,2,0:T(8,128)(2,1)}, u32[]{:S(2)}) copy-start(bf16[2,2048,352]{1,2,0:T(8,128)(2,1)} %param.34) | copy-start | bytes 8650756
  87.1 2.7 %collective-permute-start.12 = (bf16[512,1024]{1,0:T(8,128)(2,1)S(1)}, bf16[512,1024]{1,0:T(8,128)(2,1)S(1)}, u32[]{:S(2)}, u32[]{:S(2)}) collective-permute-start(bf16[512,1024]{1,0:T(8,128)(2,1)S(1)} %bitcast.26), channel_id=1, source_target_pairs={{0,1},{1,0},{2,3},{3,2},{4,5},{5,4},{6,7},{7,6},{8,9},{9,8},{10,11... | collective-permute-start | bytes 3145736 | tf_op jit(solution)/shard_map/ppermute | solution.py:577
  94.0 2.7 %collective-permute-start.13 = (bf16[512,1024]{1,0:T(8,128)(2,1)S(1)}, bf16[512,1024]{1,0:T(8,128)(2,1)S(1)}, u32[]{:S(2)}, u32[]{:S(2)}) collective-permute-start(bf16[512,1024]{1,0:T(8,128)(2,1)S(1)} %get-tuple-element.62), channel_id=1, source_target_pairs={{0,1},{1,0},{2,3},{3,2},{4,5},{5,4},{6,7},{7,6},{8,9},{9,8},{10,11... | collective-permute-start | bytes 3145736 | tf_op jit(solution)/shard_map/ppermute | solution.py:612
